TPU v7x, 768 devices: a whole 4x8x12 slice. The times are simulated.
768 devices in a mesh: section: 32 (over x, z_hi, core), tensor: 24 (over y, z_lo).
Axes of the slice: x: 4, y: 8, z: 12 (z_hi: 4, z_lo: 3; z = z_hi * 3 + z_lo), core: 2. Of those that a mesh axis runs over, the one named last changes fastest.
Arguments:
- fwd_input: bfloat16 [32, 64, 4608], P('section', None, 'tensor'), may hold values from -6 to 6
- bwd_grad: bfloat16 [32, 64, 4608], P('section', None, 'tensor'), may hold values from -6 to 6
- parked: bfloat16 [32, 64, 4608], P('section', None, 'tensor'), may hold values from -6 to 6
- norm_gain: float32 [32, 4608], P('section'), may hold values from 0.25 to 1.75
- w_query: bfloat16 [32, 4608, 3072], P('section', None, 'tensor'), may hold values from -1 to 1
- w_key: bfloat16 [32, 4608, 3072], P('section', None, 'tensor'), may hold values from -1 to 1
- w_value: bfloat16 [32, 4608, 3072], P('section', None, 'tensor'), may hold values from -0.09375 to 0.09375
- w_out: bfloat16 [32, 3072, 4608], P('section', 'tensor'), may hold values from -0.109375 to 0.109375
- offsets: int32 [32, 2, 8], P('section'), may hold values from 0 to 56, as said below
- mirror: int32 [32], replicated, may hold values from 0 to 31, as said below
Outputs:
- next_input: bfloat16 [32, 64, 4608], P('section', None, 'tensor')
- prev_grad: bfloat16 [32, 64, 4608], P('section', None, 'tensor')
- parked_new: bfloat16 [32, 64, 4608], P('section', None, 'tensor')
Inputs may be any that keep to these rules, and one draw needn't show every extreme that they name: Each row offsets[s, j] holds the numbers 0, 8, ..., 56 once each. mirror[t] = t XOR m for one m with 32 / 2 <= m < 32, so sections of the first half pair with sections of the second half.
All inputs are finite; a program needn't handle non-finite values.
Results may differ from a plain program's by a relative error of at most 0.018.
Values may be sent and summed in bfloat16 or wider, within the bound.
No kernel may reach another device: no remote copies, remote signals or barrier semaphores. Data moves between devices by JAX's collectives and lax.ppermute only.
A program may use at most 32 MiB of HBM per device.

v0:
```python
import math

import jax
import jax.numpy as jnp
from jax import lax
from jax.sharding import PartitionSpec as P

HD = 64
SPAN = 8


def partner(value, axis, bit):
    return lax.ppermute(value, axis, [(i, i ^ 1 << bit) for i in range(lax.axis_size(axis))])


def passed_along(block, axis, distance):
    devices = range(lax.axis_size(axis))
    route = [(i - distance, i) for i in devices if i - distance in devices]
    return lax.ppermute(block, axis, route)


def token_positions(starts, row_count):
    rows_iota = jnp.arange(row_count, dtype=jnp.int32)
    block_id = rows_iota // SPAN
    chosen = block_id[:, None] == jnp.arange(starts.shape[0], dtype=jnp.int32)[None, :]
    return jnp.sum(jnp.where(chosen, starts[None, :], 0), axis=1) + rows_iota % SPAN


def branch(inputs, norm_scale, query_part, key_part, value_part, out_part, places):
    row_count = inputs.shape[0]
    head_count = query_part.shape[1] // HD
    widened = inputs.astype(jnp.float32)
    inverse = lax.rsqrt(jnp.mean(widened * widened, axis=1, keepdims=True) + 1e-05)
    normed = (widened * inverse * norm_scale[None, :]).astype(jnp.bfloat16)
    queries = (
        jnp.dot(normed, query_part, preferred_element_type=jnp.float32)
        .astype(jnp.bfloat16)
        .reshape(row_count, head_count, HD)
    )
    key_rows = (
        jnp.dot(normed, key_part, preferred_element_type=jnp.float32)
        .astype(jnp.bfloat16)
        .reshape(row_count, head_count, HD)
    )
    value_rows = (
        jnp.dot(normed, value_part, preferred_element_type=jnp.float32)
        .astype(jnp.bfloat16)
        .reshape(row_count, head_count, HD)
    )
    scores = jnp.einsum(
        "qhd,khd->hqk", queries.astype(jnp.float32), key_rows.astype(jnp.float32)
    ) / math.sqrt(HD)
    allowed = places[None, :, None] >= places[None, None, :]
    scores = jnp.where(allowed, scores, -1e30)
    row_max = jnp.max(scores, axis=2, keepdims=True)
    exp_scores = jnp.exp(scores - row_max)
    weights = (exp_scores / jnp.sum(exp_scores, axis=2, keepdims=True)).astype(jnp.bfloat16)
    context = jnp.einsum(
        "hqk,khd->qhd", weights.astype(jnp.float32), value_rows.astype(jnp.float32)
    ).astype(jnp.bfloat16)
    return jnp.dot(
        context.reshape(row_count, head_count * HD), out_part, preferred_element_type=jnp.float32
    )


def swap_on_bit(values, bit_number):
    return partner(values, "section", bit_number)


def keep_values(values):
    return values


def local(fwd_input, bwd_grad, parked, norm_gain, w_query, w_key, w_value, w_out, offsets, mirror):
    fwd_rows = fwd_input[0]
    grad_rows = bwd_grad[0]
    stashed = parked[0]
    section_count = lax.axis_size("section")
    paired = jnp.stack([fwd_rows, stashed])
    xor_mask = mirror[0]
    swapped = paired
    for bit_number in range(section_count.bit_length() - 1):
        flipped = xor_mask >> bit_number & 1 == 1
        swapped = lax.cond(flipped, partial_swap(bit_number), keep_values, swapped)
    parked_rows = swapped[0]
    fetched = swapped[1]
    full_fwd, full_back, full_grad = (
        lax.all_gather(fwd_rows, "tensor", axis=1, tiled=True),
        lax.all_gather(fetched, "tensor", axis=1, tiled=True),
        lax.all_gather(grad_rows, "tensor", axis=1, tiled=True),
    )
    scale_row = norm_gain[0]
    pos_fwd = token_positions(offsets[0, 0], full_fwd.shape[0])
    pos_bwd = token_positions(offsets[0, 1], full_back.shape[0])
    query_part = w_query[0]
    key_part = w_key[0]
    value_part = w_value[0]
    out_part = w_out[0]
    forward_term = branch(full_fwd, scale_row, query_part, key_part, value_part, out_part, pos_fwd)

    def stashed_branch(layer_in):
        return branch(layer_in, scale_row, query_part, key_part, value_part, out_part, pos_bwd)

    unused, pullback = jax.vjp(stashed_branch, full_back)
    (back_term,) = pullback(full_grad.astype(jnp.float32))
    back_term = back_term.astype(jnp.float32)
    whole_fwd, whole_back = (
        lax.psum(forward_term.astype(jnp.bfloat16), "tensor").astype(jnp.float32),
        lax.psum(back_term.astype(jnp.bfloat16), "tensor").astype(jnp.float32),
    )
    share = fwd_rows.shape[1]
    first_col = lax.axis_index("tensor") * share
    forward_sum = lax.dynamic_slice_in_dim(whole_fwd, first_col, share, 1)
    back_sum = lax.dynamic_slice_in_dim(whole_back, first_col, share, 1)
    layer_out = (fwd_rows.astype(jnp.float32) + forward_sum).astype(jnp.bfloat16)
    grad_out = (grad_rows.astype(jnp.float32) + back_sum).astype(jnp.bfloat16)
    next_rows = passed_along(layer_out, "section", 1)
    prev_rows = passed_along(grad_out, "section", -1)
    return (next_rows[None], prev_rows[None], parked_rows[None])


def partial_swap(bit_number):

    def swapper(values):
        return swap_on_bit(values, bit_number)

    return swapper


def solution(mesh):
    in_specs = (
        P("section", None, "tensor"),
        P("section", None, "tensor"),
        P("section", None, "tensor"),
        P("section", None),
        P("section", None, "tensor"),
        P("section", None, "tensor"),
        P("section", None, "tensor"),
        P("section", "tensor", None),
        P("section", None, None),
        P(),
    )
    out_specs = (
        P("section", None, "tensor"),
        P("section", None, "tensor"),
        P("section", None, "tensor"),
    )
    return jax.shard_map(local, mesh=mesh, in_specs=in_specs, out_specs=out_specs, check_vma=False)
```

profile of v0, /device:TPU:1, one launch (start us, length us, event | category | flops | bytes accessed | tf_op | source)
XLA Modules:
  0.0 624.9 jit_solution(13756065553635614460)
XLA Ops:
  10.6 1.5 copy.78
  12.9 17.5 %conditional.7 = (bf16[2,64,192]{2,1,0:T(8,128)(2,1)S(1)}) conditional(s32[]{:T(128)} %bitcast.19, bf16[2,64,192]{2,1,0:T(8,128)(2,1)S(1)} %get-tuple-element.55, bf16[2,64,192]{2,1,0:T(8,128)(2,1)S(1)} %get-tuple-element.55), branch_computations={%region_10.11_spmd, %region_11.12_spmd} | conditional | bytes 294960 | solution.py:84
  12.9 15.7 %collective-permute-start.2 = (bf16[2,64,192]{2,1,0:T(8,128)(2,1)S(1)}, bf16[2,64,192]{2,1,0:T(8,128)(2,1)S(1)}, u32[]{:S(2)}, u32[]{:S(2)}) collective-permute-start(bf16[2,64,192]{2,1,0:T(8,128)(2,1)S(1)} %param.5), channel_id=1, source_target_pairs={{0,96},{24,120},{48,144},{72,168},{96,0},{120,24},{144,48},{168,72... | collective-permute-start | bytes 147464 | tf_op jit(solution)/shard_map/cond/branch_1_fun/ppermute | solution.py:13
  28.6 1.8 collective-permute-done.2
  30.4 5.0 conditional.8
  30.4 3.1 collective-permute-start.3
  33.6 1.9 collective-permute-done.3
  35.5 6.5 %conditional.9 = (bf16[2,64,192]{2,1,0:T(8,128)(2,1)S(1)}) conditional(s32[]{:T(128)} %bitcast.17, bf16[2,64,192]{2,1,0:T(8,128)(2,1)S(1)} %get-tuple-element.57, bf16[2,64,192]{2,1,0:T(8,128)(2,1)S(1)} %get-tuple-element.57), branch_computations={%region_14.15_spmd, %region_15.16_spmd} | conditional | bytes 294960 | solution.py:84
  35.5 4.6 collective-permute-start.4
  40.1 1.9 collective-permute-done.4
  43.3 70.7 %all-gather = bf16[1,64,4608]{1,0,2:T(2,128)(2,1)S(1)} all-gather(bf16[1,64,192]{1,0,2:T(2,128)(2,1)} %copy.78), channel_id=2, replica_groups=mesh['section'=32,'tensor'=24] {'tensor'}, dimensions={2}, use_global_device_ids=true | all-gather | bytes 614400 | tf_op jit(solution)/shard_map/all_gather | solution.py:88
  114.1 3.9 copy.79
  118.0 1.3 fusion.5
  120.2 2.4 fusion.50
  122.6 1.0 fusion.38
  123.6 71.2 %all-gather.2 = bf16[1,64,4608]{1,0,2:T(2,128)(2,1)} all-gather(bf16[1,64,192]{1,0,2:T(2,128)(2,1)S(1)} %copy-done.6), channel_id=4, replica_groups=mesh['section'=32,'tensor'=24] {'tensor'}, dimensions={2}, use_global_device_ids=true | all-gather | bytes 614400 | tf_op jit(solution)/shard_map/all_gather | solution.py:89
  194.7 4.9 copy.88
  200.5 1.7 fusion.53
  202.2 1.0 fusion.41
  203.5 1.0 fusion.44
  204.5 1.0 fusion.47
  206.9 69.2 %all-gather.1 = bf16[1,64,4608]{1,0,2:T(2,128)(2,1)} all-gather(bf16[1,64,192]{1,0,2:T(2,128)(2,1)S(1)} %copy.84), channel_id=3, replica_groups=mesh['section'=32,'tensor'=24] {'tensor'}, dimensions={2}, use_global_device_ids=true | all-gather | bytes 614400 | tf_op jit(solution)/shard_map/all_gather | solution.py:90
  276.1 4.9 copy.85
  286.5 1.2 convolution_convert_fusion.3
  287.9 1.9 convolution_convert_fusion
  291.3 1.1 fusion.8
  292.5 283.6 %all-reduce.3.cloned.1.call-done = (bf16[64,4608]{1,0:T(8,128)(2,1)}, bf16[64,4608]{1,0:T(8,128)(2,1)}) async-done(((bf16[64,4608]{1,0:T(8,128)(2,1)}, bf16[64,4608]{1,0:T(8,128)(2,1)}), (bf16[64,4608]{1,0:T(8,128)(2,1)}, bf16[64,4608]{1,0:T(8,128)(2,1)})) %all-reduce.3.cloned.1.call-update) | async-done | bytes 1179664 | tf_op jit(solution)/shard_map/psum | solution.py:108
  576.1 0.9 fusion.60
  577.0 19.3 %collective-permute-start.6 = (bf16[64,192]{1,0:T(8,128)(2,1)S(1)}, bf16[64,192]{1,0:T(8,128)(2,1)S(1)}, u32[]{:S(2)}, u32[]{:S(2)}) collective-permute-start(bf16[64,192]{1,0:T(8,128)(2,1)S(1)} %fusion.60), channel_id=1, source_target_pairs={{24,0},{48,24},{72,48},{96,72},{120,96},{144,120},{168,144},{192,1... | collective-permute-start | bytes 73736 | tf_op jit(solution)/shard_map/ppermute | solution.py:19
  596.3 0.9 fusion.61
  597.2 18.7 %collective-permute-start.5 = (bf16[64,192]{1,0:T(8,128)(2,1)S(1)}, bf16[64,192]{1,0:T(8,128)(2,1)S(1)}, u32[]{:S(2)}, u32[]{:S(2)}) collective-permute-start(bf16[64,192]{1,0:T(8,128)(2,1)S(1)} %fusion.61), channel_id=1, source_target_pairs={{0,24},{24,48},{48,72},{72,96},{96,120},{120,144},{144,168},{168,1... | collective-permute-start | bytes 73736 | tf_op jit(solution)/shard_map/ppermute | solution.py:19
  615.9 1.0 collective-permute-done.5
  (99 shorter events, 13.9 us)
Async XLA Ops:
  7.2 115.4 %copy-start = (bf16[1,4608,128]{2,1,0:T(8,128)(2,1)S(1)}, bf16[1,4608,128]{2,1,0:T(8,128)(2,1)}, u32[]{:S(2)}) copy-start(bf16[1,4608,128]{2,1,0:T(8,128)(2,1)} %param.26) | copy-start | bytes 3538948
  7.2 568.9 %all-reduce.3.cloned.1.call-start = ((), (), s32[]{:S(2)}) async-start(), calls=%async_computation | async-start | bytes 2359296 | tf_op jit(solution)/shard_map/psum | solution.py:108
  12.9 17.5 %collective-permute-start.2 = (bf16[2,64,192]{2,1,0:T(8,128)(2,1)S(1)}, bf16[2,64,192]{2,1,0:T(8,128)(2,1)S(1)}, u32[]{:S(2)}, u32[]{:S(2)}) collective-permute-start(bf16[2,64,192]{2,1,0:T(8,128)(2,1)S(1)} %param.5), channel_id=1, source_target_pairs={{0,96},{24,120},{48,144},{72,168},{96,0},{120,24},{144,48},{168,72... | collective-permute-start | bytes 147464 | tf_op jit(solution)/shard_map/cond/branch_1_fun/ppermute | solution.py:13
  30.4 5.0 collective-permute-start.3
  35.5 6.5 %collective-permute-start.4 = (bf16[2,64,192]{2,1,0:T(8,128)(2,1)S(1)}, bf16[2,64,192]{2,1,0:T(8,128)(2,1)S(1)}, u32[]{:S(2)}, u32[]{:S(2)}) collective-permute-start(bf16[2,64,192]{2,1,0:T(8,128)(2,1)S(1)} %param.9), channel_id=1, source_target_pairs={{0,384},{24,408},{48,432},{72,456},{96,480},{120,504},{144,528},{1... | collective-permute-start | bytes 147464 | tf_op jit(solution)/shard_map/cond/branch_1_fun/ppermute | solution.py:13
  118.0 4.6 copy-start.2
  120.1 3.4 copy-start.10
  122.6 1.0 copy-start.6
  194.7 5.8 copy-start.4
  199.7 2.5 copy-start.11
  199.9 0.6 copy-start.19
  200.5 3.9 copy-start.21
  202.2 1.3 copy-start.3
  204.5 1.0 copy-start.17
  204.5 2.3 copy-start.8
  276.1 4.9 copy-start.1
  281.5 3.9 copy-start.13
  281.5 4.2 copy-start.18
  281.6 4.3 copy-start.16
  281.6 4.4 copy-start.15
  281.6 4.5 copy-start.14
  287.7 2.2 copy-start.5
  289.8 0.7 copy-start.12
  290.6 0.7 copy-start.20
  290.6 0.8 copy-start.22
  292.5 283.6 %copy-start.9 = (bf16[1,64,192]{2,1,0:T(8,128)(2,1)S(1)}, bf16[1,64,192]{2,1,0:T(8,128)(2,1)}, u32[]{:S(2)}) copy-start(bf16[1,64,192]{2,1,0:T(8,128)(2,1)} %param.21) | copy-start | bytes 73732
  292.5 303.8 %copy-start.7 = (bf16[1,64,192]{2,1,0:T(8,128)(2,1)S(1)}, bf16[1,64,192]{2,1,0:T(8,128)(2,1)}, u32[]{:S(2)}) copy-start(bf16[1,64,192]{2,1,0:T(8,128)(2,1)} %param.20) | copy-start | bytes 73732
  577.0 38.9 %collective-permute-start.6 = (bf16[64,192]{1,0:T(8,128)(2,1)S(1)}, bf16[64,192]{1,0:T(8,128)(2,1)S(1)}, u32[]{:S(2)}, u32[]{:S(2)}) collective-permute-start(bf16[64,192]{1,0:T(8,128)(2,1)S(1)} %fusion.60), channel_id=1, source_target_pairs={{24,0},{48,24},{72,48},{96,72},{120,96},{144,120},{168,144},{192,1... | collective-permute-start | bytes 73736 | tf_op jit(solution)/shard_map/ppermute | solution.py:19
  597.2 19.7 %collective-permute-start.5 = (bf16[64,192]{1,0:T(8,128)(2,1)S(1)}, bf16[64,192]{1,0:T(8,128)(2,1)S(1)}, u32[]{:S(2)}, u32[]{:S(2)}) collective-permute-start(bf16[64,192]{1,0:T(8,128)(2,1)S(1)} %fusion.61), channel_id=1, source_target_pairs={{0,24},{24,48},{48,72},{72,96},{96,120},{120,144},{144,168},{168,1... | collective-permute-start | bytes 73736 | tf_op jit(solution)/shard_map/ppermute | solution.py:19
Sparse Core Ops, SparseCore 0:
  292.6 283.4 all-reduce.2
where the time goes:
time: 626 us; the launch traced here: 625 us
  waiting for transfers between devices  290 us (46%)
  blocking collectives  211 us (34%)
  starting transfers between devices  61.4 us (10%)
  local copies, waits for them, and re-layouts  22.2 us (4%)
  between operations  17.7 us (3%)
  matrix products  14.6 us (2%)
  other arithmetic  7.59 us (1%)
    psum x1, waiting for transfers between devices, local(): lax.psum(forward_term.astype(jnp.bfloat16), 'tensor').astype(jnp.float32)  284 us
    all_gather x1, blocking collectives, local(): lax.all_gather(fetched, 'tensor', axis=1, tiled=True)  71.2 us
    all_gather x1, blocking collectives, local(): lax.all_gather(fwd_rows, 'tensor', axis=1, tiled=True)  70.7 us
    all_gather x1, blocking collectives, local(): lax.all_gather(grad_rows, 'tensor', axis=1, tiled=True)  69.2 us
    ppermute x2, starting transfers between devices, passed_along(): return lax.ppermute(block, axis, route)  38 us
    ppermute x3, starting transfers between devices, partner(): lax.ppermute(value, axis, [(i, i ^ 1 << bit) for i in range(lax.axis_size...  23.4 us
  transfers between devices with their start and end apart: 6, of which 5 were waited for; matrix products, arithmetic and copies ran while one was open for 0% of the time, Pallas kernels for 0%

commit v1 on v0

--- a/solution.py
+++ b/solution.py
@@ -7,10 +7,6 @@
 
 HD = 64
 SPAN = 8
-
-
-def partner(value, axis, bit):
-    return lax.ppermute(value, axis, [(i, i ^ 1 << bit) for i in range(lax.axis_size(axis))])
 
 
 def passed_along(block, axis, distance):
@@ -63,32 +59,45 @@
     )
 
 
-def swap_on_bit(values, bit_number):
-    return partner(values, "section", bit_number)
+def mirrored(values, mask):
+    section_count = lax.axis_size("section")
+    half = section_count // 2
+
+    def swap_by(distance):
+        route = [(i, i ^ distance) for i in range(section_count)]
+        return lambda held: lax.ppermute(held, "section", route)
+
+    return lax.switch(mask - half, [swap_by(half + i) for i in range(half)], values)
 
 
-def keep_values(values):
-    return values
+def exchanged(blocks):
+    return lax.all_to_all(blocks, "tensor", 0, 0, tiled=True)
+
+
+def spread(block):
+    return exchanged(jnp.broadcast_to(block[None], (lax.axis_size("tensor"),) + block.shape))
+
+
+def side_by_side(blocks):
+    return blocks.transpose(1, 0, 2).reshape(blocks.shape[1], -1)
+
+
+def by_device(whole):
+    parts = lax.axis_size("tensor")
+    return whole.reshape(whole.shape[0], parts, -1).transpose(1, 0, 2)
 
 
 def local(fwd_input, bwd_grad, parked, norm_gain, w_query, w_key, w_value, w_out, offsets, mirror):
     fwd_rows = fwd_input[0]
     grad_rows = bwd_grad[0]
-    stashed = parked[0]
-    section_count = lax.axis_size("section")
-    paired = jnp.stack([fwd_rows, stashed])
-    xor_mask = mirror[0]
-    swapped = paired
-    for bit_number in range(section_count.bit_length() - 1):
-        flipped = xor_mask >> bit_number & 1 == 1
-        swapped = lax.cond(flipped, partial_swap(bit_number), keep_values, swapped)
-    parked_rows = swapped[0]
-    fetched = swapped[1]
-    full_fwd, full_back, full_grad = (
-        lax.all_gather(fwd_rows, "tensor", axis=1, tiled=True),
-        lax.all_gather(fetched, "tensor", axis=1, tiled=True),
-        lax.all_gather(grad_rows, "tensor", axis=1, tiled=True),
-    )
+    share = fwd_rows.shape[1]
+    swapped = mirrored(jnp.concatenate([fwd_rows, parked[0]], axis=1), mirror[0])
+    parked_rows = swapped[:, :share]
+    fetched = swapped[:, share:]
+    pair = spread(jnp.concatenate([fwd_rows, grad_rows, fetched], axis=1))
+    full_fwd = side_by_side(pair[:, :, :share])
+    full_grad = side_by_side(pair[:, :, share : 2 * share])
+    full_back = side_by_side(pair[:, :, 2 * share : 3 * share])
     scale_row = norm_gain[0]
     pos_fwd = token_positions(offsets[0, 0], full_fwd.shape[0])
     pos_bwd = token_positions(offsets[0, 1], full_back.shape[0])
@@ -103,28 +112,15 @@
 
     unused, pullback = jax.vjp(stashed_branch, full_back)
     (back_term,) = pullback(full_grad.astype(jnp.float32))
-    back_term = back_term.astype(jnp.float32)
-    whole_fwd, whole_back = (
-        lax.psum(forward_term.astype(jnp.bfloat16), "tensor").astype(jnp.float32),
-        lax.psum(back_term.astype(jnp.bfloat16), "tensor").astype(jnp.float32),
+    terms = jnp.concatenate(
+        [by_device(forward_term.astype(jnp.bfloat16)), by_device(back_term.astype(jnp.bfloat16))], axis=2
     )
-    share = fwd_rows.shape[1]
-    first_col = lax.axis_index("tensor") * share
-    forward_sum = lax.dynamic_slice_in_dim(whole_fwd, first_col, share, 1)
-    back_sum = lax.dynamic_slice_in_dim(whole_back, first_col, share, 1)
-    layer_out = (fwd_rows.astype(jnp.float32) + forward_sum).astype(jnp.bfloat16)
-    grad_out = (grad_rows.astype(jnp.float32) + back_sum).astype(jnp.bfloat16)
+    sums = jnp.sum(exchanged(terms).astype(jnp.float32), axis=0)
+    layer_out = (fwd_rows.astype(jnp.float32) + sums[:, :share]).astype(jnp.bfloat16)
+    grad_out = (grad_rows.astype(jnp.float32) + sums[:, share:]).astype(jnp.bfloat16)
     next_rows = passed_along(layer_out, "section", 1)
     prev_rows = passed_along(grad_out, "section", -1)
     return (next_rows[None], prev_rows[None], parked_rows[None])
-
-
-def partial_swap(bit_number):
-
-    def swapper(values):
-        return swap_on_bit(values, bit_number)
-
-    return swapper
 
 
 def solution(mesh):

time: 626 us -> 187 us (0.30)
  the two profiles are of different devices: /device:TPU:1 before, /device:TPU:10 now
where the time goes in v1:
time: 187 us; the launch traced here: 185 us
  waiting for transfers between devices  57.7 us (31%)
  blocking collectives  37.8 us (20%)
  starting transfers between devices  33.7 us (18%)
  local copies, waits for them, and re-layouts  32.3 us (17%)
  matrix products  15.4 us (8%)
  other arithmetic  5.92 us (3%)
    all_to_all x1, waiting for transfers between devices, exchanged(): return lax.all_to_all(blocks, 'tensor', 0, 0, tiled=True)  48.4 us
    all_to_all x1, blocking collectives, exchanged(): return lax.all_to_all(blocks, 'tensor', 0, 0, tiled=True)  37.8 us
    ppermute x1, starting transfers between devices, swap_by(): return lambda held: lax.ppermute(held, 'section', route)  15.6 us
    all_to_all x1, starting transfers between devices, exchanged(): return lax.all_to_all(blocks, 'tensor', 0, 0, tiled=True)  11.8 us
    ppermute x2, waiting for transfers between devices, passed_along(): return lax.ppermute(block, axis, route)  7.2 us
    convert_element_type x3, local copies, waits for them, and re-layouts, branch(): normed = (widened * inverse * norm_scale[None, :]).astype(jnp.bfloat16)  6.43 us
    ppermute x2, starting transfers between devices, passed_along(): return lax.ppermute(block, axis, route)  6.37 us
    convert_element_type x2, local copies, waits for them, and re-layouts, branch(): widened = inputs.astype(jnp.float32)  4.34 us
  transfers between devices with their start and end apart: 4, of which 3 were waited for; matrix products, arithmetic and copies ran while one was open for 0% of the time, Pallas kernels for 0%

profile of v1, /device:TPU:10, one launch (start us, length us, event | category | flops | bytes accessed | tf_op | source)
XLA Modules:
  0.0 184.7 jit_solution(16762804874711253804)
XLA Ops:
  2.3 20.7 %conditional.1 = (bf16[64,384]{1,0:T(8,128)(2,1)}, bf16[64,192]{1,0:T(8,128)(2,1)}, bf16[64,192]{1,0:T(8,128)(2,1)S(1)}, bf16[1,64,192]{2,1,0:T(8,128)(2,1)S(1)}) conditional(s32[]{:T(128)} %bitcast.18, bf16[64,384]{1,0:T(8,128)(2,1)S(1)} %pad_maximum_fusion.2, bf16[64,384]{1,0:T(8,128)(2,1)S(1)} %pad_maximum_fusion.2, ...), branch_computations={%region_0.0_spmd, %region_1.0_spmd, %region_2.0_spmd, %region_3.0_... | conditional | bytes 344136 | solution.py:70
  2.3 15.6 %collective-permute-start.7 = (bf16[64,384]{1,0:T(8,128)(2,1)S(1)}, bf16[64,384]{1,0:T(8,128)(2,1)}, u32[]{:S(2)}, u32[]{:S(2)}) collective-permute-start(bf16[64,384]{1,0:T(8,128)(2,1)S(1)} %param.7), channel_id=1, source_target_pairs={{0,552},{24,528},{48,504},{72,480},{96,456},{120,432},{144,408},{1... | collective-permute-start | bytes 147464 | tf_op jit(solution)/shard_map/cond/branch_7_fun/ppermute | solution.py:68
  17.9 2.2 %collective-permute-done.7 = bf16[64,384]{1,0:T(8,128)(2,1)} collective-permute-done((bf16[64,384]{1,0:T(8,128)(2,1)S(1)}, bf16[64,384]{1,0:T(8,128)(2,1)}, u32[]{:S(2)}, u32[]{:S(2)}) %collective-permute-start.7) | collective-permute-done | bytes 49184 | tf_op jit(solution)/shard_map/cond/branch_7_fun/ppermute | solution.py:68
  20.1 1.4 slice.172
  23.9 1.6 broadcast_in_dim.150
  25.5 11.8 %all-to-all-start = ((bf16[24,64,576]{2,1,0:T(8,128)(2,1)}), bf16[24,64,576]{2,1,0:T(8,128)(2,1)S(1)}, u32[]{:S(2)}, u32[]{:S(2)}) async-start(bf16[24,64,576]{2,1,0:T(8,128)(2,1)} %broadcast_in_dim.150), calls=%async_computation | async-start | bytes 3932160 | tf_op jit(solution)/shard_map/all_to_all | solution.py:74
  37.7 48.4 %all-to-all-done = bf16[24,64,576]{2,1,0:T(8,128)(2,1)S(1)} async-done(((bf16[24,64,576]{2,1,0:T(8,128)(2,1)}), bf16[24,64,576]{2,1,0:T(8,128)(2,1)S(1)}, u32[]{:S(2)}, u32[]{:S(2)}) %all-to-all-start) | async-done | bytes 1769504 | tf_op jit(solution)/shard_map/all_to_all | solution.py:74
  86.6 1.4 fusion.59
  88.0 1.4 copy.76
  89.4 2.5 %convert_element_type.151 = bf16[64,4608]{1,0:T(8,128)(2,1)} reshape(bf16[64,24,192]{2,1,0:T(8,128)(2,1)} %copy.76) | data formatting | bytes 1179648 | tf_op jit(solution)/shard_map/convert_element_type | solution.py:30
  91.9 1.8 %fusion.49 = bf16[64,128]{1,0:T(8,128)(2,1)S(1)} fusion(bf16[64,4608]{1,0:T(8,128)(2,1)} %convert_element_type.151, bf16[1,4608,128]{2,1,0:T(8,128)(2,1)} %param.31), kind=kOutput, calls=%fused_computation.61 | convolution fusion | flops 75505664 | bytes 1785856 | tf_op jit(solution)/shard_map/dot_general | solution.py:37
  94.9 1.3 copy.84
  96.3 2.5 %convert_element_type.161 = bf16[64,4608]{1,0:T(8,128)(2,1)} reshape(bf16[64,24,192]{2,1,0:T(8,128)(2,1)} %copy.84) | data formatting | bytes 1179648 | tf_op jit(solution)/shard_map/jvp()/convert_element_type | solution.py:30
  98.8 1.5 fusion.40
  100.7 0.9 copy-done.1
  102.5 1.6 slice_bitcast_fusion
  104.6 1.5 reshape.284
  106.1 1.6 fusion.55
  111.5 1.2 convolution_convert_fusion.3
  112.7 1.8 reshape.283
  114.5 1.1 copy.124
  117.1 1.4 copy.93
  118.5 1.5 reshape.291
  119.9 2.1 %convolution_convert_fusion = bf16[64,4608]{1,0:T(8,128)(2,1)} fusion(bf16[64,128]{1,0:T(8,128)(2,1)} %reshape.291, bf16[1,4608,128]{2,1,0:T(8,128)(2,1)S(1)} %copy-done.2), kind=kOutput, calls=%fused_computation.1 | convolution fusion | flops 75792384 | bytes 1785856 | tf_op jit(solution)/shard_map/transpose(jvp())/dot_general | solution.py:32
  122.0 1.3 convolution_convert_fusion.1
  123.4 2.1 %copy.94 = f32[64,24,192]{2,1,0:T(8,128)} copy(f32[64,24,192]{2,0,1:T(8,128)S(1)} %copy-done.8) | data formatting | bytes 2359296 | tf_op jit(solution)/shard_map/jvp()/convert_element_type | solution.py:28
  125.5 2.3 %reshape.293 = f32[64,4608]{1,0:T(8,128)S(1)} reshape(f32[64,24,192]{2,1,0:T(8,128)} %copy.94) | data formatting | bytes 2359296 | tf_op jit(solution)/shard_map/jvp()/convert_element_type | solution.py:28
  127.8 1.4 multiply_reduce_fusion
  131.2 37.8 %all_to_all.10 = bf16[24,64,384]{2,1,0:T(8,128)(2,1)S(1)} all-to-all(bf16[24,64,384]{2,1,0:T(8,128)(2,1)S(1)} %pad_maximum_fusion), channel_id=1, replica_groups=mesh['section'=32,'tensor'=24] {'tensor'}, dimensions={0} | all-to-all | bytes 2359296 | tf_op jit(solution)/shard_map/all_to_all | solution.py:74
  169.8 4.5 %collective-permute-start.17 = (bf16[64,192]{1,0:T(8,128)(2,1)S(1)}, bf16[64,192]{1,0:T(8,128)(2,1)S(1)}, u32[]{:S(2)}, u32[]{:S(2)}) collective-permute-start(bf16[64,192]{1,0:T(8,128)(2,1)S(1)} %get-tuple-element.46), channel_id=1, source_target_pairs={{24,0},{48,24},{72,48},{96,72},{120,96},{144,120},{168,144},{192,1... | collective-permute-start | bytes 73736 | tf_op jit(solution)/shard_map/ppermute | solution.py:15
  174.3 1.9 %collective-permute-start.16 = (bf16[64,192]{1,0:T(8,128)(2,1)S(1)}, bf16[64,192]{1,0:T(8,128)(2,1)S(1)}, u32[]{:S(2)}, u32[]{:S(2)}) collective-permute-start(bf16[64,192]{1,0:T(8,128)(2,1)S(1)} %get-tuple-element.47), channel_id=1, source_target_pairs={{0,24},{24,48},{48,72},{72,96},{96,120},{120,144},{144,168},{168,1... | collective-permute-start | bytes 73736 | tf_op jit(solution)/shard_map/ppermute | solution.py:15
  176.2 7.2 %collective-permute-done.16 = bf16[64,192]{1,0:T(8,128)(2,1)S(1)} collective-permute-done((bf16[64,192]{1,0:T(8,128)(2,1)S(1)}, bf16[64,192]{1,0:T(8,128)(2,1)S(1)}, u32[]{:S(2)}, u32[]{:S(2)}) %collective-permute-start.16) | collective-permute-done | bytes 24608 | tf_op jit(solution)/shard_map/ppermute | solution.py:15
  (105 shorter events, 16.3 us)
Async XLA Ops:
  0.6 93.1 %copy-start = (bf16[1,4608,128]{2,1,0:T(8,128)(2,1)S(1)}, bf16[1,4608,128]{2,1,0:T(8,128)(2,1)}, u32[]{:S(2)}) copy-start(bf16[1,4608,128]{2,1,0:T(8,128)(2,1)} %param.32) | copy-start | bytes 3538948
  2.3 21.6 %copy-start.14 = (bf16[1,64,192]{2,1,0:T(8,128)(2,1)S(1)}, bf16[1,64,192]{2,1,0:T(8,128)(2,1)}, u32[]{:S(2)}) copy-start(bf16[1,64,192]{2,1,0:T(8,128)(2,1)} %param.26) | copy-start | bytes 73732
  2.3 21.6 %copy-start.17 = (bf16[1,64,192]{2,1,0:T(8,128)(2,1)S(1)}, bf16[1,64,192]{2,1,0:T(8,128)(2,1)}, u32[]{:S(2)}) copy-start(bf16[1,64,192]{2,1,0:T(8,128)(2,1)} %param.27) | copy-start | bytes 73732
  2.3 17.7 %collective-permute-start.7 = (bf16[64,384]{1,0:T(8,128)(2,1)S(1)}, bf16[64,384]{1,0:T(8,128)(2,1)}, u32[]{:S(2)}, u32[]{:S(2)}) collective-permute-start(bf16[64,384]{1,0:T(8,128)(2,1)S(1)} %param.7), channel_id=1, source_target_pairs={{0,552},{24,528},{48,504},{72,480},{96,456},{120,432},{144,408},{1... | collective-permute-start | bytes 147464 | tf_op jit(solution)/shard_map/cond/branch_7_fun/ppermute | solution.py:68
  23.0 0.9 copy-start.20
  25.5 11.8 %copy-start.21 = (f32[1,4608]{1,0:T(1,128)S(1)}, f32[1,4608]{1,0:T(1,128)}, u32[]{:S(2)}) copy-start(f32[1,4608]{1,0:T(1,128)} %param.29) | copy-start | bytes 55300
  25.5 12.0 %copy-start.26 = (s32[1,2,8]{2,1,0:T(2,128)S(1)}, s32[1,2,8]{2,1,0:T(2,128)}, u32[]{:S(2)}) copy-start(s32[1,2,8]{2,1,0:T(2,128)} %param.34) | copy-start | bytes 196
  25.5 60.6 %all-to-all-start = ((bf16[24,64,576]{2,1,0:T(8,128)(2,1)}), bf16[24,64,576]{2,1,0:T(8,128)(2,1)S(1)}, u32[]{:S(2)}, u32[]{:S(2)}) async-start(bf16[24,64,576]{2,1,0:T(8,128)(2,1)} %broadcast_in_dim.150), calls=%async_computation | async-start | bytes 3932160 | tf_op jit(solution)/shard_map/all_to_all | solution.py:74
  37.4 50.6 %copy-start.16 = (f32[4608]{0:T(1024)}, f32[4608]{0:T(1024)S(1)}, u32[]{:S(2)}) copy-start(f32[4608]{0:T(1024)S(1)} %reduce.4) | copy-start | bytes 55300
  86.6 1.4 copy-start.24
  86.6 1.4 copy-start.22
  91.9 1.9 %copy-start.5 = (bf16[64,4608]{1,0:T(8,128)(2,1)S(1)}, bf16[64,4608]{1,0:T(8,128)(2,1)}, u32[]{:S(2)}) copy-start(bf16[64,4608]{1,0:T(8,128)(2,1)} %convert_element_type.151) | copy-start | bytes 1769476
  93.8 1.1 copy-start.11
  98.8 1.6 copy-start.3
  98.8 1.6 copy-start.7
  100.4 1.3 copy-start.1
  100.4 1.4 copy-start.6
  104.2 2.0 %copy-start.9 = (bf16[1,128,4608]{2,1,0:T(8,128)(2,1)S(1)}, bf16[1,128,4608]{2,1,0:T(8,128)(2,1)}, u32[]{:S(2)}) copy-start(bf16[1,128,4608]{2,1,0:T(8,128)(2,1)} %param.33) | copy-start | bytes 3538948
  114.5 1.1 copy-start.19
  114.5 5.4 %copy-start.2 = (bf16[1,4608,128]{2,1,0:T(8,128)(2,1)S(1)}, bf16[1,4608,128]{2,1,0:T(8,128)(2,1)}, u32[]{:S(2)}) copy-start(bf16[1,4608,128]{2,1,0:T(8,128)(2,1)} %param.30) | copy-start | bytes 3538948
  115.6 6.4 %copy-start.4 = (bf16[1,4608,128]{2,1,0:T(8,128)(2,1)S(1)}, bf16[1,4608,128]{2,1,0:T(8,128)(2,1)}, u32[]{:S(2)}) copy-start(bf16[1,4608,128]{2,1,0:T(8,128)(2,1)} %param.31) | copy-start | bytes 3538948
  122.0 1.4 copy-start.8
  125.5 2.3 %copy-start.12 = (bf16[64,4608]{1,0:T(8,128)(2,1)S(1)}, bf16[64,4608]{1,0:T(8,128)(2,1)}, u32[]{:S(2)}) copy-start(bf16[64,4608]{1,0:T(8,128)(2,1)} %convolution_convert_fusion) | copy-start | bytes 1769476
  125.5 2.3 %copy-start.13 = (bf16[64,4608]{1,0:T(8,128)(2,1)S(1)}, bf16[64,4608]{1,0:T(8,128)(2,1)}, u32[]{:S(2)}) copy-start(bf16[64,4608]{1,0:T(8,128)(2,1)} %convolution_convert_fusion.1) | copy-start | bytes 1769476
  127.8 1.5 copy-start.25
  127.8 1.5 copy-start.23
  129.6 1.1 copy-start.10
  169.0 0.8 copy-start.15
  169.0 0.8 copy-start.18
  169.8 6.4 %collective-permute-start.17 = (bf16[64,192]{1,0:T(8,128)(2,1)S(1)}, bf16[64,192]{1,0:T(8,128)(2,1)S(1)}, u32[]{:S(2)}, u32[]{:S(2)}) collective-permute-start(bf16[64,192]{1,0:T(8,128)(2,1)S(1)} %get-tuple-element.46), channel_id=1, source_target_pairs={{24,0},{48,24},{72,48},{96,72},{120,96},{144,120},{168,144},{192,1... | collective-permute-start | bytes 73736 | tf_op jit(solution)/shard_map/ppermute | solution.py:15
  174.3 9.1 %collective-permute-start.16 = (bf16[64,192]{1,0:T(8,128)(2,1)S(1)}, bf16[64,192]{1,0:T(8,128)(2,1)S(1)}, u32[]{:S(2)}, u32[]{:S(2)}) collective-permute-start(bf16[64,192]{1,0:T(8,128)(2,1)S(1)} %get-tuple-element.47), channel_id=1, source_target_pairs={{0,24},{24,48},{48,72},{72,96},{96,120},{120,144},{144,168},{168,1... | collective-permute-start | bytes 73736 | tf_op jit(solution)/shard_map/ppermute | solution.py:15

commit v2 on v1

v2 whole, which is shorter than its diff:
```python
import math

import jax
import jax.numpy as jnp
from jax import lax
from jax.experimental import pallas as pl
from jax.experimental.pallas import tpu as pltpu
from jax.sharding import PartitionSpec as P

HD = 64
EPS = 1e-05
F32 = jnp.float32
BF16 = jnp.bfloat16


def dot(a, b):
    return jnp.dot(a, b, preferred_element_type=F32)


def dot_t(a, b):
    return lax.dot_general(a, b, (((1,), (1,)), ((), ())), preferred_element_type=F32)


def dot_tl(a, b):
    return lax.dot_general(a, b, (((0,), (0,)), ((), ())), preferred_element_type=F32)


def causal(off_ref, which, rows):
    row = lax.broadcasted_iota(jnp.int32, (rows, rows), 0)
    col = lax.broadcasted_iota(jnp.int32, (rows, rows), 1)
    row_start = jnp.zeros((rows, rows), jnp.int32)
    col_start = jnp.zeros((rows, rows), jnp.int32)
    for c in range(off_ref.shape[2]):
        start = off_ref[0, which, c]
        row_start = jnp.where((row >> 3) == c, start, row_start)
        col_start = jnp.where((col >> 3) == c, start, col_start)
    return row_start + (row & 7) >= col_start + (col & 7)


def softmax(queries, keys, mask):
    scores = dot_t(queries, keys) * (1.0 / math.sqrt(HD))
    scores = jnp.where(mask, scores, -1e30)
    top = jnp.max(scores, axis=1, keepdims=True)
    grown = jnp.exp(scores - top)
    return grown / jnp.sum(grown, axis=1, keepdims=True)


def heads_of(*arrays):
    count = arrays[0].shape[1] // HD
    return [tuple(a[:, h * HD : (h + 1) * HD] for a in arrays) for h in range(count)]


def forward_kernel(off_ref, pair_ref, gain_ref, wq_ref, wk_ref, wv_ref, wo_ref, term_ref, dctx_ref, xs, gs):
    parts, rows, wide = pair_ref.shape
    share = wide // 2
    half = rows // 2
    width = parts * share
    squares = jnp.zeros((rows, wide), F32)
    for u in range(parts // 2):
        a = pair_ref[2 * u]
        b = pair_ref[2 * u + 1]
        span = slice(wide * u, wide * (u + 1))
        x = jnp.concatenate([a[:, :share], b[:, :share]], axis=1)
        xs[:, span] = x
        gs[:, span] = jnp.concatenate([a[:, share:], b[:, share:]], axis=1)
        x = x.astype(F32)
        squares = squares + x * x
    inverse = lax.rsqrt(jnp.sum(squares, axis=1, keepdims=True) * (1.0 / width) + EPS)
    for u in range(parts // 2):
        span = slice(wide * u, wide * (u + 1))
        xs[:, span] = (xs[:, span].astype(F32) * inverse * gain_ref[:, span]).astype(BF16)
    normed = xs[...]
    queries = dot(normed, wq_ref[...]).astype(BF16)
    keys = dot(normed, wk_ref[...]).astype(BF16)
    values = dot(normed, wv_ref[...]).astype(BF16)
    mask = causal(off_ref, 0, rows)
    context = jnp.concatenate(
        [dot(softmax(q, k, mask).astype(BF16), v) for q, k, v in heads_of(queries, keys, values)], axis=1
    ).astype(BF16)
    for u in range(parts // 2):
        span = slice(wide * u, wide * (u + 1))
        out = dot(context, wo_ref[:, span]).astype(BF16)
        term_ref[2 * u] = jnp.concatenate([out[:half, :share], out[half:, :share]], axis=1)
        term_ref[2 * u + 1] = jnp.concatenate([out[:half, share:], out[half:, share:]], axis=1)
    dctx_ref[...] = dot_t(gs[...], wo_ref[...]).astype(BF16)


def backward_kernel(off_ref, back_ref, dctx_ref, gain_ref, wq_ref, wk_ref, wv_ref, term_ref, xs, ns, ds):
    parts, half, wide = back_ref.shape
    share = wide // 2
    rows = half * 2
    width = parts * share
    squares = jnp.zeros((rows, wide), F32)
    for u in range(parts // 2):
        a = back_ref[2 * u]
        b = back_ref[2 * u + 1]
        span = slice(wide * u, wide * (u + 1))
        x = jnp.concatenate(
            [
                jnp.concatenate([a[:, :share], b[:, :share]], axis=1),
                jnp.concatenate([a[:, share:], b[:, share:]], axis=1),
            ],
            axis=0,
        )
        xs[:, span] = x
        x = x.astype(F32)
        squares = squares + x * x
    inverse = lax.rsqrt(jnp.sum(squares, axis=1, keepdims=True) * (1.0 / width) + EPS)
    for u in range(parts // 2):
        span = slice(wide * u, wide * (u + 1))
        ns[:, span] = (xs[:, span].astype(F32) * inverse * gain_ref[:, span]).astype(BF16)
    normed = ns[...]
    queries = dot(normed, wq_ref[...]).astype(BF16)
    keys = dot(normed, wk_ref[...]).astype(BF16)
    values = dot(normed, wv_ref[...]).astype(BF16)
    mask = causal(off_ref, 1, rows)
    grads = []
    for q, k, v, dc in heads_of(queries, keys, values, dctx_ref[...]):
        weights = softmax(q, k, mask)
        dvalue = dot_tl(weights.astype(BF16), dc)
        dweights = dot_t(dc, v).astype(BF16).astype(F32)
        dscores = weights * (dweights - jnp.sum(dweights * weights, axis=1, keepdims=True))
        dscores = jnp.where(mask, dscores, 0.0) * (1.0 / math.sqrt(HD))
        dscores = dscores.astype(BF16)
        grads.append((dot(dscores, k), dot_tl(dscores, q), dvalue))
    dq, dk, dv = (jnp.concatenate(g, axis=1).astype(BF16) for g in zip(*grads))
    along = jnp.zeros((rows, wide), F32)
    for u in range(parts // 2):
        span = slice(wide * u, wide * (u + 1))
        grown = dot_t(dq, wq_ref[span, :]) + dot_t(dk, wk_ref[span, :]) + dot_t(dv, wv_ref[span, :])
        grown = grown * gain_ref[:, span]
        ds[:, span] = grown
        along = along + grown * xs[:, span].astype(F32)
    factor = jnp.sum(along, axis=1, keepdims=True) * (inverse * inverse * inverse) * (1.0 / width)
    for u in range(parts // 2):
        span = slice(wide * u, wide * (u + 1))
        out = (ds[:, span] * inverse - xs[:, span].astype(F32) * factor).astype(BF16)
        term_ref[2 * u] = jnp.concatenate([out[:half, :share], out[half:, :share]], axis=1)
        term_ref[2 * u + 1] = jnp.concatenate([out[:half, share:], out[half:, share:]], axis=1)


def kernel_call(body, outs, scratch, args):
    vmem = pl.BlockSpec(memory_space=pltpu.VMEM)
    specs = [pl.BlockSpec(memory_space=pltpu.SMEM)] + [vmem] * (len(args) - 1)
    return pl.pallas_call(
        body,
        out_shape=outs,
        in_specs=specs,
        out_specs=jax.tree.map(lambda _: vmem, outs),
        scratch_shapes=scratch,
        compiler_params=pltpu.CompilerParams(vmem_limit_bytes=VMEM_LIMIT),
    )(*args)


VMEM_LIMIT = 24 * 2**20


def forward_term(offsets, pair, gain, wq, wk, wv, wo):
    parts, rows, wide = pair.shape
    width = gain.shape[1]
    outs = (
        jax.ShapeDtypeStruct((parts, rows // 2, wide), BF16),
        jax.ShapeDtypeStruct((rows, wo.shape[0]), BF16),
    )
    scratch = [pltpu.VMEM((rows, width), BF16), pltpu.VMEM((rows, width), BF16)]
    return kernel_call(forward_kernel, outs, scratch, (offsets, pair, gain, wq, wk, wv, wo))


def backward_term(offsets, back, dctx, gain, wq, wk, wv):
    _, half, _ = back.shape
    width = gain.shape[1]
    outs = jax.ShapeDtypeStruct(back.shape, BF16)
    scratch = [
        pltpu.VMEM((2 * half, width), BF16),
        pltpu.VMEM((2 * half, width), BF16),
        pltpu.VMEM((2 * half, width), F32),
    ]
    return kernel_call(backward_kernel, outs, scratch, (offsets, back, dctx, gain, wq, wk, wv))


def folded(block):
    half = block.shape[0] // 2
    return jnp.concatenate([block[:half], block[half:]], axis=1)


def unfolded(block):
    share = block.shape[1] // 2
    return jnp.concatenate([block[:, :share], block[:, share:]], axis=0)


def passed_along(block, axis, distance):
    devices = range(lax.axis_size(axis))
    route = [(i - distance, i) for i in devices if i - distance in devices]
    return lax.ppermute(block, axis, route)


def mirrored(values, mask):
    section_count = lax.axis_size("section")
    half = section_count // 2

    def swap_by(distance):
        route = [(i, i ^ distance) for i in range(section_count)]
        return lambda held: lax.ppermute(held, "section", route)

    return lax.switch(mask - half, [swap_by(half + i) for i in range(half)], values)


def exchanged(blocks):
    return lax.all_to_all(blocks, "tensor", 0, 0, tiled=True)


def spread(block):
    return exchanged(jnp.broadcast_to(block[None], (lax.axis_size("tensor"),) + block.shape))


def total(rows, terms):
    summed = jnp.sum(exchanged(terms).astype(F32), axis=0)
    return unfolded((folded(rows).astype(F32) + summed).astype(BF16))


def local(fwd_input, bwd_grad, parked, norm_gain, w_query, w_key, w_value, w_out, offsets, mirror):
    fwd_rows = fwd_input[0]
    grad_rows = bwd_grad[0]
    half = fwd_rows.shape[0] // 2
    pair = spread(jnp.concatenate([fwd_rows, grad_rows], axis=1))
    swapped = mirrored(jnp.concatenate([folded(fwd_rows), folded(parked[0])], axis=0), mirror[0])
    back = spread(swapped[half:])
    parked_rows = unfolded(swapped[:half])
    term, dctx = forward_term(offsets, pair, norm_gain, w_query[0], w_key[0], w_value[0], w_out[0])
    layer_out = total(fwd_rows, term)
    next_rows = passed_along(layer_out, "section", 1)
    back_term = backward_term(offsets, back, dctx, norm_gain, w_query[0], w_key[0], w_value[0])
    grad_out = total(grad_rows, back_term)
    prev_rows = passed_along(grad_out, "section", -1)
    return (next_rows[None], prev_rows[None], parked_rows[None])


def solution(mesh):
    in_specs = (
        P("section", None, "tensor"),
        P("section", None, "tensor"),
        P("section", None, "tensor"),
        P("section", None),
        P("section", None, "tensor"),
        P("section", None, "tensor"),
        P("section", None, "tensor"),
        P("section", "tensor", None),
        P("section", None, None),
        P(),
    )
    out_specs = (
        P("section", None, "tensor"),
        P("section", None, "tensor"),
        P("section", None, "tensor"),
    )
    return jax.shard_map(local, mesh=mesh, in_specs=in_specs, out_specs=out_specs, check_vma=False)
```

time: 187 us -> 137 us (0.73)
  the two profiles are of different devices: /device:TPU:10 before, /device:TPU:1 now
where the time goes in v2:
time: 137 us; the launch traced here: 136 us
  starting transfers between devices  67.5 us (49%)
  waiting for transfers between devices  42 us (31%)
  local copies, waits for them, and re-layouts  15 us (11%)
  Pallas kernels  7.48 us (5%)
  other arithmetic  2.99 us (2%)
    all_to_all x4, starting transfers between devices, exchanged(): return lax.all_to_all(blocks, 'tensor', 0, 0, tiled=True)  34.2 us
    ppermute x2, starting transfers between devices, passed_along(): return lax.ppermute(block, axis, route)  17.5 us
    ppermute x1, starting transfers between devices, swap_by(): return lambda held: lax.ppermute(held, 'section', route)  15.9 us
    ppermute x1, waiting for transfers between devices, swap_by(): return lambda held: lax.ppermute(held, 'section', route)  15.6 us
    all_to_all x4, waiting for transfers between devices, exchanged(): return lax.all_to_all(blocks, 'tensor', 0, 0, tiled=True)  15.2 us
    ppermute x2, waiting for transfers between devices, passed_along(): return lax.ppermute(block, axis, route)  11.2 us
    unnamed x36, local copies, waits for them, and re-layouts  8.24 us
    pallas_call x2, Pallas kernels, kernel_call(): pl.pallas_call(body, out_shape=outs, in_specs=specs, out_specs=jax.tree.m...  7.48 us
  transfers between devices with their start and end apart: 7, of which 5 were waited for; matrix products, arithmetic and copies ran while one was open for 4% of the time, Pallas kernels for 6%

profile of v2, /device:TPU:1, one launch (start us, length us, event | category | flops | bytes accessed | tf_op | source)
XLA Modules:
  0.0 135.8 jit_solution(12852225443483372986)
XLA Ops:
  0.6 0.9 pad_maximum_fusion
  1.5 1.2 broadcast_in_dim.10
  2.7 11.6 %all-to-all-start = ((bf16[24,64,384]{2,1,0:T(8,128)(2,1)}), bf16[24,64,384]{2,1,0:T(8,128)(2,1)S(1)}, u32[]{:S(2)}, u32[]{:S(2)}) async-start(bf16[24,64,384]{2,1,0:T(8,128)(2,1)} %broadcast_in_dim.10), calls=%async_computation | async-start | bytes 2359296 | tf_op jit(solution)/shard_map/all_to_all | solution.py:209
  14.4 0.8 slice_bitcast_fusion.5
  15.2 0.7 slice_bitcast_fusion.1
  16.1 31.5 %conditional.1 = (bf16[64,384]{1,0:T(8,128)(2,1)}) conditional(s32[]{:T(128)} %bitcast.11, bf16[64,384]{1,0:T(8,128)(2,1)S(1)} %maximum_maximum_fusion, bf16[64,384]{1,0:T(8,128)(2,1)S(1)} %maximum_maximum_fusion, bf16[64,384]{1,0:T(8,128)(2,1)S(1)} %maximum_maximum_fusion, ...), branch_computations={%region_1.0_spmd, %region_2.0_spmd, %region_3.0_spmd, %region_4.0_... | conditional | bytes 196656 | solution.py:205
  16.1 15.9 %collective-permute-start.12 = (bf16[64,384]{1,0:T(8,128)(2,1)S(1)}, bf16[64,384]{1,0:T(8,128)(2,1)}, u32[]{:S(2)}, u32[]{:S(2)}) collective-permute-start(bf16[64,384]{1,0:T(8,128)(2,1)S(1)} %param.12), channel_id=1, source_target_pairs={{0,672},{24,696},{48,720},{72,744},{96,576},{120,600},{144,624},{1... | collective-permute-start | bytes 147464 | tf_op jit(solution)/shard_map/cond/branch_12_fun/ppermute | solution.py:203
  32.0 15.6 %collective-permute-done.12 = bf16[64,384]{1,0:T(8,128)(2,1)} collective-permute-done((bf16[64,384]{1,0:T(8,128)(2,1)S(1)}, bf16[64,384]{1,0:T(8,128)(2,1)}, u32[]{:S(2)}, u32[]{:S(2)}) %collective-permute-start.12) | collective-permute-done | bytes 49184 | tf_op jit(solution)/shard_map/cond/branch_12_fun/ppermute | solution.py:203
  47.5 1.3 slice.87
  48.9 1.6 %broadcast_in_dim.23 = bf16[24,32,384]{2,1,0:T(8,128)(2,1)} broadcast(bf16[32,384]{1,0:T(8,128)(2,1)} %slice.87), dimensions={1,2} | broadcast | bytes 614400 | tf_op jit(solution)/shard_map/broadcast_in_dim | solution.py:213
  50.5 6.4 %all-to-all-start.2 = ((bf16[24,32,384]{2,1,0:T(8,128)(2,1)}), bf16[24,32,384]{2,1,0:T(8,128)(2,1)}, u32[]{:S(2)}, u32[]{:S(2)}) async-start(bf16[24,32,384]{2,1,0:T(8,128)(2,1)} %broadcast_in_dim.23), calls=%async_computation.2 | async-start | bytes 1179648 | tf_op jit(solution)/shard_map/all_to_all | solution.py:209
  56.9 1.3 copy-done.2
  58.2 1.3 copy-done.5
  59.4 0.7 copy-done.7
  60.2 0.7 copy-done.9
  60.8 2.7 %shard_map.121 = (bf16[24,32,384]{2,1,0:T(8,128)(2,1)S(1)}, bf16[64,128]{1,0:T(8,128)(2,1)S(1)}) custom-call(s32[1,2,8]{2,1,0:T(2,128)S(1)} %copy-done.9, bf16[24,64,384]{2,1,0:T(8,128)(2,1)S(1)} %all-to-all-done.pair_ref, f32[1,4608]{1,0:T(1,128)S(1)} %copy-done.7, bf16[4608,128]{1,0:T(8,128)(2,1)S(1)} %bitcast.24, bf16[4608,128]{1,0:T(8,128)(2,1)S(1)} %bitcast.26, ...), custom_call_target="tpu_custom_call" | custom-call | tf_op jit(solution)/shard_map/pallas_call | solution.py:145
  63.5 0.8 copy-done.6
  64.4 6.7 %all-to-all-done.2.back_ref = bf16[24,32,384]{2,1,0:T(8,128)(2,1)} async-done(((bf16[24,32,384]{2,1,0:T(8,128)(2,1)}), bf16[24,32,384]{2,1,0:T(8,128)(2,1)}, u32[]{:S(2)}, u32[]{:S(2)}) %all-to-all-start.2) | async-done | bytes 589856 | tf_op jit(solution)/shard_map/all_to_all | solution.py:209
  71.1 8.6 %all-to-all-start.1 = ((bf16[24,32,384]{2,1,0:T(8,128)(2,1)}), bf16[24,32,384]{2,1,0:T(8,128)(2,1)}, u32[]{:S(2)}, u32[]{:S(2)}) async-start(bf16[24,32,384]{2,1,0:T(8,128)(2,1)} %copy-done.6), calls=%async_computation.1 | async-start | bytes 1179648 | tf_op jit(solution)/shard_map/all_to_all | solution.py:209
  79.8 0.7 copy-done.8
  80.5 0.7 copy-done.10
  81.1 4.8 %shard_map.122 = bf16[24,32,384]{2,1,0:T(8,128)(2,1)S(1)} custom-call(s32[1,2,8]{2,1,0:T(2,128)S(1)} %copy-done.10, bf16[24,32,384]{2,1,0:T(8,128)(2,1)} %all-to-all-done.2.back_ref, bf16[64,128]{1,0:T(8,128)(2,1)S(1)} %get-tuple-element.39.dctx_ref, f32[1,4608]{1,0:T(1,128)S(1)} %copy-done.8, bf16[4608,128]{1,0:T(8,128)(2,1)S(1)} %bitcast.25, ...), custom_call_target="tpu_custom_call" | custom-call | tf_op jit(solution)/shard_map/pallas_call | solution.py:145
  86.0 0.8 copy-done.4
  86.8 8.2 %all-to-all-done.1 = bf16[24,32,384]{2,1,0:T(8,128)(2,1)} async-done(((bf16[24,32,384]{2,1,0:T(8,128)(2,1)}), bf16[24,32,384]{2,1,0:T(8,128)(2,1)}, u32[]{:S(2)}, u32[]{:S(2)}) %all-to-all-start.1) | async-done | bytes 589856 | tf_op jit(solution)/shard_map/all_to_all | solution.py:209
  94.9 7.6 %all-to-all-start.3 = ((bf16[24,32,384]{2,1,0:T(8,128)(2,1)}), bf16[24,32,384]{2,1,0:T(8,128)(2,1)S(1)}, u32[]{:S(2)}, u32[]{:S(2)}) async-start(bf16[24,32,384]{2,1,0:T(8,128)(2,1)} %copy-done.4), calls=%async_computation.3 | async-start | bytes 1179648 | tf_op jit(solution)/shard_map/all_to_all | solution.py:209
  102.5 0.9 fusion
  103.4 1.2 convert_reduce_fusion.1
  104.7 12.6 %collective-permute-start.16 = (bf16[64,192]{1,0:T(8,128)(2,1)S(1)}, bf16[64,192]{1,0:T(8,128)(2,1)S(1)}, u32[]{:S(2)}, u32[]{:S(2)}) collective-permute-start(bf16[64,192]{1,0:T(8,128)(2,1)S(1)} %pad_maximum_fusion.1), channel_id=1, source_target_pairs={{0,24},{24,48},{48,72},{72,96},{96,120},{120,144},{144,168},{168,1... | collective-permute-start | bytes 73736 | tf_op jit(solution)/shard_map/ppermute | solution.py:194
  118.0 4.8 %collective-permute-start.17 = (bf16[64,192]{1,0:T(8,128)(2,1)S(1)}, bf16[64,192]{1,0:T(8,128)(2,1)S(1)}, u32[]{:S(2)}, u32[]{:S(2)}) collective-permute-start(bf16[64,192]{1,0:T(8,128)(2,1)S(1)} %pad_maximum_fusion.2), channel_id=1, source_target_pairs={{24,0},{48,24},{72,48},{96,72},{120,96},{144,120},{168,144},{192,1... | collective-permute-start | bytes 73736 | tf_op jit(solution)/shard_map/ppermute | solution.py:194
  122.8 0.6 maximum_bitcast_fusion
  123.4 11.2 %collective-permute-done.17 = bf16[64,192]{1,0:T(8,128)(2,1)S(1)} collective-permute-done((bf16[64,192]{1,0:T(8,128)(2,1)S(1)}, bf16[64,192]{1,0:T(8,128)(2,1)S(1)}, u32[]{:S(2)}, u32[]{:S(2)}) %collective-permute-start.17) | collective-permute-done | bytes 24608 | tf_op jit(solution)/shard_map/ppermute | solution.py:194
  134.6 0.6 copy.31
  (39 shorter events, 1.5 us)
Async XLA Ops:
  2.7 11.7 %copy-start.16 = (s32[32]{0:T(128)S(1)}, s32[32]{0:T(128)}, u32[]{:S(2)}) copy-start(s32[32]{0:T(128)} %param.35) | copy-start | bytes 388
  2.7 54.2 %copy-start.1 = (bf16[1,4608,128]{2,1,0:T(8,128)(2,1)S(1)}, bf16[1,4608,128]{2,1,0:T(8,128)(2,1)}, u32[]{:S(2)}) copy-start(bf16[1,4608,128]{2,1,0:T(8,128)(2,1)} %param.31) | copy-start | bytes 3538948
  2.7 46.2 %all-to-all-start = ((bf16[24,64,384]{2,1,0:T(8,128)(2,1)}), bf16[24,64,384]{2,1,0:T(8,128)(2,1)S(1)}, u32[]{:S(2)}, u32[]{:S(2)}) async-start(bf16[24,64,384]{2,1,0:T(8,128)(2,1)} %broadcast_in_dim.10), calls=%async_computation | async-start | bytes 2359296 | tf_op jit(solution)/shard_map/all_to_all | solution.py:209
  14.3 42.5 %copy-start = (bf16[1,4608,128]{2,1,0:T(8,128)(2,1)S(1)}, bf16[1,4608,128]{2,1,0:T(8,128)(2,1)}, u32[]{:S(2)}) copy-start(bf16[1,4608,128]{2,1,0:T(8,128)(2,1)} %param.30) | copy-start | bytes 3538948
  15.2 0.8 copy-start.11
  15.2 0.8 copy-start.13
  16.1 31.4 %collective-permute-start.12 = (bf16[64,384]{1,0:T(8,128)(2,1)S(1)}, bf16[64,384]{1,0:T(8,128)(2,1)}, u32[]{:S(2)}, u32[]{:S(2)}) collective-permute-start(bf16[64,384]{1,0:T(8,128)(2,1)S(1)} %param.12), channel_id=1, source_target_pairs={{0,672},{24,696},{48,720},{72,744},{96,576},{120,600},{144,624},{1... | collective-permute-start | bytes 147464 | tf_op jit(solution)/shard_map/cond/branch_12_fun/ppermute | solution.py:203
  50.5 20.6 %all-to-all-start.2 = ((bf16[24,32,384]{2,1,0:T(8,128)(2,1)}), bf16[24,32,384]{2,1,0:T(8,128)(2,1)}, u32[]{:S(2)}, u32[]{:S(2)}) async-start(bf16[24,32,384]{2,1,0:T(8,128)(2,1)} %broadcast_in_dim.23), calls=%async_computation.2 | async-start | bytes 1179648 | tf_op jit(solution)/shard_map/all_to_all | solution.py:209
  56.9 1.3 copy-start.2
  58.2 1.3 copy-start.5
  59.4 0.7 copy-start.7
  60.2 0.7 copy-start.9
  63.5 0.8 copy-start.6
  64.4 15.4 %copy-start.3 = (bf16[1,4608,128]{2,1,0:T(8,128)(2,1)S(1)}, bf16[1,4608,128]{2,1,0:T(8,128)(2,1)}, u32[]{:S(2)}) copy-start(bf16[1,4608,128]{2,1,0:T(8,128)(2,1)} %param.32) | copy-start | bytes 3538948
  71.1 23.8 %all-to-all-start.1 = ((bf16[24,32,384]{2,1,0:T(8,128)(2,1)}), bf16[24,32,384]{2,1,0:T(8,128)(2,1)}, u32[]{:S(2)}, u32[]{:S(2)}) async-start(bf16[24,32,384]{2,1,0:T(8,128)(2,1)} %copy-done.6), calls=%async_computation.1 | async-start | bytes 1179648 | tf_op jit(solution)/shard_map/all_to_all | solution.py:209
  79.7 0.7 copy-start.8
  80.5 0.7 copy-start.10
  85.9 0.8 copy-start.4
  86.8 15.7 %copy-start.15 = (bf16[1,64,192]{2,1,0:T(8,128)(2,1)S(1)}, bf16[1,64,192]{2,1,0:T(8,128)(2,1)}, u32[]{:S(2)}) copy-start(bf16[1,64,192]{2,1,0:T(8,128)(2,1)} %param.27) | copy-start | bytes 73732
  86.8 17.8 %copy-start.12 = (bf16[32,192]{1,0:T(8,128)(2,1)S(1)}, bf16[32,192]{1,0:T(8,128)(2,1)}, u32[]{:S(2)}) copy-start(bf16[32,192]{1,0:T(8,128)(2,1)} %copy-done.11) | copy-start | bytes 36868
  86.8 17.8 %copy-start.14 = (bf16[32,192]{1,0:T(8,128)(2,1)S(1)}, bf16[32,192]{1,0:T(8,128)(2,1)}, u32[]{:S(2)}) copy-start(bf16[32,192]{1,0:T(8,128)(2,1)} %copy-done.13) | copy-start | bytes 36868
  94.9 22.8 %all-to-all-start.3 = ((bf16[24,32,384]{2,1,0:T(8,128)(2,1)}), bf16[24,32,384]{2,1,0:T(8,128)(2,1)S(1)}, u32[]{:S(2)}, u32[]{:S(2)}) async-start(bf16[24,32,384]{2,1,0:T(8,128)(2,1)} %copy-done.4), calls=%async_computation.3 | async-start | bytes 1179648 | tf_op jit(solution)/shard_map/all_to_all | solution.py:209
  104.7 18.7 %collective-permute-start.16 = (bf16[64,192]{1,0:T(8,128)(2,1)S(1)}, bf16[64,192]{1,0:T(8,128)(2,1)S(1)}, u32[]{:S(2)}, u32[]{:S(2)}) collective-permute-start(bf16[64,192]{1,0:T(8,128)(2,1)S(1)} %pad_maximum_fusion.1), channel_id=1, source_target_pairs={{0,24},{24,48},{48,72},{72,96},{96,120},{120,144},{144,168},{168,1... | collective-permute-start | bytes 73736 | tf_op jit(solution)/shard_map/ppermute | solution.py:194
  118.0 16.7 %collective-permute-start.17 = (bf16[64,192]{1,0:T(8,128)(2,1)S(1)}, bf16[64,192]{1,0:T(8,128)(2,1)S(1)}, u32[]{:S(2)}, u32[]{:S(2)}) collective-permute-start(bf16[64,192]{1,0:T(8,128)(2,1)S(1)} %pad_maximum_fusion.2), channel_id=1, source_target_pairs={{24,0},{48,24},{72,48},{96,72},{120,96},{144,120},{168,144},{192,1... | collective-permute-start | bytes 73736 | tf_op jit(solution)/shard_map/ppermute | solution.py:194

commit v3 on v2

--- a/solution.py
+++ b/solution.py
@@ -5,6 +5,7 @@
 from jax import lax
 from jax.experimental import pallas as pl
 from jax.experimental.pallas import tpu as pltpu
+from jax.sharding import Mesh
 from jax.sharding import PartitionSpec as P
 
 HD = 64
@@ -50,15 +51,27 @@
     return [tuple(a[:, h * HD : (h + 1) * HD] for a in arrays) for h in range(count)]
 
 
-def forward_kernel(off_ref, pair_ref, gain_ref, wq_ref, wk_ref, wv_ref, wo_ref, term_ref, dctx_ref, xs, gs):
-    parts, rows, wide = pair_ref.shape
+def gathered(own_ref, low_ref, high_ref, all_ref):
+    count = all_ref.shape[0]
+    at = lax.axis_index("run")
+    all_ref[at] = own_ref[...]
+    all_ref[lax.rem(at + count - 1, count)] = low_ref[...]
+    all_ref[lax.rem(at + 1, count)] = high_ref[...]
+
+
+def forward_kernel(
+    off_ref, own_ref, low_ref, high_ref, gain_ref, wq_ref, wk_ref, wv_ref, wo_ref, term_ref, dctx_ref, blocks, xs, gs
+):
+    gathered(own_ref, low_ref, high_ref, blocks)
+    runs, lines, rows, wide = blocks.shape
+    parts = runs * lines
     share = wide // 2
     half = rows // 2
     width = parts * share
     squares = jnp.zeros((rows, wide), F32)
     for u in range(parts // 2):
-        a = pair_ref[2 * u]
-        b = pair_ref[2 * u + 1]
+        a = blocks[(2 * u) % runs, (2 * u) // runs]
+        b = blocks[(2 * u + 1) % runs, (2 * u + 1) // runs]
         span = slice(wide * u, wide * (u + 1))
         x = jnp.concatenate([a[:, :share], b[:, :share]], axis=1)
         xs[:, span] = x
@@ -85,15 +98,35 @@
     dctx_ref[...] = dot_t(gs[...], wo_ref[...]).astype(BF16)
 
 
-def backward_kernel(off_ref, back_ref, dctx_ref, gain_ref, wq_ref, wk_ref, wv_ref, term_ref, xs, ns, ds):
-    parts, half, wide = back_ref.shape
+def backward_kernel(
+    off_ref,
+    own_ref,
+    low_ref,
+    high_ref,
+    dctx_ref,
+    gain_ref,
+    wq_ref,
+    wk_ref,
+    wv_ref,
+    stay_ref,
+    up_ref,
+    down_ref,
+    blocks,
+    terms,
+    xs,
+    ns,
+    ds,
+):
+    gathered(own_ref, low_ref, high_ref, blocks)
+    runs, lines, half, wide = blocks.shape
+    parts = runs * lines
     share = wide // 2
     rows = half * 2
     width = parts * share
     squares = jnp.zeros((rows, wide), F32)
     for u in range(parts // 2):
-        a = back_ref[2 * u]
-        b = back_ref[2 * u + 1]
+        a = blocks[(2 * u) % runs, (2 * u) // runs]
+        b = blocks[(2 * u + 1) % runs, (2 * u + 1) // runs]
         span = slice(wide * u, wide * (u + 1))
         x = jnp.concatenate(
             [
@@ -135,8 +168,14 @@
     for u in range(parts // 2):
         span = slice(wide * u, wide * (u + 1))
         out = (ds[:, span] * inverse - xs[:, span].astype(F32) * factor).astype(BF16)
-        term_ref[2 * u] = jnp.concatenate([out[:half, :share], out[half:, :share]], axis=1)
-        term_ref[2 * u + 1] = jnp.concatenate([out[:half, share:], out[half:, share:]], axis=1)
+        for i in range(2):
+            t = 2 * u + i
+            cols = slice(share * i, share * (i + 1))
+            terms[t % runs, t // runs] = jnp.concatenate([out[:half, cols], out[half:, cols]], axis=1)
+    at = lax.axis_index("run")
+    stay_ref[...] = terms[at]
+    up_ref[...] = terms[lax.rem(at + 1, runs)]
+    down_ref[...] = terms[lax.rem(at + runs - 1, runs)]
 
 
 def kernel_call(body, outs, scratch, args):
@@ -152,30 +191,38 @@
     )(*args)
 
 
-VMEM_LIMIT = 24 * 2**20
-
-
-def forward_term(offsets, pair, gain, wq, wk, wv, wo):
-    parts, rows, wide = pair.shape
+VMEM_LIMIT = 16 * 2**20
+
+
+def forward_term(offsets, blocks, gain, wq, wk, wv, wo):
+    lines, rows, wide = blocks[0].shape
     width = gain.shape[1]
+    runs = len(blocks)
     outs = (
-        jax.ShapeDtypeStruct((parts, rows // 2, wide), BF16),
+        jax.ShapeDtypeStruct((runs * lines, rows // 2, wide), BF16),
         jax.ShapeDtypeStruct((rows, wo.shape[0]), BF16),
     )
-    scratch = [pltpu.VMEM((rows, width), BF16), pltpu.VMEM((rows, width), BF16)]
-    return kernel_call(forward_kernel, outs, scratch, (offsets, pair, gain, wq, wk, wv, wo))
-
-
-def backward_term(offsets, back, dctx, gain, wq, wk, wv):
-    _, half, _ = back.shape
+    scratch = [
+        pltpu.VMEM((runs, lines, rows, wide), BF16),
+        pltpu.VMEM((rows, width), BF16),
+        pltpu.VMEM((rows, width), BF16),
+    ]
+    return kernel_call(forward_kernel, outs, scratch, (offsets, *blocks, gain, wq, wk, wv, wo))
+
+
+def backward_term(offsets, blocks, dctx, gain, wq, wk, wv):
+    lines, half, wide = blocks[0].shape
     width = gain.shape[1]
-    outs = jax.ShapeDtypeStruct(back.shape, BF16)
+    runs = len(blocks)
+    outs = (jax.ShapeDtypeStruct((lines, half, wide), BF16),) * runs
     scratch = [
+        pltpu.VMEM((runs, lines, half, wide), BF16),
+        pltpu.VMEM((runs, lines, half, wide), BF16),
         pltpu.VMEM((2 * half, width), BF16),
         pltpu.VMEM((2 * half, width), BF16),
         pltpu.VMEM((2 * half, width), F32),
     ]
-    return kernel_call(backward_kernel, outs, scratch, (offsets, back, dctx, gain, wq, wk, wv))
+    return kernel_call(backward_kernel, outs, scratch, (offsets, *blocks, dctx, gain, wq, wk, wv))
 
 
 def folded(block):
@@ -188,33 +235,44 @@
     return jnp.concatenate([block[:, :share], block[:, share:]], axis=0)
 
 
-def passed_along(block, axis, distance):
-    devices = range(lax.axis_size(axis))
+SECTION = ("x", "far", "core")
+TENSOR = ("line", "run")
+RUN = 3
+
+
+def passed_along(block, distance):
+    devices = range(lax.axis_size(SECTION))
     route = [(i - distance, i) for i in devices if i - distance in devices]
-    return lax.ppermute(block, axis, route)
+    return lax.ppermute(block, SECTION, route)
+
+
+def around(block, axis, distance):
+    count = lax.axis_size(axis)
+    return lax.ppermute(block, axis, [(i, (i + distance) % count) for i in range(count)])
 
 
 def mirrored(values, mask):
-    section_count = lax.axis_size("section")
+    section_count = lax.axis_size(SECTION)
     half = section_count // 2
 
     def swap_by(distance):
         route = [(i, i ^ distance) for i in range(section_count)]
-        return lambda held: lax.ppermute(held, "section", route)
+        return lambda held: lax.ppermute(held, SECTION, route)
 
     return lax.switch(mask - half, [swap_by(half + i) for i in range(half)], values)
 
 
-def exchanged(blocks):
-    return lax.all_to_all(blocks, "tensor", 0, 0, tiled=True)
+def exchanged(blocks, axes):
+    return lax.all_to_all(blocks, axes, 0, 0, tiled=True)
 
 
 def spread(block):
-    return exchanged(jnp.broadcast_to(block[None], (lax.axis_size("tensor"),) + block.shape))
-
-
-def total(rows, terms):
-    summed = jnp.sum(exchanged(terms).astype(F32), axis=0)
+    own = exchanged(jnp.broadcast_to(block[None], (lax.axis_size("line"),) + block.shape), "line")
+    return own, around(own, "run", 1), around(own, "run", -1)
+
+
+def total(rows, blocks):
+    summed = jnp.sum(blocks.astype(F32), axis=0)
     return unfolded((folded(rows).astype(F32) + summed).astype(BF16))
 
 
@@ -227,30 +285,40 @@
     back = spread(swapped[half:])
     parked_rows = unfolded(swapped[:half])
     term, dctx = forward_term(offsets, pair, norm_gain, w_query[0], w_key[0], w_value[0], w_out[0])
-    layer_out = total(fwd_rows, term)
-    next_rows = passed_along(layer_out, "section", 1)
-    back_term = backward_term(offsets, back, dctx, norm_gain, w_query[0], w_key[0], w_value[0])
-    grad_out = total(grad_rows, back_term)
-    prev_rows = passed_along(grad_out, "section", -1)
+    layer_out = total(fwd_rows, exchanged(term, TENSOR))
+    next_rows = passed_along(layer_out, 1)
+    stay, up, down = backward_term(offsets, back, dctx, norm_gain, w_query[0], w_key[0], w_value[0])
+    low = around(up, "run", 1)
+    high = around(down, "run", -1)
+    column = (stay.astype(F32) + low.astype(F32) + high.astype(F32)).astype(BF16)
+    grad_out = total(grad_rows, exchanged(column, "line"))
+    prev_rows = passed_along(grad_out, -1)
     return (next_rows[None], prev_rows[None], parked_rows[None])
+
+
+def finer(mesh):
+    tensor = mesh.shape["tensor"]
+    x = math.isqrt(mesh.shape["section"] // 2)
+    shape = (x, mesh.shape["section"] // 2 // x, 2, tensor // RUN, RUN)
+    return Mesh(mesh.devices.reshape(shape), SECTION + TENSOR)
 
 
 def solution(mesh):
     in_specs = (
-        P("section", None, "tensor"),
-        P("section", None, "tensor"),
-        P("section", None, "tensor"),
-        P("section", None),
-        P("section", None, "tensor"),
-        P("section", None, "tensor"),
-        P("section", None, "tensor"),
-        P("section", "tensor", None),
-        P("section", None, None),
+        P(SECTION, None, TENSOR),
+        P(SECTION, None, TENSOR),
+        P(SECTION, None, TENSOR),
+        P(SECTION, None),
+        P(SECTION, None, TENSOR),
+        P(SECTION, None, TENSOR),
+        P(SECTION, None, TENSOR),
+        P(SECTION, TENSOR, None),
+        P(SECTION, None, None),
         P(),
     )
     out_specs = (
-        P("section", None, "tensor"),
-        P("section", None, "tensor"),
-        P("section", None, "tensor"),
+        P(SECTION, None, TENSOR),
+        P(SECTION, None, TENSOR),
+        P(SECTION, None, TENSOR),
     )
-    return jax.shard_map(local, mesh=mesh, in_specs=in_specs, out_specs=out_specs, check_vma=False)
+    return jax.shard_map(local, mesh=finer(mesh), in_specs=in_specs, out_specs=out_specs, check_vma=False)

time: 137 us -> 134 us (0.978)
  waiting for transfers between devices: 42 us -> 24.4 us
  blocking collectives: 0 us -> 15.5 us
  local copies, waits for them, and re-layouts: 15 us -> 8.31 us
  starting transfers between devices: 67.5 us -> 74.1 us
    ppermute x3 -> x9, starting transfers between devices: 33.3 us -> 56 us  [the longest x2 21.3 us: passed_along(): return lax.ppermute(block, SECTION, route)]
    all_to_all x4 -> x3, starting transfers between devices: 34.2 us -> 18.2 us  [exchanged(): return lax.all_to_all(blocks, axes, 0, 0, tiled=True)]
    all_to_all x0 -> x1, blocking collectives: none -> 15.5 us  [exchanged(): return lax.all_to_all(blocks, axes, 0, 0, tiled=True)]
    ppermute x3 -> x9, waiting for transfers between devices: 26.8 us -> 16.6 us  [the longest x6 14.6 us: around(): lax.ppermute(block, axis, [(i, (i + distance) % count) for i in range(cou...]
    all_to_all x4 -> x3, waiting for transfers between devices: 15.2 us -> 7.82 us  [exchanged(): return lax.all_to_all(blocks, axes, 0, 0, tiled=True)]
    unnamed x36 -> x22, local copies, waits for them, and re-layouts: 8.24 us -> 5.06 us
    slice x3, local copies, waits for them, and re-layouts: 1.58 us -> 0.01 us  [folded(): return jnp.concatenate([block[:half], block[half:]], axis=1)]
  transfers between devices with their start and end apart: 7 -> 12, of which waited for: 5 -> 7; matrix products, arithmetic and copies ran while one was open for 4% -> 2% of each run, Pallas kernels for 6% -> 3%
where the time goes in v3:
time: 134 us; the launch traced here: 133 us
  starting transfers between devices  74.1 us (55%)
  waiting for transfers between devices  24.4 us (18%)
  blocking collectives  15.5 us (12%)
  local copies, waits for them, and re-layouts  8.31 us (6%)
  Pallas kernels  7.89 us (6%)
  other arithmetic  2.04 us (2%)
    ppermute x2, starting transfers between devices, passed_along(): return lax.ppermute(block, SECTION, route)  21.3 us
    all_to_all x3, starting transfers between devices, exchanged(): return lax.all_to_all(blocks, axes, 0, 0, tiled=True)  18.2 us
    ppermute x6, starting transfers between devices, around(): lax.ppermute(block, axis, [(i, (i + distance) % count) for i in range(cou...  17.6 us
    ppermute x1, starting transfers between devices, swap_by(): return lambda held: lax.ppermute(held, SECTION, route)  17.1 us
    all_to_all x1, blocking collectives, exchanged(): return lax.all_to_all(blocks, axes, 0, 0, tiled=True)  15.5 us
    ppermute x6, waiting for transfers between devices, around(): lax.ppermute(block, axis, [(i, (i + distance) % count) for i in range(cou...  14.6 us
    pallas_call x2, Pallas kernels, kernel_call(): pl.pallas_call(body, out_shape=outs, in_specs=specs, out_specs=jax.tree.m...  7.89 us
    all_to_all x3, waiting for transfers between devices, exchanged(): return lax.all_to_all(blocks, axes, 0, 0, tiled=True)  7.82 us
  transfers between devices with their start and end apart: 12, of which 7 were waited for; matrix products, arithmetic and copies ran while one was open for 2% of the time, Pallas kernels for 3%

profile of v3, /device:TPU:1, one launch (start us, length us, event | category | flops | bytes accessed | tf_op | source)
XLA Modules:
  0.0 133.2 jit_solution(1350387870428935140)
XLA Ops:
  0.7 1.0 pad_maximum_fusion
  1.6 0.8 broadcast_in_dim.10
  2.4 7.6 %all-to-all-start = ((bf16[8,64,384]{2,1,0:T(8,128)(2,1)}), bf16[8,64,384]{2,1,0:T(8,128)(2,1)S(1)}, u32[]{:S(2)}, u32[]{:S(2)}) async-start(bf16[8,64,384]{2,1,0:T(8,128)(2,1)} %broadcast_in_dim.10), calls=%async_computation | async-start | bytes 786432 | tf_op jit(solution)/shard_map/all_to_all | solution.py:266
  10.2 18.7 %conditional.1 = (bf16[64,384]{1,0:T(8,128)(2,1)}) conditional(s32[]{:T(128)} %bitcast.11, bf16[64,384]{1,0:T(8,128)(2,1)S(1)} %maximum_maximum_fusion, bf16[64,384]{1,0:T(8,128)(2,1)S(1)} %maximum_maximum_fusion, bf16[64,384]{1,0:T(8,128)(2,1)S(1)} %maximum_maximum_fusion, ...), branch_computations={%region_1.0_spmd, %region_2.0_spmd, %region_3.0_spmd, %region_4.0_... | conditional | bytes 196656 | solution.py:262
  10.2 17.1 %collective-permute-start.12 = (bf16[64,384]{1,0:T(8,128)(2,1)S(1)}, bf16[64,384]{1,0:T(8,128)(2,1)}, u32[]{:S(2)}, u32[]{:S(2)}) collective-permute-start(bf16[64,384]{1,0:T(8,128)(2,1)S(1)} %param.12), channel_id=1, source_target_pairs={{0,672},{24,696},{48,720},{72,744},{96,576},{120,600},{144,624},{1... | collective-permute-start | bytes 147464 | tf_op jit(solution)/shard_map/cond/branch_12_fun/ppermute | solution.py:260
  27.3 1.6 %collective-permute-done.12 = bf16[64,384]{1,0:T(8,128)(2,1)} collective-permute-done((bf16[64,384]{1,0:T(8,128)(2,1)S(1)}, bf16[64,384]{1,0:T(8,128)(2,1)}, u32[]{:S(2)}, u32[]{:S(2)}) %collective-permute-start.12) | collective-permute-done | bytes 49184 | tf_op jit(solution)/shard_map/cond/branch_12_fun/ppermute | solution.py:260
  28.9 0.7 slice.87
  29.7 0.7 broadcast_in_dim.23
  30.4 6.6 %all-to-all-start.2 = ((bf16[8,32,384]{2,1,0:T(8,128)(2,1)}), bf16[8,32,384]{2,1,0:T(8,128)(2,1)S(1)}, u32[]{:S(2)}, u32[]{:S(2)}) async-start(bf16[8,32,384]{2,1,0:T(8,128)(2,1)} %broadcast_in_dim.23), calls=%async_computation.2 | async-start | bytes 393216 | tf_op jit(solution)/shard_map/all_to_all | solution.py:266
  37.0 3.0 %collective-permute-start.16 = (bf16[8,64,384]{2,1,0:T(8,128)(2,1)S(1)}, bf16[8,64,384]{2,1,0:T(8,128)(2,1)S(1)}, u32[]{:S(2)}, u32[]{:S(2)}) collective-permute-start(bf16[8,64,384]{2,1,0:T(8,128)(2,1)S(1)} %all-to-all-done.own_ref), channel_id=1, source_target_pairs={{0,1},{1,2},{2,0},{3,4},{4,5},{5,3},{6,7},{7,8},{8,6},{9,10},{10,1... | collective-permute-start | bytes 1179656 | tf_op jit(solution)/shard_map/ppermute | solution.py:251
  40.1 3.1 %collective-permute-start.17 = (bf16[8,64,384]{2,1,0:T(8,128)(2,1)S(1)}, bf16[8,64,384]{2,1,0:T(8,128)(2,1)S(1)}, u32[]{:S(2)}, u32[]{:S(2)}) collective-permute-start(bf16[8,64,384]{2,1,0:T(8,128)(2,1)S(1)} %all-to-all-done.own_ref), channel_id=1, source_target_pairs={{0,2},{1,0},{2,1},{3,5},{4,3},{5,4},{6,8},{7,6},{8,7},{9,11},{10,9... | collective-permute-start | bytes 1179656 | tf_op jit(solution)/shard_map/ppermute | solution.py:251
  43.2 2.5 %all-to-all-done.2.own_ref = bf16[8,32,384]{2,1,0:T(8,128)(2,1)S(1)} async-done(((bf16[8,32,384]{2,1,0:T(8,128)(2,1)}), bf16[8,32,384]{2,1,0:T(8,128)(2,1)S(1)}, u32[]{:S(2)}, u32[]{:S(2)}) %all-to-all-start.2) | async-done | bytes 196640 | tf_op jit(solution)/shard_map/all_to_all | solution.py:266
  45.7 3.1 %collective-permute-start.19 = (bf16[8,32,384]{2,1,0:T(8,128)(2,1)S(1)}, bf16[8,32,384]{2,1,0:T(8,128)(2,1)S(1)}, u32[]{:S(2)}, u32[]{:S(2)}) collective-permute-start(bf16[8,32,384]{2,1,0:T(8,128)(2,1)S(1)} %all-to-all-done.2.own_ref), channel_id=1, source_target_pairs={{0,1},{1,2},{2,0},{3,4},{4,5},{5,3},{6,7},{7,8},{8,6},{9,10},{10,1... | collective-permute-start | bytes 589832 | tf_op jit(solution)/shard_map/ppermute | solution.py:251
  48.8 3.1 %collective-permute-start.20 = (bf16[8,32,384]{2,1,0:T(8,128)(2,1)S(1)}, bf16[8,32,384]{2,1,0:T(8,128)(2,1)S(1)}, u32[]{:S(2)}, u32[]{:S(2)}) collective-permute-start(bf16[8,32,384]{2,1,0:T(8,128)(2,1)S(1)} %all-to-all-done.2.own_ref), channel_id=1, source_target_pairs={{0,2},{1,0},{2,1},{3,5},{4,3},{5,4},{6,8},{7,6},{8,7},{9,11},{10,9... | collective-permute-start | bytes 589832 | tf_op jit(solution)/shard_map/ppermute | solution.py:251
  51.9 9.2 %collective-permute-done.17.high_ref = bf16[8,64,384]{2,1,0:T(8,128)(2,1)S(1)} collective-permute-done((bf16[8,64,384]{2,1,0:T(8,128)(2,1)S(1)}, bf16[8,64,384]{2,1,0:T(8,128)(2,1)S(1)}, u32[]{:S(2)}, u32[]{:S(2)}) %collective-permute-start.17) | collective-permute-done | bytes 393248 | tf_op jit(solution)/shard_map/ppermute | solution.py:251
  61.2 1.3 copy-done.1
  62.4 1.3 copy-done.2
  63.7 1.3 copy-done.3
  65.0 3.4 %shard_map.121 = (bf16[24,32,384]{2,1,0:T(8,128)(2,1)}, bf16[64,128]{1,0:T(8,128)(2,1)S(1)}) custom-call(s32[1,2,8]{2,1,0:T(2,128)S(1)} %copy-done.5, bf16[8,64,384]{2,1,0:T(8,128)(2,1)S(1)} %all-to-all-done.own_ref, bf16[8,64,384]{2,1,0:T(8,128)(2,1)S(1)} %collective-permute-done.16.low_ref, bf16[8,64,384]{2,1,0:T(8,128)(2,1)S(1)} %collective-permute-done.17.high_ref, ...), custom_call_target="tpu_custom_call" | custom-call | tf_op jit(solution)/shard_map/pallas_call | solution.py:184
  68.4 4.4 %shard_map.122 = (bf16[8,32,384]{2,1,0:T(8,128)(2,1)S(1)}, bf16[8,32,384]{2,1,0:T(8,128)(2,1)S(1)}, bf16[8,32,384]{2,1,0:T(8,128)(2,1)S(1)}) custom-call(s32[1,2,8]{2,1,0:T(2,128)S(1)} %copy-done.5, bf16[8,32,384]{2,1,0:T(8,128)(2,1)S(1)} %all-to-all-done.2.own_ref, bf16[8,32,384]{2,1,0:T(8,128)(2,1)S(1)} %collective-permute-done.19.low_ref, ...), custom_call_target="tpu_custom_call" | custom-call | tf_op jit(solution)/shard_map/pallas_call | solution.py:184
  72.9 1.9 %collective-permute-start.22 = (bf16[8,32,384]{2,1,0:T(8,128)(2,1)S(1)}, bf16[8,32,384]{2,1,0:T(8,128)(2,1)S(1)}, u32[]{:S(2)}, u32[]{:S(2)}) collective-permute-start(bf16[8,32,384]{2,1,0:T(8,128)(2,1)S(1)} %get-tuple-element.45), channel_id=1, source_target_pairs={{0,2},{1,0},{2,1},{3,5},{4,3},{5,4},{6,8},{7,6},{8,7},{9,11},{10,9... | collective-permute-start | bytes 589832 | tf_op jit(solution)/shard_map/ppermute | solution.py:251
  74.8 3.4 %collective-permute-start.21 = (bf16[8,32,384]{2,1,0:T(8,128)(2,1)S(1)}, bf16[8,32,384]{2,1,0:T(8,128)(2,1)S(1)}, u32[]{:S(2)}, u32[]{:S(2)}) collective-permute-start(bf16[8,32,384]{2,1,0:T(8,128)(2,1)S(1)} %get-tuple-element.44), channel_id=1, source_target_pairs={{0,1},{1,2},{2,0},{3,4},{4,5},{5,3},{6,7},{7,8},{8,6},{9,10},{10,1... | collective-permute-start | bytes 589832 | tf_op jit(solution)/shard_map/ppermute | solution.py:251
  78.2 2.1 %collective-permute-done.22 = bf16[8,32,384]{2,1,0:T(8,128)(2,1)S(1)} collective-permute-done((bf16[8,32,384]{2,1,0:T(8,128)(2,1)S(1)}, bf16[8,32,384]{2,1,0:T(8,128)(2,1)S(1)}, u32[]{:S(2)}, u32[]{:S(2)}) %collective-permute-start.22) | collective-permute-done | bytes 196640 | tf_op jit(solution)/shard_map/ppermute | solution.py:251
  80.2 3.3 %collective-permute-done.21 = bf16[8,32,384]{2,1,0:T(8,128)(2,1)S(1)} collective-permute-done((bf16[8,32,384]{2,1,0:T(8,128)(2,1)S(1)}, bf16[8,32,384]{2,1,0:T(8,128)(2,1)S(1)}, u32[]{:S(2)}, u32[]{:S(2)}) %collective-permute-start.21) | collective-permute-done | bytes 196640 | tf_op jit(solution)/shard_map/ppermute | solution.py:251
  83.6 15.5 %all_to_all.20 = bf16[8,32,384]{2,1,0:T(8,128)(2,1)S(1)} all-to-all(bf16[8,32,384]{2,1,0:T(8,128)(2,1)S(1)} %add_convert_fusion), channel_id=1, replica_groups=mesh['x'=4,'far'=4,'core'=2,'line'=8,'run'=3] {'line'}, dimensions={0} | all-to-all | bytes 393216 | tf_op jit(solution)/shard_map/all_to_all | solution.py:266
  99.1 3.9 %all-to-all-start.1 = ((bf16[24,32,384]{2,1,0:T(8,128)(2,1)}), bf16[24,32,384]{2,1,0:T(8,128)(2,1)S(1)}, u32[]{:S(2)}, u32[]{:S(2)}) async-start(bf16[24,32,384]{2,1,0:T(8,128)(2,1)} %get-tuple-element.41), calls=%async_computation.1 | async-start | bytes 1179648 | tf_op jit(solution)/shard_map/all_to_all | solution.py:266
  103.0 0.9 fusion
  104.1 6.6 %collective-permute-start.23 = (bf16[64,192]{1,0:T(8,128)(2,1)S(1)}, bf16[64,192]{1,0:T(8,128)(2,1)S(1)}, u32[]{:S(2)}, u32[]{:S(2)}) collective-permute-start(bf16[64,192]{1,0:T(8,128)(2,1)S(1)} %pad_maximum_fusion.2), channel_id=1, source_target_pairs={{24,0},{48,24},{72,48},{96,72},{120,96},{144,120},{168,144},{192,1... | collective-permute-start | bytes 73736 | tf_op jit(solution)/shard_map/ppermute | solution.py:246
  110.8 5.3 %all-to-all-done.1 = bf16[24,32,384]{2,1,0:T(8,128)(2,1)S(1)} async-done(((bf16[24,32,384]{2,1,0:T(8,128)(2,1)}), bf16[24,32,384]{2,1,0:T(8,128)(2,1)S(1)}, u32[]{:S(2)}, u32[]{:S(2)}) %all-to-all-start.1) | async-done | bytes 589856 | tf_op jit(solution)/shard_map/all_to_all | solution.py:266
  116.3 14.7 %collective-permute-start.18 = (bf16[64,192]{1,0:T(8,128)(2,1)S(1)}, bf16[64,192]{1,0:T(8,128)(2,1)S(1)}, u32[]{:S(2)}, u32[]{:S(2)}) collective-permute-start(bf16[64,192]{1,0:T(8,128)(2,1)S(1)} %pad_maximum_fusion.1), channel_id=1, source_target_pairs={{0,24},{24,48},{48,72},{72,96},{96,120},{120,144},{144,168},{168,1... | collective-permute-start | bytes 73736 | tf_op jit(solution)/shard_map/ppermute | solution.py:246
  130.9 0.6 maximum_bitcast_fusion
  131.9 0.6 copy.31
  (37 shorter events, 1.7 us)
Async XLA Ops:
  0.6 9.5 %copy-start.6 = (bf16[1,64,192]{2,1,0:T(8,128)(2,1)S(1)}, bf16[1,64,192]{2,1,0:T(8,128)(2,1)}, u32[]{:S(2)}) copy-start(bf16[1,64,192]{2,1,0:T(8,128)(2,1)} %param.26) | copy-start | bytes 73732
  0.6 9.4 %copy-start.9 = (s32[32]{0:T(128)S(1)}, s32[32]{0:T(128)}, u32[]{:S(2)}) copy-start(s32[32]{0:T(128)} %param.35) | copy-start | bytes 388
  0.7 9.5 %copy-start.8 = (bf16[1,64,192]{2,1,0:T(8,128)(2,1)S(1)}, bf16[1,64,192]{2,1,0:T(8,128)(2,1)}, u32[]{:S(2)}) copy-start(bf16[1,64,192]{2,1,0:T(8,128)(2,1)} %param.28) | copy-start | bytes 73732
  0.7 60.5 %copy-start.5 = (s32[1,2,8]{2,1,0:T(2,128)S(1)}, s32[1,2,8]{2,1,0:T(2,128)}, u32[]{:S(2)}) copy-start(s32[1,2,8]{2,1,0:T(2,128)} %off_ref.3) | copy-start | bytes 196
  0.7 60.5 %copy-start.4 = (f32[1,4608]{1,0:T(1,128)S(1)}, f32[1,4608]{1,0:T(1,128)}, u32[]{:S(2)}) copy-start(f32[1,4608]{1,0:T(1,128)} %gain_ref.3) | copy-start | bytes 55300
  0.7 60.5 %copy-start = (bf16[1,4608,128]{2,1,0:T(8,128)(2,1)S(1)}, bf16[1,4608,128]{2,1,0:T(8,128)(2,1)}, u32[]{:S(2)}) copy-start(bf16[1,4608,128]{2,1,0:T(8,128)(2,1)} %param.30) | copy-start | bytes 3538948
  2.4 27.2 %all-to-all-start = ((bf16[8,64,384]{2,1,0:T(8,128)(2,1)}), bf16[8,64,384]{2,1,0:T(8,128)(2,1)S(1)}, u32[]{:S(2)}, u32[]{:S(2)}) async-start(bf16[8,64,384]{2,1,0:T(8,128)(2,1)} %broadcast_in_dim.10), calls=%async_computation | async-start | bytes 786432 | tf_op jit(solution)/shard_map/all_to_all | solution.py:266
  10.2 18.7 %collective-permute-start.12 = (bf16[64,384]{1,0:T(8,128)(2,1)S(1)}, bf16[64,384]{1,0:T(8,128)(2,1)}, u32[]{:S(2)}, u32[]{:S(2)}) collective-permute-start(bf16[64,384]{1,0:T(8,128)(2,1)S(1)} %param.12), channel_id=1, source_target_pairs={{0,672},{24,696},{48,720},{72,744},{96,576},{120,600},{144,624},{1... | collective-permute-start | bytes 147464 | tf_op jit(solution)/shard_map/cond/branch_12_fun/ppermute | solution.py:260
  30.4 15.4 %all-to-all-start.2 = ((bf16[8,32,384]{2,1,0:T(8,128)(2,1)}), bf16[8,32,384]{2,1,0:T(8,128)(2,1)S(1)}, u32[]{:S(2)}, u32[]{:S(2)}) async-start(bf16[8,32,384]{2,1,0:T(8,128)(2,1)} %broadcast_in_dim.23), calls=%async_computation.2 | async-start | bytes 393216 | tf_op jit(solution)/shard_map/all_to_all | solution.py:266
  37.0 14.9 %collective-permute-start.16 = (bf16[8,64,384]{2,1,0:T(8,128)(2,1)S(1)}, bf16[8,64,384]{2,1,0:T(8,128)(2,1)S(1)}, u32[]{:S(2)}, u32[]{:S(2)}) collective-permute-start(bf16[8,64,384]{2,1,0:T(8,128)(2,1)S(1)} %all-to-all-done.own_ref), channel_id=1, source_target_pairs={{0,1},{1,2},{2,0},{3,4},{4,5},{5,3},{6,7},{7,8},{8,6},{9,10},{10,1... | collective-permute-start | bytes 1179656 | tf_op jit(solution)/shard_map/ppermute | solution.py:251
  40.1 21.1 %collective-permute-start.17 = (bf16[8,64,384]{2,1,0:T(8,128)(2,1)S(1)}, bf16[8,64,384]{2,1,0:T(8,128)(2,1)S(1)}, u32[]{:S(2)}, u32[]{:S(2)}) collective-permute-start(bf16[8,64,384]{2,1,0:T(8,128)(2,1)S(1)} %all-to-all-done.own_ref), channel_id=1, source_target_pairs={{0,2},{1,0},{2,1},{3,5},{4,3},{5,4},{6,8},{7,6},{8,7},{9,11},{10,9... | collective-permute-start | bytes 1179656 | tf_op jit(solution)/shard_map/ppermute | solution.py:251
  45.7 22.7 %collective-permute-start.19 = (bf16[8,32,384]{2,1,0:T(8,128)(2,1)S(1)}, bf16[8,32,384]{2,1,0:T(8,128)(2,1)S(1)}, u32[]{:S(2)}, u32[]{:S(2)}) collective-permute-start(bf16[8,32,384]{2,1,0:T(8,128)(2,1)S(1)} %all-to-all-done.2.own_ref), channel_id=1, source_target_pairs={{0,1},{1,2},{2,0},{3,4},{4,5},{5,3},{6,7},{7,8},{8,6},{9,10},{10,1... | collective-permute-start | bytes 589832 | tf_op jit(solution)/shard_map/ppermute | solution.py:251
  48.8 19.6 %collective-permute-start.20 = (bf16[8,32,384]{2,1,0:T(8,128)(2,1)S(1)}, bf16[8,32,384]{2,1,0:T(8,128)(2,1)S(1)}, u32[]{:S(2)}, u32[]{:S(2)}) collective-permute-start(bf16[8,32,384]{2,1,0:T(8,128)(2,1)S(1)} %all-to-all-done.2.own_ref), channel_id=1, source_target_pairs={{0,2},{1,0},{2,1},{3,5},{4,3},{5,4},{6,8},{7,6},{8,7},{9,11},{10,9... | collective-permute-start | bytes 589832 | tf_op jit(solution)/shard_map/ppermute | solution.py:251
  61.2 1.3 copy-start.1
  62.4 1.3 copy-start.2
  63.7 1.3 copy-start.3
  72.9 7.4 %collective-permute-start.22 = (bf16[8,32,384]{2,1,0:T(8,128)(2,1)S(1)}, bf16[8,32,384]{2,1,0:T(8,128)(2,1)S(1)}, u32[]{:S(2)}, u32[]{:S(2)}) collective-permute-start(bf16[8,32,384]{2,1,0:T(8,128)(2,1)S(1)} %get-tuple-element.45), channel_id=1, source_target_pairs={{0,2},{1,0},{2,1},{3,5},{4,3},{5,4},{6,8},{7,6},{8,7},{9,11},{10,9... | collective-permute-start | bytes 589832 | tf_op jit(solution)/shard_map/ppermute | solution.py:251
  74.8 8.8 %collective-permute-start.21 = (bf16[8,32,384]{2,1,0:T(8,128)(2,1)S(1)}, bf16[8,32,384]{2,1,0:T(8,128)(2,1)S(1)}, u32[]{:S(2)}, u32[]{:S(2)}) collective-permute-start(bf16[8,32,384]{2,1,0:T(8,128)(2,1)S(1)} %get-tuple-element.44), channel_id=1, source_target_pairs={{0,1},{1,2},{2,0},{3,4},{4,5},{5,3},{6,7},{7,8},{8,6},{9,10},{10,1... | collective-permute-start | bytes 589832 | tf_op jit(solution)/shard_map/ppermute | solution.py:251
  83.6 19.4 %copy-start.7 = (bf16[1,64,192]{2,1,0:T(8,128)(2,1)S(1)}, bf16[1,64,192]{2,1,0:T(8,128)(2,1)}, u32[]{:S(2)}) copy-start(bf16[1,64,192]{2,1,0:T(8,128)(2,1)} %param.27) | copy-start | bytes 73732
  99.1 16.9 %all-to-all-start.1 = ((bf16[24,32,384]{2,1,0:T(8,128)(2,1)}), bf16[24,32,384]{2,1,0:T(8,128)(2,1)S(1)}, u32[]{:S(2)}, u32[]{:S(2)}) async-start(bf16[24,32,384]{2,1,0:T(8,128)(2,1)} %get-tuple-element.41), calls=%async_computation.1 | async-start | bytes 1179648 | tf_op jit(solution)/shard_map/all_to_all | solution.py:266
  104.1 27.5 %collective-permute-start.23 = (bf16[64,192]{1,0:T(8,128)(2,1)S(1)}, bf16[64,192]{1,0:T(8,128)(2,1)S(1)}, u32[]{:S(2)}, u32[]{:S(2)}) collective-permute-start(bf16[64,192]{1,0:T(8,128)(2,1)S(1)} %pad_maximum_fusion.2), channel_id=1, source_target_pairs={{24,0},{48,24},{72,48},{96,72},{120,96},{144,120},{168,144},{192,1... | collective-permute-start | bytes 73736 | tf_op jit(solution)/shard_map/ppermute | solution.py:246
  116.3 15.7 %collective-permute-start.18 = (bf16[64,192]{1,0:T(8,128)(2,1)S(1)}, bf16[64,192]{1,0:T(8,128)(2,1)S(1)}, u32[]{:S(2)}, u32[]{:S(2)}) collective-permute-start(bf16[64,192]{1,0:T(8,128)(2,1)S(1)} %pad_maximum_fusion.1), channel_id=1, source_target_pairs={{0,24},{24,48},{48,72},{72,96},{96,120},{120,144},{144,168},{168,1... | collective-permute-start | bytes 73736 | tf_op jit(solution)/shard_map/ppermute | solution.py:246

commit v4 on v3

--- a/solution.py
+++ b/solution.py
@@ -59,9 +59,49 @@
     all_ref[lax.rem(at + 1, count)] = high_ref[...]
 
 
+def fetches(sources, targets, sems):
+    copies = []
+    for n, (source, target) in enumerate(zip(sources, targets)):
+        step = source.shape[0] // PIECES
+        pieces = [
+            pltpu.make_async_copy(source.at[pl.ds(i * step, step)], target.at[pl.ds(i * step, step)], sems.at[n, i])
+            for i in range(PIECES)
+        ]
+        for piece in pieces:
+            piece.start()
+        copies.append(pieces)
+    return copies
+
+
+def arrive(pieces):
+    for piece in pieces:
+        piece.wait()
+
+
 def forward_kernel(
-    off_ref, own_ref, low_ref, high_ref, gain_ref, wq_ref, wk_ref, wv_ref, wo_ref, term_ref, dctx_ref, blocks, xs, gs
+    off_ref,
+    own_ref,
+    low_ref,
+    high_ref,
+    gain_ref,
+    wq_hbm,
+    wk_hbm,
+    wv_hbm,
+    wo_hbm,
+    term_ref,
+    dctx_ref,
+    blocks,
+    xs,
+    gs,
+    wq_ref,
+    wk_ref,
+    wv_ref,
+    wo_ref,
+    sems,
 ):
+    wq_in, wk_in, wv_in, wo_in = fetches(
+        (wq_hbm, wk_hbm, wv_hbm, wo_hbm), (wq_ref, wk_ref, wv_ref, wo_ref), sems
+    )
     gathered(own_ref, low_ref, high_ref, blocks)
     runs, lines, rows, wide = blocks.shape
     parts = runs * lines
@@ -83,13 +123,17 @@
         span = slice(wide * u, wide * (u + 1))
         xs[:, span] = (xs[:, span].astype(F32) * inverse * gain_ref[:, span]).astype(BF16)
     normed = xs[...]
+    arrive(wq_in)
     queries = dot(normed, wq_ref[...]).astype(BF16)
+    arrive(wk_in)
     keys = dot(normed, wk_ref[...]).astype(BF16)
+    arrive(wv_in)
     values = dot(normed, wv_ref[...]).astype(BF16)
     mask = causal(off_ref, 0, rows)
     context = jnp.concatenate(
         [dot(softmax(q, k, mask).astype(BF16), v) for q, k, v in heads_of(queries, keys, values)], axis=1
     ).astype(BF16)
+    arrive(wo_in)
     for u in range(parts // 2):
         span = slice(wide * u, wide * (u + 1))
         out = dot(context, wo_ref[:, span]).astype(BF16)
@@ -105,9 +149,9 @@
     high_ref,
     dctx_ref,
     gain_ref,
-    wq_ref,
-    wk_ref,
-    wv_ref,
+    wq_hbm,
+    wk_hbm,
+    wv_hbm,
     stay_ref,
     up_ref,
     down_ref,
@@ -116,7 +160,12 @@
     xs,
     ns,
     ds,
+    wq_ref,
+    wk_ref,
+    wv_ref,
+    sems,
 ):
+    wq_in, wk_in, wv_in = fetches((wq_hbm, wk_hbm, wv_hbm), (wq_ref, wk_ref, wv_ref), sems)
     gathered(own_ref, low_ref, high_ref, blocks)
     runs, lines, half, wide = blocks.shape
     parts = runs * lines
@@ -143,8 +192,11 @@
         span = slice(wide * u, wide * (u + 1))
         ns[:, span] = (xs[:, span].astype(F32) * inverse * gain_ref[:, span]).astype(BF16)
     normed = ns[...]
+    arrive(wq_in)
     queries = dot(normed, wq_ref[...]).astype(BF16)
+    arrive(wk_in)
     keys = dot(normed, wk_ref[...]).astype(BF16)
+    arrive(wv_in)
     values = dot(normed, wv_ref[...]).astype(BF16)
     mask = causal(off_ref, 1, rows)
     grads = []
@@ -178,9 +230,12 @@
     down_ref[...] = terms[lax.rem(at + runs - 1, runs)]
 
 
-def kernel_call(body, outs, scratch, args):
+def kernel_call(body, outs, scratch, offsets, args, weights):
     vmem = pl.BlockSpec(memory_space=pltpu.VMEM)
-    specs = [pl.BlockSpec(memory_space=pltpu.SMEM)] + [vmem] * (len(args) - 1)
+    specs = [pl.BlockSpec(memory_space=pltpu.SMEM)] + [vmem] * len(args)
+    specs += [pl.BlockSpec(memory_space=pltpu.HBM)] * len(weights)
+    scratch = scratch + [pltpu.VMEM(w.shape, w.dtype) for w in weights]
+    scratch.append(pltpu.SemaphoreType.DMA((len(weights), PIECES)))
     return pl.pallas_call(
         body,
         out_shape=outs,
@@ -188,9 +243,10 @@
         out_specs=jax.tree.map(lambda _: vmem, outs),
         scratch_shapes=scratch,
         compiler_params=pltpu.CompilerParams(vmem_limit_bytes=VMEM_LIMIT),
-    )(*args)
-
-
+    )(offsets, *args, *[pltpu.with_memory_space_constraint(w, pltpu.HBM) for w in weights])
+
+
+PIECES = 2
 VMEM_LIMIT = 16 * 2**20
 
 
@@ -207,7 +263,7 @@
         pltpu.VMEM((rows, width), BF16),
         pltpu.VMEM((rows, width), BF16),
     ]
-    return kernel_call(forward_kernel, outs, scratch, (offsets, *blocks, gain, wq, wk, wv, wo))
+    return kernel_call(forward_kernel, outs, scratch, offsets, (*blocks, gain), (wq, wk, wv, wo))
 
 
 def backward_term(offsets, blocks, dctx, gain, wq, wk, wv):
@@ -222,7 +278,7 @@
         pltpu.VMEM((2 * half, width), BF16),
         pltpu.VMEM((2 * half, width), F32),
     ]
-    return kernel_call(backward_kernel, outs, scratch, (offsets, *blocks, dctx, gain, wq, wk, wv))
+    return kernel_call(backward_kernel, outs, scratch, offsets, (*blocks, dctx, gain), (wq, wk, wv))
 
 
 def folded(block):

time: 134 us -> 135 us (level)
  local copies, waits for them, and re-layouts: 8.31 us -> 4.52 us
  Pallas kernels: 7.89 us -> 10.5 us
  waiting for transfers between devices: 24.4 us -> 26.1 us
    unnamed x22 -> x14, local copies, waits for them, and re-layouts: 5.06 us -> 1.25 us
    pallas_call x2, Pallas kernels: 7.89 us -> 10.5 us  [kernel_call(): pl.pallas_call(body, out_shape=outs, in_specs=specs, out_specs=jax.tree.m...]
  transfers between devices with their start and end apart: 12 -> 12, of which waited for: 7 -> 8; matrix products, arithmetic and copies ran while one was open for 2% -> 2% of each run, Pallas kernels for 3% -> 3%
where the time goes in v4:
time: 135 us; the launch traced here: 134 us
  starting transfers between devices  74.6 us (55%)
  waiting for transfers between devices  26.1 us (19%)
  blocking collectives  15 us (11%)
  Pallas kernels  10.5 us (8%)
  local copies, waits for them, and re-layouts  4.52 us (3%)
  other arithmetic  1.97 us (1%)
    ppermute x2, starting transfers between devices, passed_along(): return lax.ppermute(block, SECTION, route)  21.2 us
    all_to_all x3, starting transfers between devices, exchanged(): return lax.all_to_all(blocks, axes, 0, 0, tiled=True)  18.7 us
    ppermute x6, starting transfers between devices, around(): lax.ppermute(block, axis, [(i, (i + distance) % count) for i in range(cou...  17.6 us
    ppermute x1, starting transfers between devices, swap_by(): return lambda held: lax.ppermute(held, SECTION, route)  17.1 us
    ppermute x6, waiting for transfers between devices, around(): lax.ppermute(block, axis, [(i, (i + distance) % count) for i in range(cou...  15.5 us
    all_to_all x1, blocking collectives, exchanged(): return lax.all_to_all(blocks, axes, 0, 0, tiled=True)  15 us
    pallas_call x2, Pallas kernels, kernel_call(): pl.pallas_call(body, out_shape=outs, in_specs=specs, out_specs=jax.tree.m...  10.5 us
    all_to_all x3, waiting for transfers between devices, exchanged(): return lax.all_to_all(blocks, axes, 0, 0, tiled=True)  8.56 us
  transfers between devices with their start and end apart: 12, of which 8 were waited for; matrix products, arithmetic and copies ran while one was open for 2% of the time, Pallas kernels for 3%

profile of v4, /device:TPU:1, one launch (start us, length us, event | category | flops | bytes accessed | tf_op | source)
XLA Modules:
  0.0 133.7 jit_solution(15729361278816217804)
XLA Ops:
  0.7 0.9 pad_maximum_fusion
  1.6 0.8 broadcast_in_dim.10
  2.4 7.6 %all-to-all-start = ((bf16[8,64,384]{2,1,0:T(8,128)(2,1)}), bf16[8,64,384]{2,1,0:T(8,128)(2,1)S(1)}, u32[]{:S(2)}, u32[]{:S(2)}) async-start(bf16[8,64,384]{2,1,0:T(8,128)(2,1)} %broadcast_in_dim.10), calls=%async_computation | async-start | bytes 786432 | tf_op jit(solution)/shard_map/all_to_all | solution.py:322
  10.2 18.7 %conditional.1 = (bf16[64,384]{1,0:T(8,128)(2,1)}) conditional(s32[]{:T(128)} %bitcast.11, bf16[64,384]{1,0:T(8,128)(2,1)S(1)} %maximum_maximum_fusion, bf16[64,384]{1,0:T(8,128)(2,1)S(1)} %maximum_maximum_fusion, bf16[64,384]{1,0:T(8,128)(2,1)S(1)} %maximum_maximum_fusion, ...), branch_computations={%region_1.0_spmd, %region_2.0_spmd, %region_3.0_spmd, %region_4.0_... | conditional | bytes 196656 | solution.py:318
  10.2 17.1 %collective-permute-start.12 = (bf16[64,384]{1,0:T(8,128)(2,1)S(1)}, bf16[64,384]{1,0:T(8,128)(2,1)}, u32[]{:S(2)}, u32[]{:S(2)}) collective-permute-start(bf16[64,384]{1,0:T(8,128)(2,1)S(1)} %param.12), channel_id=1, source_target_pairs={{0,672},{24,696},{48,720},{72,744},{96,576},{120,600},{144,624},{1... | collective-permute-start | bytes 147464 | tf_op jit(solution)/shard_map/cond/branch_12_fun/ppermute | solution.py:316
  27.2 1.6 %collective-permute-done.12 = bf16[64,384]{1,0:T(8,128)(2,1)} collective-permute-done((bf16[64,384]{1,0:T(8,128)(2,1)S(1)}, bf16[64,384]{1,0:T(8,128)(2,1)}, u32[]{:S(2)}, u32[]{:S(2)}) %collective-permute-start.12) | collective-permute-done | bytes 49184 | tf_op jit(solution)/shard_map/cond/branch_12_fun/ppermute | solution.py:316
  28.9 0.7 slice.87
  29.6 0.7 broadcast_in_dim.23
  30.3 6.6 %all-to-all-start.2 = ((bf16[8,32,384]{2,1,0:T(8,128)(2,1)}), bf16[8,32,384]{2,1,0:T(8,128)(2,1)S(1)}, u32[]{:S(2)}, u32[]{:S(2)}) async-start(bf16[8,32,384]{2,1,0:T(8,128)(2,1)} %broadcast_in_dim.23), calls=%async_computation.2 | async-start | bytes 393216 | tf_op jit(solution)/shard_map/all_to_all | solution.py:322
  36.9 3.0 %collective-permute-start.16 = (bf16[8,64,384]{2,1,0:T(8,128)(2,1)S(1)}, bf16[8,64,384]{2,1,0:T(8,128)(2,1)S(1)}, u32[]{:S(2)}, u32[]{:S(2)}) collective-permute-start(bf16[8,64,384]{2,1,0:T(8,128)(2,1)S(1)} %all-to-all-done.own_ref), channel_id=1, source_target_pairs={{0,1},{1,2},{2,0},{3,4},{4,5},{5,3},{6,7},{7,8},{8,6},{9,10},{10,1... | collective-permute-start | bytes 1179656 | tf_op jit(solution)/shard_map/ppermute | solution.py:307
  40.0 3.1 %collective-permute-start.17 = (bf16[8,64,384]{2,1,0:T(8,128)(2,1)S(1)}, bf16[8,64,384]{2,1,0:T(8,128)(2,1)S(1)}, u32[]{:S(2)}, u32[]{:S(2)}) collective-permute-start(bf16[8,64,384]{2,1,0:T(8,128)(2,1)S(1)} %all-to-all-done.own_ref), channel_id=1, source_target_pairs={{0,2},{1,0},{2,1},{3,5},{4,3},{5,4},{6,8},{7,6},{8,7},{9,11},{10,9... | collective-permute-start | bytes 1179656 | tf_op jit(solution)/shard_map/ppermute | solution.py:307
  43.1 2.5 %all-to-all-done.2.own_ref = bf16[8,32,384]{2,1,0:T(8,128)(2,1)S(1)} async-done(((bf16[8,32,384]{2,1,0:T(8,128)(2,1)}), bf16[8,32,384]{2,1,0:T(8,128)(2,1)S(1)}, u32[]{:S(2)}, u32[]{:S(2)}) %all-to-all-start.2) | async-done | bytes 196640 | tf_op jit(solution)/shard_map/all_to_all | solution.py:322
  45.7 3.1 %collective-permute-start.19 = (bf16[8,32,384]{2,1,0:T(8,128)(2,1)S(1)}, bf16[8,32,384]{2,1,0:T(8,128)(2,1)S(1)}, u32[]{:S(2)}, u32[]{:S(2)}) collective-permute-start(bf16[8,32,384]{2,1,0:T(8,128)(2,1)S(1)} %all-to-all-done.2.own_ref), channel_id=1, source_target_pairs={{0,1},{1,2},{2,0},{3,4},{4,5},{5,3},{6,7},{7,8},{8,6},{9,10},{10,1... | collective-permute-start | bytes 589832 | tf_op jit(solution)/shard_map/ppermute | solution.py:307
  48.7 3.1 %collective-permute-start.20 = (bf16[8,32,384]{2,1,0:T(8,128)(2,1)S(1)}, bf16[8,32,384]{2,1,0:T(8,128)(2,1)S(1)}, u32[]{:S(2)}, u32[]{:S(2)}) collective-permute-start(bf16[8,32,384]{2,1,0:T(8,128)(2,1)S(1)} %all-to-all-done.2.own_ref), channel_id=1, source_target_pairs={{0,2},{1,0},{2,1},{3,5},{4,3},{5,4},{6,8},{7,6},{8,7},{9,11},{10,9... | collective-permute-start | bytes 589832 | tf_op jit(solution)/shard_map/ppermute | solution.py:307
  51.9 9.2 %collective-permute-done.17.high_ref = bf16[8,64,384]{2,1,0:T(8,128)(2,1)S(1)} collective-permute-done((bf16[8,64,384]{2,1,0:T(8,128)(2,1)S(1)}, bf16[8,64,384]{2,1,0:T(8,128)(2,1)S(1)}, u32[]{:S(2)}, u32[]{:S(2)}) %collective-permute-start.17) | collective-permute-done | bytes 393248 | tf_op jit(solution)/shard_map/ppermute | solution.py:307
  61.1 4.7 %shard_map.121 = (bf16[24,32,384]{2,1,0:T(8,128)(2,1)}, bf16[64,128]{1,0:T(8,128)(2,1)S(1)}) custom-call(s32[1,2,8]{2,1,0:T(2,128)S(1)} %copy-done.1, bf16[8,64,384]{2,1,0:T(8,128)(2,1)S(1)} %all-to-all-done.own_ref, bf16[8,64,384]{2,1,0:T(8,128)(2,1)S(1)} %collective-permute-done.16.low_ref, bf16[8,64,384]{2,1,0:T(8,128)(2,1)S(1)} %collective-permute-done.17.high_ref, ...), custom_call_target="tpu_custom_call" | custom-call | tf_op jit(solution)/shard_map/pallas_call | solution.py:239
  65.8 1.6 %collective-permute-done.20.high_ref = bf16[8,32,384]{2,1,0:T(8,128)(2,1)S(1)} collective-permute-done((bf16[8,32,384]{2,1,0:T(8,128)(2,1)S(1)}, bf16[8,32,384]{2,1,0:T(8,128)(2,1)S(1)}, u32[]{:S(2)}, u32[]{:S(2)}) %collective-permute-start.20) | collective-permute-done | bytes 196640 | tf_op jit(solution)/shard_map/ppermute | solution.py:307
  67.4 5.8 %shard_map.122 = (bf16[8,32,384]{2,1,0:T(8,128)(2,1)S(1)}, bf16[8,32,384]{2,1,0:T(8,128)(2,1)S(1)}, bf16[8,32,384]{2,1,0:T(8,128)(2,1)S(1)}) custom-call(s32[1,2,8]{2,1,0:T(2,128)S(1)} %copy-done.1, bf16[8,32,384]{2,1,0:T(8,128)(2,1)S(1)} %all-to-all-done.2.own_ref, bf16[8,32,384]{2,1,0:T(8,128)(2,1)S(1)} %collective-permute-done.19.low_ref, ...), custom_call_target="tpu_custom_call" | custom-call | tf_op jit(solution)/shard_map/pallas_call | solution.py:239
  73.2 1.9 %collective-permute-start.22 = (bf16[8,32,384]{2,1,0:T(8,128)(2,1)S(1)}, bf16[8,32,384]{2,1,0:T(8,128)(2,1)S(1)}, u32[]{:S(2)}, u32[]{:S(2)}) collective-permute-start(bf16[8,32,384]{2,1,0:T(8,128)(2,1)S(1)} %get-tuple-element.45), channel_id=1, source_target_pairs={{0,2},{1,0},{2,1},{3,5},{4,3},{5,4},{6,8},{7,6},{8,7},{9,11},{10,9... | collective-permute-start | bytes 589832 | tf_op jit(solution)/shard_map/ppermute | solution.py:307
  75.2 3.4 %collective-permute-start.21 = (bf16[8,32,384]{2,1,0:T(8,128)(2,1)S(1)}, bf16[8,32,384]{2,1,0:T(8,128)(2,1)S(1)}, u32[]{:S(2)}, u32[]{:S(2)}) collective-permute-start(bf16[8,32,384]{2,1,0:T(8,128)(2,1)S(1)} %get-tuple-element.44), channel_id=1, source_target_pairs={{0,1},{1,2},{2,0},{3,4},{4,5},{5,3},{6,7},{7,8},{8,6},{9,10},{10,1... | collective-permute-start | bytes 589832 | tf_op jit(solution)/shard_map/ppermute | solution.py:307
  78.5 2.6 %collective-permute-done.22 = bf16[8,32,384]{2,1,0:T(8,128)(2,1)S(1)} collective-permute-done((bf16[8,32,384]{2,1,0:T(8,128)(2,1)S(1)}, bf16[8,32,384]{2,1,0:T(8,128)(2,1)S(1)}, u32[]{:S(2)}, u32[]{:S(2)}) %collective-permute-start.22) | collective-permute-done | bytes 196640 | tf_op jit(solution)/shard_map/ppermute | solution.py:307
  81.1 2.1 %collective-permute-done.21 = bf16[8,32,384]{2,1,0:T(8,128)(2,1)S(1)} collective-permute-done((bf16[8,32,384]{2,1,0:T(8,128)(2,1)S(1)}, bf16[8,32,384]{2,1,0:T(8,128)(2,1)S(1)}, u32[]{:S(2)}, u32[]{:S(2)}) %collective-permute-start.21) | collective-permute-done | bytes 196640 | tf_op jit(solution)/shard_map/ppermute | solution.py:307
  83.3 15.0 %all_to_all.20 = bf16[8,32,384]{2,1,0:T(8,128)(2,1)S(1)} all-to-all(bf16[8,32,384]{2,1,0:T(8,128)(2,1)S(1)} %add_convert_fusion), channel_id=1, replica_groups=mesh['x'=4,'far'=4,'core'=2,'line'=8,'run'=3] {'line'}, dimensions={0} | all-to-all | bytes 393216 | tf_op jit(solution)/shard_map/all_to_all | solution.py:322
  98.4 4.4 %all-to-all-start.1 = ((bf16[24,32,384]{2,1,0:T(8,128)(2,1)}), bf16[24,32,384]{2,1,0:T(8,128)(2,1)S(1)}, u32[]{:S(2)}, u32[]{:S(2)}) async-start(bf16[24,32,384]{2,1,0:T(8,128)(2,1)} %get-tuple-element.41), calls=%async_computation.1 | async-start | bytes 1179648 | tf_op jit(solution)/shard_map/all_to_all | solution.py:322
  102.8 0.9 fusion
  103.9 6.0 %collective-permute-start.23 = (bf16[64,192]{1,0:T(8,128)(2,1)S(1)}, bf16[64,192]{1,0:T(8,128)(2,1)S(1)}, u32[]{:S(2)}, u32[]{:S(2)}) collective-permute-start(bf16[64,192]{1,0:T(8,128)(2,1)S(1)} %pad_maximum_fusion.2), channel_id=1, source_target_pairs={{24,0},{48,24},{72,48},{96,72},{120,96},{144,120},{168,144},{192,1... | collective-permute-start | bytes 73736 | tf_op jit(solution)/shard_map/ppermute | solution.py:302
  109.9 6.0 %all-to-all-done.1 = bf16[24,32,384]{2,1,0:T(8,128)(2,1)S(1)} async-done(((bf16[24,32,384]{2,1,0:T(8,128)(2,1)}), bf16[24,32,384]{2,1,0:T(8,128)(2,1)S(1)}, u32[]{:S(2)}, u32[]{:S(2)}) %all-to-all-start.1) | async-done | bytes 589856 | tf_op jit(solution)/shard_map/all_to_all | solution.py:322
  116.1 15.3 %collective-permute-start.18 = (bf16[64,192]{1,0:T(8,128)(2,1)S(1)}, bf16[64,192]{1,0:T(8,128)(2,1)S(1)}, u32[]{:S(2)}, u32[]{:S(2)}) collective-permute-start(bf16[64,192]{1,0:T(8,128)(2,1)S(1)} %pad_maximum_fusion.1), channel_id=1, source_target_pairs={{0,24},{24,48},{48,72},{72,96},{96,120},{120,144},{144,168},{168,1... | collective-permute-start | bytes 73736 | tf_op jit(solution)/shard_map/ppermute | solution.py:302
  131.4 0.6 maximum_bitcast_fusion
  132.1 0.4 collective-permute-done.18
  132.4 0.6 copy.31
  133.0 0.6 copy.32
  (29 shorter events, 0.7 us)
Async XLA Ops:
  0.6 9.4 %copy-start.2 = (bf16[1,64,192]{2,1,0:T(8,128)(2,1)S(1)}, bf16[1,64,192]{2,1,0:T(8,128)(2,1)}, u32[]{:S(2)}) copy-start(bf16[1,64,192]{2,1,0:T(8,128)(2,1)} %param.26) | copy-start | bytes 73732
  0.6 9.4 %copy-start.5 = (s32[32]{0:T(128)S(1)}, s32[32]{0:T(128)}, u32[]{:S(2)}) copy-start(s32[32]{0:T(128)} %param.35) | copy-start | bytes 388
  0.7 9.4 %copy-start.4 = (bf16[1,64,192]{2,1,0:T(8,128)(2,1)S(1)}, bf16[1,64,192]{2,1,0:T(8,128)(2,1)}, u32[]{:S(2)}) copy-start(bf16[1,64,192]{2,1,0:T(8,128)(2,1)} %param.28) | copy-start | bytes 73732
  0.7 60.4 %copy-start.1 = (s32[1,2,8]{2,1,0:T(2,128)S(1)}, s32[1,2,8]{2,1,0:T(2,128)}, u32[]{:S(2)}) copy-start(s32[1,2,8]{2,1,0:T(2,128)} %off_ref.3) | copy-start | bytes 196
  0.7 60.4 %copy-start = (f32[1,4608]{1,0:T(1,128)S(1)}, f32[1,4608]{1,0:T(1,128)}, u32[]{:S(2)}) copy-start(f32[1,4608]{1,0:T(1,128)} %gain_ref.3) | copy-start | bytes 55300
  2.4 27.2 %all-to-all-start = ((bf16[8,64,384]{2,1,0:T(8,128)(2,1)}), bf16[8,64,384]{2,1,0:T(8,128)(2,1)S(1)}, u32[]{:S(2)}, u32[]{:S(2)}) async-start(bf16[8,64,384]{2,1,0:T(8,128)(2,1)} %broadcast_in_dim.10), calls=%async_computation | async-start | bytes 786432 | tf_op jit(solution)/shard_map/all_to_all | solution.py:322
  10.2 18.7 %collective-permute-start.12 = (bf16[64,384]{1,0:T(8,128)(2,1)S(1)}, bf16[64,384]{1,0:T(8,128)(2,1)}, u32[]{:S(2)}, u32[]{:S(2)}) collective-permute-start(bf16[64,384]{1,0:T(8,128)(2,1)S(1)} %param.12), channel_id=1, source_target_pairs={{0,672},{24,696},{48,720},{72,744},{96,576},{120,600},{144,624},{1... | collective-permute-start | bytes 147464 | tf_op jit(solution)/shard_map/cond/branch_12_fun/ppermute | solution.py:316
  30.3 15.4 %all-to-all-start.2 = ((bf16[8,32,384]{2,1,0:T(8,128)(2,1)}), bf16[8,32,384]{2,1,0:T(8,128)(2,1)S(1)}, u32[]{:S(2)}, u32[]{:S(2)}) async-start(bf16[8,32,384]{2,1,0:T(8,128)(2,1)} %broadcast_in_dim.23), calls=%async_computation.2 | async-start | bytes 393216 | tf_op jit(solution)/shard_map/all_to_all | solution.py:322
  36.9 14.9 %collective-permute-start.16 = (bf16[8,64,384]{2,1,0:T(8,128)(2,1)S(1)}, bf16[8,64,384]{2,1,0:T(8,128)(2,1)S(1)}, u32[]{:S(2)}, u32[]{:S(2)}) collective-permute-start(bf16[8,64,384]{2,1,0:T(8,128)(2,1)S(1)} %all-to-all-done.own_ref), channel_id=1, source_target_pairs={{0,1},{1,2},{2,0},{3,4},{4,5},{5,3},{6,7},{7,8},{8,6},{9,10},{10,1... | collective-permute-start | bytes 1179656 | tf_op jit(solution)/shard_map/ppermute | solution.py:307
  40.0 21.1 %collective-permute-start.17 = (bf16[8,64,384]{2,1,0:T(8,128)(2,1)S(1)}, bf16[8,64,384]{2,1,0:T(8,128)(2,1)S(1)}, u32[]{:S(2)}, u32[]{:S(2)}) collective-permute-start(bf16[8,64,384]{2,1,0:T(8,128)(2,1)S(1)} %all-to-all-done.own_ref), channel_id=1, source_target_pairs={{0,2},{1,0},{2,1},{3,5},{4,3},{5,4},{6,8},{7,6},{8,7},{9,11},{10,9... | collective-permute-start | bytes 1179656 | tf_op jit(solution)/shard_map/ppermute | solution.py:307
  45.7 20.1 %collective-permute-start.19 = (bf16[8,32,384]{2,1,0:T(8,128)(2,1)S(1)}, bf16[8,32,384]{2,1,0:T(8,128)(2,1)S(1)}, u32[]{:S(2)}, u32[]{:S(2)}) collective-permute-start(bf16[8,32,384]{2,1,0:T(8,128)(2,1)S(1)} %all-to-all-done.2.own_ref), channel_id=1, source_target_pairs={{0,1},{1,2},{2,0},{3,4},{4,5},{5,3},{6,7},{7,8},{8,6},{9,10},{10,1... | collective-permute-start | bytes 589832 | tf_op jit(solution)/shard_map/ppermute | solution.py:307
  48.7 18.7 %collective-permute-start.20 = (bf16[8,32,384]{2,1,0:T(8,128)(2,1)S(1)}, bf16[8,32,384]{2,1,0:T(8,128)(2,1)S(1)}, u32[]{:S(2)}, u32[]{:S(2)}) collective-permute-start(bf16[8,32,384]{2,1,0:T(8,128)(2,1)S(1)} %all-to-all-done.2.own_ref), channel_id=1, source_target_pairs={{0,2},{1,0},{2,1},{3,5},{4,3},{5,4},{6,8},{7,6},{8,7},{9,11},{10,9... | collective-permute-start | bytes 589832 | tf_op jit(solution)/shard_map/ppermute | solution.py:307
  73.2 7.9 %collective-permute-start.22 = (bf16[8,32,384]{2,1,0:T(8,128)(2,1)S(1)}, bf16[8,32,384]{2,1,0:T(8,128)(2,1)S(1)}, u32[]{:S(2)}, u32[]{:S(2)}) collective-permute-start(bf16[8,32,384]{2,1,0:T(8,128)(2,1)S(1)} %get-tuple-element.45), channel_id=1, source_target_pairs={{0,2},{1,0},{2,1},{3,5},{4,3},{5,4},{6,8},{7,6},{8,7},{9,11},{10,9... | collective-permute-start | bytes 589832 | tf_op jit(solution)/shard_map/ppermute | solution.py:307
  75.2 8.1 %collective-permute-start.21 = (bf16[8,32,384]{2,1,0:T(8,128)(2,1)S(1)}, bf16[8,32,384]{2,1,0:T(8,128)(2,1)S(1)}, u32[]{:S(2)}, u32[]{:S(2)}) collective-permute-start(bf16[8,32,384]{2,1,0:T(8,128)(2,1)S(1)} %get-tuple-element.44), channel_id=1, source_target_pairs={{0,1},{1,2},{2,0},{3,4},{4,5},{5,3},{6,7},{7,8},{8,6},{9,10},{10,1... | collective-permute-start | bytes 589832 | tf_op jit(solution)/shard_map/ppermute | solution.py:307
  83.2 19.6 %copy-start.3 = (bf16[1,64,192]{2,1,0:T(8,128)(2,1)S(1)}, bf16[1,64,192]{2,1,0:T(8,128)(2,1)}, u32[]{:S(2)}) copy-start(bf16[1,64,192]{2,1,0:T(8,128)(2,1)} %param.27) | copy-start | bytes 73732
  98.4 17.5 %all-to-all-start.1 = ((bf16[24,32,384]{2,1,0:T(8,128)(2,1)}), bf16[24,32,384]{2,1,0:T(8,128)(2,1)S(1)}, u32[]{:S(2)}, u32[]{:S(2)}) async-start(bf16[24,32,384]{2,1,0:T(8,128)(2,1)} %get-tuple-element.41), calls=%async_computation.1 | async-start | bytes 1179648 | tf_op jit(solution)/shard_map/all_to_all | solution.py:322
  103.9 28.2 %collective-permute-start.23 = (bf16[64,192]{1,0:T(8,128)(2,1)S(1)}, bf16[64,192]{1,0:T(8,128)(2,1)S(1)}, u32[]{:S(2)}, u32[]{:S(2)}) collective-permute-start(bf16[64,192]{1,0:T(8,128)(2,1)S(1)} %pad_maximum_fusion.2), channel_id=1, source_target_pairs={{24,0},{48,24},{72,48},{96,72},{120,96},{144,120},{168,144},{192,1... | collective-permute-start | bytes 73736 | tf_op jit(solution)/shard_map/ppermute | solution.py:302
  116.1 16.3 %collective-permute-start.18 = (bf16[64,192]{1,0:T(8,128)(2,1)S(1)}, bf16[64,192]{1,0:T(8,128)(2,1)S(1)}, u32[]{:S(2)}, u32[]{:S(2)}) collective-permute-start(bf16[64,192]{1,0:T(8,128)(2,1)S(1)} %pad_maximum_fusion.1), channel_id=1, source_target_pairs={{0,24},{24,48},{48,72},{72,96},{96,120},{120,144},{144,168},{168,1... | collective-permute-start | bytes 73736 | tf_op jit(solution)/shard_map/ppermute | solution.py:302

commit v5 on v4

--- a/solution.py
+++ b/solution.py
@@ -147,16 +147,14 @@
     own_ref,
     low_ref,
     high_ref,
+    forward_ref,
     dctx_ref,
     gain_ref,
     wq_hbm,
     wk_hbm,
     wv_hbm,
-    stay_ref,
-    up_ref,
-    down_ref,
+    term_ref,
     blocks,
-    terms,
     xs,
     ns,
     ds,
@@ -166,6 +164,7 @@
     sems,
 ):
     wq_in, wk_in, wv_in = fetches((wq_hbm, wk_hbm, wv_hbm), (wq_ref, wk_ref, wv_ref), sems)
+    term_ref[:, : forward_ref.shape[1], :] = forward_ref[...]
     gathered(own_ref, low_ref, high_ref, blocks)
     runs, lines, half, wide = blocks.shape
     parts = runs * lines
@@ -220,14 +219,8 @@
     for u in range(parts // 2):
         span = slice(wide * u, wide * (u + 1))
         out = (ds[:, span] * inverse - xs[:, span].astype(F32) * factor).astype(BF16)
-        for i in range(2):
-            t = 2 * u + i
-            cols = slice(share * i, share * (i + 1))
-            terms[t % runs, t // runs] = jnp.concatenate([out[:half, cols], out[half:, cols]], axis=1)
-    at = lax.axis_index("run")
-    stay_ref[...] = terms[at]
-    up_ref[...] = terms[lax.rem(at + 1, runs)]
-    down_ref[...] = terms[lax.rem(at + runs - 1, runs)]
+        term_ref[2 * u, half:, :] = jnp.concatenate([out[:half, :share], out[half:, :share]], axis=1)
+        term_ref[2 * u + 1, half:, :] = jnp.concatenate([out[:half, share:], out[half:, share:]], axis=1)
 
 
 def kernel_call(body, outs, scratch, offsets, args, weights):
@@ -266,19 +259,18 @@
     return kernel_call(forward_kernel, outs, scratch, offsets, (*blocks, gain), (wq, wk, wv, wo))
 
 
-def backward_term(offsets, blocks, dctx, gain, wq, wk, wv):
+def both_terms(offsets, blocks, term, dctx, gain, wq, wk, wv):
     lines, half, wide = blocks[0].shape
     width = gain.shape[1]
     runs = len(blocks)
-    outs = (jax.ShapeDtypeStruct((lines, half, wide), BF16),) * runs
+    outs = jax.ShapeDtypeStruct((runs * lines, 2 * half, wide), BF16)
     scratch = [
-        pltpu.VMEM((runs, lines, half, wide), BF16),
         pltpu.VMEM((runs, lines, half, wide), BF16),
         pltpu.VMEM((2 * half, width), BF16),
         pltpu.VMEM((2 * half, width), BF16),
         pltpu.VMEM((2 * half, width), F32),
     ]
-    return kernel_call(backward_kernel, outs, scratch, offsets, (*blocks, dctx, gain), (wq, wk, wv))
+    return kernel_call(backward_kernel, outs, scratch, offsets, (*blocks, term, dctx, gain), (wq, wk, wv))
 
 
 def folded(block):
@@ -325,11 +317,6 @@
 def spread(block):
     own = exchanged(jnp.broadcast_to(block[None], (lax.axis_size("line"),) + block.shape), "line")
     return own, around(own, "run", 1), around(own, "run", -1)
-
-
-def total(rows, blocks):
-    summed = jnp.sum(blocks.astype(F32), axis=0)
-    return unfolded((folded(rows).astype(F32) + summed).astype(BF16))
 
 
 def local(fwd_input, bwd_grad, parked, norm_gain, w_query, w_key, w_value, w_out, offsets, mirror):
@@ -341,13 +328,11 @@
     back = spread(swapped[half:])
     parked_rows = unfolded(swapped[:half])
     term, dctx = forward_term(offsets, pair, norm_gain, w_query[0], w_key[0], w_value[0], w_out[0])
-    layer_out = total(fwd_rows, exchanged(term, TENSOR))
+    terms = both_terms(offsets, back, term, dctx, norm_gain, w_query[0], w_key[0], w_value[0])
+    summed = jnp.sum(exchanged(terms, TENSOR).astype(F32), axis=0)
+    layer_out = unfolded((folded(fwd_rows).astype(F32) + summed[:half]).astype(BF16))
+    grad_out = unfolded((folded(grad_rows).astype(F32) + summed[half:]).astype(BF16))
     next_rows = passed_along(layer_out, 1)
-    stay, up, down = backward_term(offsets, back, dctx, norm_gain, w_query[0], w_key[0], w_value[0])
-    low = around(up, "run", 1)
-    high = around(down, "run", -1)
-    column = (stay.astype(F32) + low.astype(F32) + high.astype(F32)).astype(BF16)
-    grad_out = total(grad_rows, exchanged(column, "line"))
     prev_rows = passed_along(grad_out, -1)
     return (next_rows[None], prev_rows[None], parked_rows[None])
 

time: 135 us -> 132 us (0.978)
  the two profiles are of different devices: /device:TPU:1 before, /device:TPU:66 now
where the time goes in v5:
time: 132 us; the launch traced here: 131 us
  starting transfers between devices  65.1 us (49%)
  waiting for transfers between devices  47.2 us (36%)
  Pallas kernels  11.2 us (8%)
  local copies, waits for them, and re-layouts  4.44 us (3%)
  other arithmetic  1.86 us (1%)
    all_to_all x3, waiting for transfers between devices, exchanged(): return lax.all_to_all(blocks, axes, 0, 0, tiled=True)  30.9 us
    all_to_all x3, starting transfers between devices, exchanged(): return lax.all_to_all(blocks, axes, 0, 0, tiled=True)  24.2 us
    ppermute x1, starting transfers between devices, swap_by(): return lambda held: lax.ppermute(held, SECTION, route)  15.2 us
    ppermute x2, starting transfers between devices, passed_along(): return lax.ppermute(block, SECTION, route)  14 us
    ppermute x4, starting transfers between devices, around(): lax.ppermute(block, axis, [(i, (i + distance) % count) for i in range(cou...  11.7 us
    pallas_call x2, Pallas kernels, kernel_call(): pl.pallas_call(body, out_shape=outs, in_specs=specs, out_specs=jax.tree.m...  11.2 us
    ppermute x4, waiting for transfers between devices, around(): lax.ppermute(block, axis, [(i, (i + distance) % count) for i in range(cou...  7.54 us
    ppermute x2, waiting for transfers between devices, passed_along(): return lax.ppermute(block, SECTION, route)  6.59 us
  transfers between devices with their start and end apart: 10, of which 6 were waited for; matrix products, arithmetic and copies ran while one was open for 2% of the time, Pallas kernels for 3%

profile of v5, /device:TPU:66, one launch (start us, length us, event | category | flops | bytes accessed | tf_op | source)
XLA Modules:
  0.0 130.7 jit_solution(9099554540964269201)
XLA Ops:
  0.7 0.9 pad_maximum_fusion
  1.6 0.8 broadcast_in_dim.22
  2.4 7.1 %all-to-all-start.1 = ((bf16[8,64,384]{2,1,0:T(8,128)(2,1)}), bf16[8,64,384]{2,1,0:T(8,128)(2,1)S(1)}, u32[]{:S(2)}, u32[]{:S(2)}) async-start(bf16[8,64,384]{2,1,0:T(8,128)(2,1)} %broadcast_in_dim.22), calls=%async_computation.1 | async-start | bytes 786432 | tf_op jit(solution)/shard_map/all_to_all | solution.py:314
  9.6 0.1 maximum_maximum_fusion
  9.6 17.3 %conditional.1 = (bf16[64,384]{1,0:T(8,128)(2,1)}) conditional(s32[]{:T(128)} %bitcast.2, bf16[64,384]{1,0:T(8,128)(2,1)S(1)} %maximum_maximum_fusion, bf16[64,384]{1,0:T(8,128)(2,1)S(1)} %maximum_maximum_fusion, bf16[64,384]{1,0:T(8,128)(2,1)S(1)} %maximum_maximum_fusion, ...), branch_computations={%region_0.0_spmd, %region_1.0_spmd, %region_2.0_spmd, %region_3.0_... | conditional | bytes 196656 | solution.py:310
  9.6 15.2 %collective-permute-start.12 = (bf16[64,384]{1,0:T(8,128)(2,1)S(1)}, bf16[64,384]{1,0:T(8,128)(2,1)}, u32[]{:S(2)}, u32[]{:S(2)}) collective-permute-start(bf16[64,384]{1,0:T(8,128)(2,1)S(1)} %param.12), channel_id=1, source_target_pairs={{0,672},{24,696},{48,720},{72,744},{96,576},{120,600},{144,624},{1... | collective-permute-start | bytes 147464 | tf_op jit(solution)/shard_map/cond/branch_12_fun/ppermute | solution.py:308
  24.8 2.2 %collective-permute-done.12 = bf16[64,384]{1,0:T(8,128)(2,1)} collective-permute-done((bf16[64,384]{1,0:T(8,128)(2,1)S(1)}, bf16[64,384]{1,0:T(8,128)(2,1)}, u32[]{:S(2)}, u32[]{:S(2)}) %collective-permute-start.12) | collective-permute-done | bytes 49184 | tf_op jit(solution)/shard_map/cond/branch_12_fun/ppermute | solution.py:308
  27.0 0.7 slice.93
  27.7 0.7 broadcast_in_dim.10
  28.4 7.8 %all-to-all-start = ((bf16[8,32,384]{2,1,0:T(8,128)(2,1)}), bf16[8,32,384]{2,1,0:T(8,128)(2,1)S(1)}, u32[]{:S(2)}, u32[]{:S(2)}) async-start(bf16[8,32,384]{2,1,0:T(8,128)(2,1)} %broadcast_in_dim.10), calls=%async_computation | async-start | bytes 393216 | tf_op jit(solution)/shard_map/all_to_all | solution.py:314
  36.3 2.4 %collective-permute-start.18 = (bf16[8,64,384]{2,1,0:T(8,128)(2,1)S(1)}, bf16[8,64,384]{2,1,0:T(8,128)(2,1)S(1)}, u32[]{:S(2)}, u32[]{:S(2)}) collective-permute-start(bf16[8,64,384]{2,1,0:T(8,128)(2,1)S(1)} %all-to-all-done.1.own_ref), channel_id=1, source_target_pairs={{0,1},{1,2},{2,0},{3,4},{4,5},{5,3},{6,7},{7,8},{8,6},{9,10},{10,1... | collective-permute-start | bytes 1179656 | tf_op jit(solution)/shard_map/ppermute | solution.py:299
  38.6 3.4 %collective-permute-start.19 = (bf16[8,64,384]{2,1,0:T(8,128)(2,1)S(1)}, bf16[8,64,384]{2,1,0:T(8,128)(2,1)S(1)}, u32[]{:S(2)}, u32[]{:S(2)}) collective-permute-start(bf16[8,64,384]{2,1,0:T(8,128)(2,1)S(1)} %all-to-all-done.1.own_ref), channel_id=1, source_target_pairs={{0,2},{1,0},{2,1},{3,5},{4,3},{5,4},{6,8},{7,6},{8,7},{9,11},{10,9... | collective-permute-start | bytes 1179656 | tf_op jit(solution)/shard_map/ppermute | solution.py:299
  42.1 3.9 %all-to-all-done.own_ref = bf16[8,32,384]{2,1,0:T(8,128)(2,1)S(1)} async-done(((bf16[8,32,384]{2,1,0:T(8,128)(2,1)}), bf16[8,32,384]{2,1,0:T(8,128)(2,1)S(1)}, u32[]{:S(2)}, u32[]{:S(2)}) %all-to-all-start) | async-done | bytes 196640 | tf_op jit(solution)/shard_map/all_to_all | solution.py:314
  46.0 2.4 %collective-permute-start.16 = (bf16[8,32,384]{2,1,0:T(8,128)(2,1)S(1)}, bf16[8,32,384]{2,1,0:T(8,128)(2,1)S(1)}, u32[]{:S(2)}, u32[]{:S(2)}) collective-permute-start(bf16[8,32,384]{2,1,0:T(8,128)(2,1)S(1)} %all-to-all-done.own_ref), channel_id=1, source_target_pairs={{0,1},{1,2},{2,0},{3,4},{4,5},{5,3},{6,7},{7,8},{8,6},{9,10},{10,1... | collective-permute-start | bytes 589832 | tf_op jit(solution)/shard_map/ppermute | solution.py:299
  48.4 3.4 %collective-permute-start.17 = (bf16[8,32,384]{2,1,0:T(8,128)(2,1)S(1)}, bf16[8,32,384]{2,1,0:T(8,128)(2,1)S(1)}, u32[]{:S(2)}, u32[]{:S(2)}) collective-permute-start(bf16[8,32,384]{2,1,0:T(8,128)(2,1)S(1)} %all-to-all-done.own_ref), channel_id=1, source_target_pairs={{0,2},{1,0},{2,1},{3,5},{4,3},{5,4},{6,8},{7,6},{8,7},{9,11},{10,9... | collective-permute-start | bytes 589832 | tf_op jit(solution)/shard_map/ppermute | solution.py:299
  51.9 6.1 %collective-permute-done.19.high_ref = bf16[8,64,384]{2,1,0:T(8,128)(2,1)S(1)} collective-permute-done((bf16[8,64,384]{2,1,0:T(8,128)(2,1)S(1)}, bf16[8,64,384]{2,1,0:T(8,128)(2,1)S(1)}, u32[]{:S(2)}, u32[]{:S(2)}) %collective-permute-start.19) | collective-permute-done | bytes 393248 | tf_op jit(solution)/shard_map/ppermute | solution.py:299
  58.0 4.1 %shard_map.121 = (bf16[24,32,384]{2,1,0:T(8,128)(2,1)S(1)}, bf16[64,128]{1,0:T(8,128)(2,1)S(1)}) custom-call(s32[1,2,8]{2,1,0:T(2,128)S(1)} %copy-done.1, bf16[8,64,384]{2,1,0:T(8,128)(2,1)S(1)} %all-to-all-done.1.own_ref, bf16[8,64,384]{2,1,0:T(8,128)(2,1)S(1)} %collective-permute-done.18.low_ref, bf16[8,64,384]{2,1,0:T(8,128)(2,1)S(1)} %collective-permute-done.19.high_ref, ...), custom_call_target="tpu_custom_call" | custom-call | tf_op jit(solution)/shard_map/pallas_call | solution.py:232
  62.1 1.5 %collective-permute-done.17.high_ref = bf16[8,32,384]{2,1,0:T(8,128)(2,1)S(1)} collective-permute-done((bf16[8,32,384]{2,1,0:T(8,128)(2,1)S(1)}, bf16[8,32,384]{2,1,0:T(8,128)(2,1)S(1)}, u32[]{:S(2)}, u32[]{:S(2)}) %collective-permute-start.17) | collective-permute-done | bytes 196640 | tf_op jit(solution)/shard_map/ppermute | solution.py:299
  63.6 7.1 %shard_map.122 = bf16[24,64,384]{2,1,0:T(8,128)(2,1)} custom-call(s32[1,2,8]{2,1,0:T(2,128)S(1)} %copy-done.1, bf16[8,32,384]{2,1,0:T(8,128)(2,1)S(1)} %all-to-all-done.own_ref, bf16[8,32,384]{2,1,0:T(8,128)(2,1)S(1)} %collective-permute-done.16.low_ref, bf16[8,32,384]{2,1,0:T(8,128)(2,1)S(1)} %collective-permute-done.17.high_ref, ...), custom_call_target="tpu_custom_call" | custom-call | tf_op jit(solution)/shard_map/pallas_call | solution.py:232
  70.7 0.0 copy-start.3
  70.7 9.3 %all-to-all-start.2 = ((bf16[24,64,384]{2,1,0:T(8,128)(2,1)}), bf16[24,64,384]{2,1,0:T(8,128)(2,1)S(1)}, u32[]{:S(2)}, u32[]{:S(2)}) async-start(bf16[24,64,384]{2,1,0:T(8,128)(2,1)} %shard_map.122), calls=%async_computation.2 | async-start | bytes 2359296 | tf_op jit(solution)/shard_map/all_to_all | solution.py:314
  80.0 0.9 fusion.2
  80.9 27.0 %all-to-all-done.2 = bf16[24,64,384]{2,1,0:T(8,128)(2,1)S(1)} async-done(((bf16[24,64,384]{2,1,0:T(8,128)(2,1)}), bf16[24,64,384]{2,1,0:T(8,128)(2,1)S(1)}, u32[]{:S(2)}, u32[]{:S(2)}) %all-to-all-start.2) | async-done | bytes 1179680 | tf_op jit(solution)/shard_map/all_to_all | solution.py:314
  107.9 0.2 convert_reduce_fusion
  108.0 0.1 fusion
  108.1 0.1 fusion.3
  108.2 12.1 %collective-permute-start.21 = (bf16[64,192]{1,0:T(8,128)(2,1)S(1)}, bf16[64,192]{1,0:T(8,128)(2,1)S(1)}, u32[]{:S(2)}, u32[]{:S(2)}) collective-permute-start(bf16[64,192]{1,0:T(8,128)(2,1)S(1)} %pad_maximum_fusion.2), channel_id=1, source_target_pairs={{24,0},{48,24},{72,48},{96,72},{120,96},{144,120},{168,144},{192,1... | collective-permute-start | bytes 73736 | tf_op jit(solution)/shard_map/ppermute | solution.py:294
  120.3 1.9 %collective-permute-start.20 = (bf16[64,192]{1,0:T(8,128)(2,1)S(1)}, bf16[64,192]{1,0:T(8,128)(2,1)S(1)}, u32[]{:S(2)}, u32[]{:S(2)}) collective-permute-start(bf16[64,192]{1,0:T(8,128)(2,1)S(1)} %pad_maximum_fusion.1), channel_id=1, source_target_pairs={{0,24},{24,48},{48,72},{72,96},{96,120},{120,144},{144,168},{168,1... | collective-permute-start | bytes 73736 | tf_op jit(solution)/shard_map/ppermute | solution.py:294
  122.3 0.6 maximum_bitcast_fusion
  122.9 6.6 %collective-permute-done.20 = bf16[64,192]{1,0:T(8,128)(2,1)S(1)} collective-permute-done((bf16[64,192]{1,0:T(8,128)(2,1)S(1)}, bf16[64,192]{1,0:T(8,128)(2,1)S(1)}, u32[]{:S(2)}, u32[]{:S(2)}) %collective-permute-start.20) | collective-permute-done | bytes 24608 | tf_op jit(solution)/shard_map/ppermute | solution.py:294
  129.5 0.6 copy.31
  130.1 0.6 copy.32
  (20 shorter events, 0.1 us)
Async XLA Ops:
  0.6 8.9 %copy-start.2 = (bf16[1,64,192]{2,1,0:T(8,128)(2,1)S(1)}, bf16[1,64,192]{2,1,0:T(8,128)(2,1)}, u32[]{:S(2)}) copy-start(bf16[1,64,192]{2,1,0:T(8,128)(2,1)} %param.26) | copy-start | bytes 73732
  0.6 8.8 %copy-start.5 = (s32[32]{0:T(128)S(1)}, s32[32]{0:T(128)}, u32[]{:S(2)}) copy-start(s32[32]{0:T(128)} %param.35) | copy-start | bytes 388
  0.7 8.9 %copy-start.4 = (bf16[1,64,192]{2,1,0:T(8,128)(2,1)S(1)}, bf16[1,64,192]{2,1,0:T(8,128)(2,1)}, u32[]{:S(2)}) copy-start(bf16[1,64,192]{2,1,0:T(8,128)(2,1)} %param.28) | copy-start | bytes 73732
  0.7 57.3 %copy-start = (f32[1,4608]{1,0:T(1,128)S(1)}, f32[1,4608]{1,0:T(1,128)}, u32[]{:S(2)}) copy-start(f32[1,4608]{1,0:T(1,128)} %gain_ref.3) | copy-start | bytes 55300
  0.7 57.3 %copy-start.1 = (s32[1,2,8]{2,1,0:T(2,128)S(1)}, s32[1,2,8]{2,1,0:T(2,128)}, u32[]{:S(2)}) copy-start(s32[1,2,8]{2,1,0:T(2,128)} %off_ref.3) | copy-start | bytes 196
  2.4 25.4 %all-to-all-start.1 = ((bf16[8,64,384]{2,1,0:T(8,128)(2,1)}), bf16[8,64,384]{2,1,0:T(8,128)(2,1)S(1)}, u32[]{:S(2)}, u32[]{:S(2)}) async-start(bf16[8,64,384]{2,1,0:T(8,128)(2,1)} %broadcast_in_dim.22), calls=%async_computation.1 | async-start | bytes 786432 | tf_op jit(solution)/shard_map/all_to_all | solution.py:314
  9.6 17.3 %collective-permute-start.12 = (bf16[64,384]{1,0:T(8,128)(2,1)S(1)}, bf16[64,384]{1,0:T(8,128)(2,1)}, u32[]{:S(2)}, u32[]{:S(2)}) collective-permute-start(bf16[64,384]{1,0:T(8,128)(2,1)S(1)} %param.12), channel_id=1, source_target_pairs={{0,672},{24,696},{48,720},{72,744},{96,576},{120,600},{144,624},{1... | collective-permute-start | bytes 147464 | tf_op jit(solution)/shard_map/cond/branch_12_fun/ppermute | solution.py:308
  28.4 17.6 %all-to-all-start = ((bf16[8,32,384]{2,1,0:T(8,128)(2,1)}), bf16[8,32,384]{2,1,0:T(8,128)(2,1)S(1)}, u32[]{:S(2)}, u32[]{:S(2)}) async-start(bf16[8,32,384]{2,1,0:T(8,128)(2,1)} %broadcast_in_dim.10), calls=%async_computation | async-start | bytes 393216 | tf_op jit(solution)/shard_map/all_to_all | solution.py:314
  36.3 15.6 %collective-permute-start.18 = (bf16[8,64,384]{2,1,0:T(8,128)(2,1)S(1)}, bf16[8,64,384]{2,1,0:T(8,128)(2,1)S(1)}, u32[]{:S(2)}, u32[]{:S(2)}) collective-permute-start(bf16[8,64,384]{2,1,0:T(8,128)(2,1)S(1)} %all-to-all-done.1.own_ref), channel_id=1, source_target_pairs={{0,1},{1,2},{2,0},{3,4},{4,5},{5,3},{6,7},{7,8},{8,6},{9,10},{10,1... | collective-permute-start | bytes 1179656 | tf_op jit(solution)/shard_map/ppermute | solution.py:299
  38.6 19.3 %collective-permute-start.19 = (bf16[8,64,384]{2,1,0:T(8,128)(2,1)S(1)}, bf16[8,64,384]{2,1,0:T(8,128)(2,1)S(1)}, u32[]{:S(2)}, u32[]{:S(2)}) collective-permute-start(bf16[8,64,384]{2,1,0:T(8,128)(2,1)S(1)} %all-to-all-done.1.own_ref), channel_id=1, source_target_pairs={{0,2},{1,0},{2,1},{3,5},{4,3},{5,4},{6,8},{7,6},{8,7},{9,11},{10,9... | collective-permute-start | bytes 1179656 | tf_op jit(solution)/shard_map/ppermute | solution.py:299
  46.0 16.1 %collective-permute-start.16 = (bf16[8,32,384]{2,1,0:T(8,128)(2,1)S(1)}, bf16[8,32,384]{2,1,0:T(8,128)(2,1)S(1)}, u32[]{:S(2)}, u32[]{:S(2)}) collective-permute-start(bf16[8,32,384]{2,1,0:T(8,128)(2,1)S(1)} %all-to-all-done.own_ref), channel_id=1, source_target_pairs={{0,1},{1,2},{2,0},{3,4},{4,5},{5,3},{6,7},{7,8},{8,6},{9,10},{10,1... | collective-permute-start | bytes 589832 | tf_op jit(solution)/shard_map/ppermute | solution.py:299
  48.4 15.1 %collective-permute-start.17 = (bf16[8,32,384]{2,1,0:T(8,128)(2,1)S(1)}, bf16[8,32,384]{2,1,0:T(8,128)(2,1)S(1)}, u32[]{:S(2)}, u32[]{:S(2)}) collective-permute-start(bf16[8,32,384]{2,1,0:T(8,128)(2,1)S(1)} %all-to-all-done.own_ref), channel_id=1, source_target_pairs={{0,2},{1,0},{2,1},{3,5},{4,3},{5,4},{6,8},{7,6},{8,7},{9,11},{10,9... | collective-permute-start | bytes 589832 | tf_op jit(solution)/shard_map/ppermute | solution.py:299
  70.7 9.3 %copy-start.3 = (bf16[1,64,192]{2,1,0:T(8,128)(2,1)S(1)}, bf16[1,64,192]{2,1,0:T(8,128)(2,1)}, u32[]{:S(2)}) copy-start(bf16[1,64,192]{2,1,0:T(8,128)(2,1)} %param.27) | copy-start | bytes 73732
  70.7 37.2 %all-to-all-start.2 = ((bf16[24,64,384]{2,1,0:T(8,128)(2,1)}), bf16[24,64,384]{2,1,0:T(8,128)(2,1)S(1)}, u32[]{:S(2)}, u32[]{:S(2)}) async-start(bf16[24,64,384]{2,1,0:T(8,128)(2,1)} %shard_map.122), calls=%async_computation.2 | async-start | bytes 2359296 | tf_op jit(solution)/shard_map/all_to_all | solution.py:314
  108.2 14.7 %collective-permute-start.21 = (bf16[64,192]{1,0:T(8,128)(2,1)S(1)}, bf16[64,192]{1,0:T(8,128)(2,1)S(1)}, u32[]{:S(2)}, u32[]{:S(2)}) collective-permute-start(bf16[64,192]{1,0:T(8,128)(2,1)S(1)} %pad_maximum_fusion.2), channel_id=1, source_target_pairs={{24,0},{48,24},{72,48},{96,72},{120,96},{144,120},{168,144},{192,1... | collective-permute-start | bytes 73736 | tf_op jit(solution)/shard_map/ppermute | solution.py:294
  120.3 9.1 %collective-permute-start.20 = (bf16[64,192]{1,0:T(8,128)(2,1)S(1)}, bf16[64,192]{1,0:T(8,128)(2,1)S(1)}, u32[]{:S(2)}, u32[]{:S(2)}) collective-permute-start(bf16[64,192]{1,0:T(8,128)(2,1)S(1)} %pad_maximum_fusion.1), channel_id=1, source_target_pairs={{0,24},{24,48},{48,72},{72,96},{96,120},{120,144},{144,168},{168,1... | collective-permute-start | bytes 73736 | tf_op jit(solution)/shard_map/ppermute | solution.py:294

commit v6 on v5

--- a/solution.py
+++ b/solution.py
@@ -90,12 +90,12 @@
     wo_hbm,
     term_ref,
     dctx_ref,
+    wq_ref,
+    wk_ref,
+    wv_ref,
     blocks,
     xs,
     gs,
-    wq_ref,
-    wk_ref,
-    wv_ref,
     wo_ref,
     sems,
 ):
@@ -150,20 +150,15 @@
     forward_ref,
     dctx_ref,
     gain_ref,
-    wq_hbm,
-    wk_hbm,
-    wv_hbm,
+    wq_ref,
+    wk_ref,
+    wv_ref,
     term_ref,
     blocks,
     xs,
     ns,
     ds,
-    wq_ref,
-    wk_ref,
-    wv_ref,
-    sems,
 ):
-    wq_in, wk_in, wv_in = fetches((wq_hbm, wk_hbm, wv_hbm), (wq_ref, wk_ref, wv_ref), sems)
     term_ref[:, : forward_ref.shape[1], :] = forward_ref[...]
     gathered(own_ref, low_ref, high_ref, blocks)
     runs, lines, half, wide = blocks.shape
@@ -191,11 +186,8 @@
         span = slice(wide * u, wide * (u + 1))
         ns[:, span] = (xs[:, span].astype(F32) * inverse * gain_ref[:, span]).astype(BF16)
     normed = ns[...]
-    arrive(wq_in)
     queries = dot(normed, wq_ref[...]).astype(BF16)
-    arrive(wk_in)
     keys = dot(normed, wk_ref[...]).astype(BF16)
-    arrive(wv_in)
     values = dot(normed, wv_ref[...]).astype(BF16)
     mask = causal(off_ref, 1, rows)
     grads = []
@@ -223,17 +215,15 @@
         term_ref[2 * u + 1, half:, :] = jnp.concatenate([out[:half, share:], out[half:, share:]], axis=1)
 
 
-def kernel_call(body, outs, scratch, offsets, args, weights):
+def kernel_call(body, outs, scratch, offsets, args, weights=()):
     vmem = pl.BlockSpec(memory_space=pltpu.VMEM)
     specs = [pl.BlockSpec(memory_space=pltpu.SMEM)] + [vmem] * len(args)
     specs += [pl.BlockSpec(memory_space=pltpu.HBM)] * len(weights)
-    scratch = scratch + [pltpu.VMEM(w.shape, w.dtype) for w in weights]
-    scratch.append(pltpu.SemaphoreType.DMA((len(weights), PIECES)))
     return pl.pallas_call(
         body,
         out_shape=outs,
         in_specs=specs,
-        out_specs=jax.tree.map(lambda _: vmem, outs),
+        out_specs=tuple(vmem for _ in outs),
         scratch_shapes=scratch,
         compiler_params=pltpu.CompilerParams(vmem_limit_bytes=VMEM_LIMIT),
     )(offsets, *args, *[pltpu.with_memory_space_constraint(w, pltpu.HBM) for w in weights])
@@ -250,11 +240,14 @@
     outs = (
         jax.ShapeDtypeStruct((runs * lines, rows // 2, wide), BF16),
         jax.ShapeDtypeStruct((rows, wo.shape[0]), BF16),
+        *[pltpu.VMEM(w.shape, w.dtype) for w in (wq, wk, wv)],
     )
     scratch = [
         pltpu.VMEM((runs, lines, rows, wide), BF16),
         pltpu.VMEM((rows, width), BF16),
         pltpu.VMEM((rows, width), BF16),
+        pltpu.VMEM(wo.shape, wo.dtype),
+        pltpu.SemaphoreType.DMA((4, PIECES)),
     ]
     return kernel_call(forward_kernel, outs, scratch, offsets, (*blocks, gain), (wq, wk, wv, wo))
 
@@ -263,14 +256,14 @@
     lines, half, wide = blocks[0].shape
     width = gain.shape[1]
     runs = len(blocks)
-    outs = jax.ShapeDtypeStruct((runs * lines, 2 * half, wide), BF16)
+    outs = (jax.ShapeDtypeStruct((runs * lines, 2 * half, wide), BF16),)
     scratch = [
         pltpu.VMEM((runs, lines, half, wide), BF16),
         pltpu.VMEM((2 * half, width), BF16),
         pltpu.VMEM((2 * half, width), BF16),
         pltpu.VMEM((2 * half, width), F32),
     ]
-    return kernel_call(backward_kernel, outs, scratch, offsets, (*blocks, term, dctx, gain), (wq, wk, wv))
+    return kernel_call(backward_kernel, outs, scratch, offsets, (*blocks, term, dctx, gain, wq, wk, wv))[0]
 
 
 def folded(block):
@@ -327,8 +320,8 @@
     swapped = mirrored(jnp.concatenate([folded(fwd_rows), folded(parked[0])], axis=0), mirror[0])
     back = spread(swapped[half:])
     parked_rows = unfolded(swapped[:half])
-    term, dctx = forward_term(offsets, pair, norm_gain, w_query[0], w_key[0], w_value[0], w_out[0])
-    terms = both_terms(offsets, back, term, dctx, norm_gain, w_query[0], w_key[0], w_value[0])
+    term, dctx, wq, wk, wv = forward_term(offsets, pair, norm_gain, w_query[0], w_key[0], w_value[0], w_out[0])
+    terms = both_terms(offsets, back, term, dctx, norm_gain, wq, wk, wv)
     summed = jnp.sum(exchanged(terms, TENSOR).astype(F32), axis=0)
     layer_out = unfolded((folded(fwd_rows).astype(F32) + summed[:half]).astype(BF16))
     grad_out = unfolded((folded(grad_rows).astype(F32) + summed[half:]).astype(BF16))

time: 132 us -> 130 us (0.985)
  Pallas kernels: 11.2 us -> 9.62 us
    pallas_call x2, Pallas kernels: 11.2 us -> 9.62 us  [kernel_call(): pl.pallas_call(body, out_shape=outs, in_specs=specs, out_specs=tuple((vme...]
where the time goes in v6:
time: 130 us; the launch traced here: 129 us
  starting transfers between devices  65.3 us (50%)
  waiting for transfers between devices  47.1 us (36%)
  Pallas kernels  9.62 us (7%)
  local copies, waits for them, and re-layouts  4.44 us (3%)
  other arithmetic  1.86 us (1%)
    all_to_all x3, waiting for transfers between devices, exchanged(): return lax.all_to_all(blocks, axes, 0, 0, tiled=True)  30.9 us
    all_to_all x3, starting transfers between devices, exchanged(): return lax.all_to_all(blocks, axes, 0, 0, tiled=True)  24.4 us
    ppermute x1, starting transfers between devices, swap_by(): return lambda held: lax.ppermute(held, SECTION, route)  15.2 us
    ppermute x2, starting transfers between devices, passed_along(): return lax.ppermute(block, SECTION, route)  14.1 us
    ppermute x4, starting transfers between devices, around(): lax.ppermute(block, axis, [(i, (i + distance) % count) for i in range(cou...  11.7 us
    pallas_call x2, Pallas kernels, kernel_call(): pl.pallas_call(body, out_shape=outs, in_specs=specs, out_specs=tuple((vme...  9.62 us
    ppermute x4, waiting for transfers between devices, around(): lax.ppermute(block, axis, [(i, (i + distance) % count) for i in range(cou...  7.53 us
    ppermute x2, waiting for transfers between devices, passed_along(): return lax.ppermute(block, SECTION, route)  6.59 us
  transfers between devices with their start and end apart: 10, of which 6 were waited for; matrix products, arithmetic and copies ran while one was open for 2% of the time, Pallas kernels for 3%

profile of v6, /device:TPU:66, one launch (start us, length us, event | category | flops | bytes accessed | tf_op | source)
XLA Modules:
  0.0 129.2 jit_solution(802377202257354606)
XLA Ops:
  0.7 0.9 pad_maximum_fusion
  1.6 0.8 broadcast_in_dim.22
  2.4 7.1 %all-to-all-start.1 = ((bf16[8,64,384]{2,1,0:T(8,128)(2,1)}), bf16[8,64,384]{2,1,0:T(8,128)(2,1)S(1)}, u32[]{:S(2)}, u32[]{:S(2)}) async-start(bf16[8,64,384]{2,1,0:T(8,128)(2,1)} %broadcast_in_dim.22), calls=%async_computation.1 | async-start | bytes 786432 | tf_op jit(solution)/shard_map/all_to_all | solution.py:307
  9.6 0.1 maximum_maximum_fusion
  9.6 17.3 %conditional.1 = (bf16[64,384]{1,0:T(8,128)(2,1)}) conditional(s32[]{:T(128)} %bitcast.2, bf16[64,384]{1,0:T(8,128)(2,1)S(1)} %maximum_maximum_fusion, bf16[64,384]{1,0:T(8,128)(2,1)S(1)} %maximum_maximum_fusion, bf16[64,384]{1,0:T(8,128)(2,1)S(1)} %maximum_maximum_fusion, ...), branch_computations={%region_0.0_spmd, %region_1.0_spmd, %region_2.0_spmd, %region_3.0_... | conditional | bytes 196656 | solution.py:303
  9.6 15.2 %collective-permute-start.12 = (bf16[64,384]{1,0:T(8,128)(2,1)S(1)}, bf16[64,384]{1,0:T(8,128)(2,1)}, u32[]{:S(2)}, u32[]{:S(2)}) collective-permute-start(bf16[64,384]{1,0:T(8,128)(2,1)S(1)} %param.12), channel_id=1, source_target_pairs={{0,672},{24,696},{48,720},{72,744},{96,576},{120,600},{144,624},{1... | collective-permute-start | bytes 147464 | tf_op jit(solution)/shard_map/cond/branch_12_fun/ppermute | solution.py:301
  24.8 2.2 %collective-permute-done.12 = bf16[64,384]{1,0:T(8,128)(2,1)} collective-permute-done((bf16[64,384]{1,0:T(8,128)(2,1)S(1)}, bf16[64,384]{1,0:T(8,128)(2,1)}, u32[]{:S(2)}, u32[]{:S(2)}) %collective-permute-start.12) | collective-permute-done | bytes 49184 | tf_op jit(solution)/shard_map/cond/branch_12_fun/ppermute | solution.py:301
  27.0 0.7 slice.93
  27.7 0.0 all-to-all-done.1.own_ref
  27.7 0.7 broadcast_in_dim.10
  28.4 7.8 %all-to-all-start = ((bf16[8,32,384]{2,1,0:T(8,128)(2,1)}), bf16[8,32,384]{2,1,0:T(8,128)(2,1)S(1)}, u32[]{:S(2)}, u32[]{:S(2)}) async-start(bf16[8,32,384]{2,1,0:T(8,128)(2,1)} %broadcast_in_dim.10), calls=%async_computation | async-start | bytes 393216 | tf_op jit(solution)/shard_map/all_to_all | solution.py:307
  36.3 2.4 %collective-permute-start.18 = (bf16[8,64,384]{2,1,0:T(8,128)(2,1)S(1)}, bf16[8,64,384]{2,1,0:T(8,128)(2,1)S(1)}, u32[]{:S(2)}, u32[]{:S(2)}) collective-permute-start(bf16[8,64,384]{2,1,0:T(8,128)(2,1)S(1)} %all-to-all-done.1.own_ref), channel_id=1, source_target_pairs={{0,1},{1,2},{2,0},{3,4},{4,5},{5,3},{6,7},{7,8},{8,6},{9,10},{10,1... | collective-permute-start | bytes 1179656 | tf_op jit(solution)/shard_map/ppermute | solution.py:292
  38.6 3.4 %collective-permute-start.19 = (bf16[8,64,384]{2,1,0:T(8,128)(2,1)S(1)}, bf16[8,64,384]{2,1,0:T(8,128)(2,1)S(1)}, u32[]{:S(2)}, u32[]{:S(2)}) collective-permute-start(bf16[8,64,384]{2,1,0:T(8,128)(2,1)S(1)} %all-to-all-done.1.own_ref), channel_id=1, source_target_pairs={{0,2},{1,0},{2,1},{3,5},{4,3},{5,4},{6,8},{7,6},{8,7},{9,11},{10,9... | collective-permute-start | bytes 1179656 | tf_op jit(solution)/shard_map/ppermute | solution.py:292
  42.1 3.9 %all-to-all-done.own_ref = bf16[8,32,384]{2,1,0:T(8,128)(2,1)S(1)} async-done(((bf16[8,32,384]{2,1,0:T(8,128)(2,1)}), bf16[8,32,384]{2,1,0:T(8,128)(2,1)S(1)}, u32[]{:S(2)}, u32[]{:S(2)}) %all-to-all-start) | async-done | bytes 196640 | tf_op jit(solution)/shard_map/all_to_all | solution.py:307
  46.0 2.4 %collective-permute-start.16 = (bf16[8,32,384]{2,1,0:T(8,128)(2,1)S(1)}, bf16[8,32,384]{2,1,0:T(8,128)(2,1)S(1)}, u32[]{:S(2)}, u32[]{:S(2)}) collective-permute-start(bf16[8,32,384]{2,1,0:T(8,128)(2,1)S(1)} %all-to-all-done.own_ref), channel_id=1, source_target_pairs={{0,1},{1,2},{2,0},{3,4},{4,5},{5,3},{6,7},{7,8},{8,6},{9,10},{10,1... | collective-permute-start | bytes 589832 | tf_op jit(solution)/shard_map/ppermute | solution.py:292
  48.4 3.4 %collective-permute-start.17 = (bf16[8,32,384]{2,1,0:T(8,128)(2,1)S(1)}, bf16[8,32,384]{2,1,0:T(8,128)(2,1)S(1)}, u32[]{:S(2)}, u32[]{:S(2)}) collective-permute-start(bf16[8,32,384]{2,1,0:T(8,128)(2,1)S(1)} %all-to-all-done.own_ref), channel_id=1, source_target_pairs={{0,2},{1,0},{2,1},{3,5},{4,3},{5,4},{6,8},{7,6},{8,7},{9,11},{10,9... | collective-permute-start | bytes 589832 | tf_op jit(solution)/shard_map/ppermute | solution.py:292
  51.9 6.1 %collective-permute-done.19.high_ref = bf16[8,64,384]{2,1,0:T(8,128)(2,1)S(1)} collective-permute-done((bf16[8,64,384]{2,1,0:T(8,128)(2,1)S(1)}, bf16[8,64,384]{2,1,0:T(8,128)(2,1)S(1)}, u32[]{:S(2)}, u32[]{:S(2)}) %collective-permute-start.19) | collective-permute-done | bytes 393248 | tf_op jit(solution)/shard_map/ppermute | solution.py:292
  58.0 4.1 %shard_map.121 = (bf16[24,32,384]{2,1,0:T(8,128)(2,1)S(1)}, bf16[64,128]{1,0:T(8,128)(2,1)S(1)}, bf16[4608,128]{1,0:T(8,128)(2,1)S(1)}, bf16[4608,128]{1,0:T(8,128)(2,1)S(1)}, bf16[4608,128]{1,0:T(8,128)(2,1)S(1)}) custom-call(s32[1,2,8]{2,1,0:T(2,128)S(1)} %copy-done.1, bf16[8,64,384]{2,1,0:T(8,128)(2,1)S(1)} %all-to-all-done.1.own_ref, ...), custom_call_target="tpu_custom_call" | custom-call | tf_op jit(solution)/shard_map/pallas_call | solution.py:222
  62.1 1.5 %collective-permute-done.17.high_ref = bf16[8,32,384]{2,1,0:T(8,128)(2,1)S(1)} collective-permute-done((bf16[8,32,384]{2,1,0:T(8,128)(2,1)S(1)}, bf16[8,32,384]{2,1,0:T(8,128)(2,1)S(1)}, u32[]{:S(2)}, u32[]{:S(2)}) %collective-permute-start.17) | collective-permute-done | bytes 196640 | tf_op jit(solution)/shard_map/ppermute | solution.py:292
  63.6 5.5 %shard_map.122 = bf16[24,64,384]{2,1,0:T(8,128)(2,1)} custom-call(s32[1,2,8]{2,1,0:T(2,128)S(1)} %copy-done.1, bf16[8,32,384]{2,1,0:T(8,128)(2,1)S(1)} %all-to-all-done.own_ref, bf16[8,32,384]{2,1,0:T(8,128)(2,1)S(1)} %collective-permute-done.16.low_ref, bf16[8,32,384]{2,1,0:T(8,128)(2,1)S(1)} %collective-permute-done.17.high_ref, ...), custom_call_target="tpu_custom_call" | custom-call | tf_op jit(solution)/shard_map/pallas_call | solution.py:222
  69.1 9.4 %all-to-all-start.2 = ((bf16[24,64,384]{2,1,0:T(8,128)(2,1)}), bf16[24,64,384]{2,1,0:T(8,128)(2,1)S(1)}, u32[]{:S(2)}, u32[]{:S(2)}) async-start(bf16[24,64,384]{2,1,0:T(8,128)(2,1)} %shard_map.122), calls=%async_computation.2 | async-start | bytes 2359296 | tf_op jit(solution)/shard_map/all_to_all | solution.py:307
  78.5 0.9 fusion.2
  79.4 26.9 %all-to-all-done.2 = bf16[24,64,384]{2,1,0:T(8,128)(2,1)S(1)} async-done(((bf16[24,64,384]{2,1,0:T(8,128)(2,1)}), bf16[24,64,384]{2,1,0:T(8,128)(2,1)S(1)}, u32[]{:S(2)}, u32[]{:S(2)}) %all-to-all-start.2) | async-done | bytes 1179680 | tf_op jit(solution)/shard_map/all_to_all | solution.py:307
  106.3 0.2 convert_reduce_fusion
  106.5 0.1 fusion
  106.6 0.1 fusion.3
  106.7 12.2 %collective-permute-start.21 = (bf16[64,192]{1,0:T(8,128)(2,1)S(1)}, bf16[64,192]{1,0:T(8,128)(2,1)S(1)}, u32[]{:S(2)}, u32[]{:S(2)}) collective-permute-start(bf16[64,192]{1,0:T(8,128)(2,1)S(1)} %pad_maximum_fusion.2), channel_id=1, source_target_pairs={{24,0},{48,24},{72,48},{96,72},{120,96},{144,120},{168,144},{192,1... | collective-permute-start | bytes 73736 | tf_op jit(solution)/shard_map/ppermute | solution.py:287
  118.9 1.9 %collective-permute-start.20 = (bf16[64,192]{1,0:T(8,128)(2,1)S(1)}, bf16[64,192]{1,0:T(8,128)(2,1)S(1)}, u32[]{:S(2)}, u32[]{:S(2)}) collective-permute-start(bf16[64,192]{1,0:T(8,128)(2,1)S(1)} %pad_maximum_fusion.1), channel_id=1, source_target_pairs={{0,24},{24,48},{48,72},{72,96},{96,120},{120,144},{144,168},{168,1... | collective-permute-start | bytes 73736 | tf_op jit(solution)/shard_map/ppermute | solution.py:287
  120.8 0.6 maximum_bitcast_fusion
  121.4 6.6 %collective-permute-done.20 = bf16[64,192]{1,0:T(8,128)(2,1)S(1)} collective-permute-done((bf16[64,192]{1,0:T(8,128)(2,1)S(1)}, bf16[64,192]{1,0:T(8,128)(2,1)S(1)}, u32[]{:S(2)}, u32[]{:S(2)}) %collective-permute-start.20) | collective-permute-done | bytes 24608 | tf_op jit(solution)/shard_map/ppermute | solution.py:287
  128.0 0.6 copy.31
  128.6 0.6 copy.32
  (20 shorter events, 0.1 us)
Async XLA Ops:
  0.6 8.9 %copy-start.2 = (bf16[1,64,192]{2,1,0:T(8,128)(2,1)S(1)}, bf16[1,64,192]{2,1,0:T(8,128)(2,1)}, u32[]{:S(2)}) copy-start(bf16[1,64,192]{2,1,0:T(8,128)(2,1)} %param.26) | copy-start | bytes 73732
  0.6 8.8 %copy-start.5 = (s32[32]{0:T(128)S(1)}, s32[32]{0:T(128)}, u32[]{:S(2)}) copy-start(s32[32]{0:T(128)} %param.35) | copy-start | bytes 388
  0.7 8.9 %copy-start.4 = (bf16[1,64,192]{2,1,0:T(8,128)(2,1)S(1)}, bf16[1,64,192]{2,1,0:T(8,128)(2,1)}, u32[]{:S(2)}) copy-start(bf16[1,64,192]{2,1,0:T(8,128)(2,1)} %param.28) | copy-start | bytes 73732
  0.7 57.3 %copy-start = (f32[1,4608]{1,0:T(1,128)S(1)}, f32[1,4608]{1,0:T(1,128)}, u32[]{:S(2)}) copy-start(f32[1,4608]{1,0:T(1,128)} %gain_ref.3) | copy-start | bytes 55300
  0.7 57.3 %copy-start.1 = (s32[1,2,8]{2,1,0:T(2,128)S(1)}, s32[1,2,8]{2,1,0:T(2,128)}, u32[]{:S(2)}) copy-start(s32[1,2,8]{2,1,0:T(2,128)} %off_ref.3) | copy-start | bytes 196
  2.4 25.4 %all-to-all-start.1 = ((bf16[8,64,384]{2,1,0:T(8,128)(2,1)}), bf16[8,64,384]{2,1,0:T(8,128)(2,1)S(1)}, u32[]{:S(2)}, u32[]{:S(2)}) async-start(bf16[8,64,384]{2,1,0:T(8,128)(2,1)} %broadcast_in_dim.22), calls=%async_computation.1 | async-start | bytes 786432 | tf_op jit(solution)/shard_map/all_to_all | solution.py:307
  9.6 17.3 %collective-permute-start.12 = (bf16[64,384]{1,0:T(8,128)(2,1)S(1)}, bf16[64,384]{1,0:T(8,128)(2,1)}, u32[]{:S(2)}, u32[]{:S(2)}) collective-permute-start(bf16[64,384]{1,0:T(8,128)(2,1)S(1)} %param.12), channel_id=1, source_target_pairs={{0,672},{24,696},{48,720},{72,744},{96,576},{120,600},{144,624},{1... | collective-permute-start | bytes 147464 | tf_op jit(solution)/shard_map/cond/branch_12_fun/ppermute | solution.py:301
  28.4 17.6 %all-to-all-start = ((bf16[8,32,384]{2,1,0:T(8,128)(2,1)}), bf16[8,32,384]{2,1,0:T(8,128)(2,1)S(1)}, u32[]{:S(2)}, u32[]{:S(2)}) async-start(bf16[8,32,384]{2,1,0:T(8,128)(2,1)} %broadcast_in_dim.10), calls=%async_computation | async-start | bytes 393216 | tf_op jit(solution)/shard_map/all_to_all | solution.py:307
  36.3 15.6 %collective-permute-start.18 = (bf16[8,64,384]{2,1,0:T(8,128)(2,1)S(1)}, bf16[8,64,384]{2,1,0:T(8,128)(2,1)S(1)}, u32[]{:S(2)}, u32[]{:S(2)}) collective-permute-start(bf16[8,64,384]{2,1,0:T(8,128)(2,1)S(1)} %all-to-all-done.1.own_ref), channel_id=1, source_target_pairs={{0,1},{1,2},{2,0},{3,4},{4,5},{5,3},{6,7},{7,8},{8,6},{9,10},{10,1... | collective-permute-start | bytes 1179656 | tf_op jit(solution)/shard_map/ppermute | solution.py:292
  38.6 19.3 %collective-permute-start.19 = (bf16[8,64,384]{2,1,0:T(8,128)(2,1)S(1)}, bf16[8,64,384]{2,1,0:T(8,128)(2,1)S(1)}, u32[]{:S(2)}, u32[]{:S(2)}) collective-permute-start(bf16[8,64,384]{2,1,0:T(8,128)(2,1)S(1)} %all-to-all-done.1.own_ref), channel_id=1, source_target_pairs={{0,2},{1,0},{2,1},{3,5},{4,3},{5,4},{6,8},{7,6},{8,7},{9,11},{10,9... | collective-permute-start | bytes 1179656 | tf_op jit(solution)/shard_map/ppermute | solution.py:292
  46.0 16.1 %collective-permute-start.16 = (bf16[8,32,384]{2,1,0:T(8,128)(2,1)S(1)}, bf16[8,32,384]{2,1,0:T(8,128)(2,1)S(1)}, u32[]{:S(2)}, u32[]{:S(2)}) collective-permute-start(bf16[8,32,384]{2,1,0:T(8,128)(2,1)S(1)} %all-to-all-done.own_ref), channel_id=1, source_target_pairs={{0,1},{1,2},{2,0},{3,4},{4,5},{5,3},{6,7},{7,8},{8,6},{9,10},{10,1... | collective-permute-start | bytes 589832 | tf_op jit(solution)/shard_map/ppermute | solution.py:292
  48.4 15.1 %collective-permute-start.17 = (bf16[8,32,384]{2,1,0:T(8,128)(2,1)S(1)}, bf16[8,32,384]{2,1,0:T(8,128)(2,1)S(1)}, u32[]{:S(2)}, u32[]{:S(2)}) collective-permute-start(bf16[8,32,384]{2,1,0:T(8,128)(2,1)S(1)} %all-to-all-done.own_ref), channel_id=1, source_target_pairs={{0,2},{1,0},{2,1},{3,5},{4,3},{5,4},{6,8},{7,6},{8,7},{9,11},{10,9... | collective-permute-start | bytes 589832 | tf_op jit(solution)/shard_map/ppermute | solution.py:292
  69.1 9.4 %copy-start.3 = (bf16[1,64,192]{2,1,0:T(8,128)(2,1)S(1)}, bf16[1,64,192]{2,1,0:T(8,128)(2,1)}, u32[]{:S(2)}) copy-start(bf16[1,64,192]{2,1,0:T(8,128)(2,1)} %param.27) | copy-start | bytes 73732
  69.1 37.2 %all-to-all-start.2 = ((bf16[24,64,384]{2,1,0:T(8,128)(2,1)}), bf16[24,64,384]{2,1,0:T(8,128)(2,1)S(1)}, u32[]{:S(2)}, u32[]{:S(2)}) async-start(bf16[24,64,384]{2,1,0:T(8,128)(2,1)} %shard_map.122), calls=%async_computation.2 | async-start | bytes 2359296 | tf_op jit(solution)/shard_map/all_to_all | solution.py:307
  106.7 14.8 %collective-permute-start.21 = (bf16[64,192]{1,0:T(8,128)(2,1)S(1)}, bf16[64,192]{1,0:T(8,128)(2,1)S(1)}, u32[]{:S(2)}, u32[]{:S(2)}) collective-permute-start(bf16[64,192]{1,0:T(8,128)(2,1)S(1)} %pad_maximum_fusion.2), channel_id=1, source_target_pairs={{24,0},{48,24},{72,48},{96,72},{120,96},{144,120},{168,144},{192,1... | collective-permute-start | bytes 73736 | tf_op jit(solution)/shard_map/ppermute | solution.py:287
  118.9 9.1 %collective-permute-start.20 = (bf16[64,192]{1,0:T(8,128)(2,1)S(1)}, bf16[64,192]{1,0:T(8,128)(2,1)S(1)}, u32[]{:S(2)}, u32[]{:S(2)}) collective-permute-start(bf16[64,192]{1,0:T(8,128)(2,1)S(1)} %pad_maximum_fusion.1), channel_id=1, source_target_pairs={{0,24},{24,48},{48,72},{72,96},{96,120},{120,144},{144,168},{168,1... | collective-permute-start | bytes 73736 | tf_op jit(solution)/shard_map/ppermute | solution.py:287

commit v7 on v5

--- a/solution.py
+++ b/solution.py
@@ -90,10 +90,10 @@
     wo_hbm,
     term_ref,
     dctx_ref,
+    wq_ref,
     blocks,
     xs,
     gs,
-    wq_ref,
     wk_ref,
     wv_ref,
     wo_ref,
@@ -144,37 +144,31 @@
 
 def backward_kernel(
     off_ref,
-    own_ref,
-    low_ref,
-    high_ref,
+    back_ref,
     forward_ref,
     dctx_ref,
     gain_ref,
-    wq_hbm,
+    wq_ref,
     wk_hbm,
     wv_hbm,
     term_ref,
-    blocks,
     xs,
     ns,
     ds,
-    wq_ref,
     wk_ref,
     wv_ref,
     sems,
 ):
-    wq_in, wk_in, wv_in = fetches((wq_hbm, wk_hbm, wv_hbm), (wq_ref, wk_ref, wv_ref), sems)
+    wk_in, wv_in = fetches((wk_hbm, wv_hbm), (wk_ref, wv_ref), sems)
     term_ref[:, : forward_ref.shape[1], :] = forward_ref[...]
-    gathered(own_ref, low_ref, high_ref, blocks)
-    runs, lines, half, wide = blocks.shape
-    parts = runs * lines
+    parts, half, wide = back_ref.shape
     share = wide // 2
     rows = half * 2
     width = parts * share
     squares = jnp.zeros((rows, wide), F32)
     for u in range(parts // 2):
-        a = blocks[(2 * u) % runs, (2 * u) // runs]
-        b = blocks[(2 * u + 1) % runs, (2 * u + 1) // runs]
+        a = back_ref[2 * u]
+        b = back_ref[2 * u + 1]
         span = slice(wide * u, wide * (u + 1))
         x = jnp.concatenate(
             [
@@ -191,7 +185,6 @@
         span = slice(wide * u, wide * (u + 1))
         ns[:, span] = (xs[:, span].astype(F32) * inverse * gain_ref[:, span]).astype(BF16)
     normed = ns[...]
-    arrive(wq_in)
     queries = dot(normed, wq_ref[...]).astype(BF16)
     arrive(wk_in)
     keys = dot(normed, wk_ref[...]).astype(BF16)
@@ -223,23 +216,21 @@
         term_ref[2 * u + 1, half:, :] = jnp.concatenate([out[:half, share:], out[half:, share:]], axis=1)
 
 
-def kernel_call(body, outs, scratch, offsets, args, weights):
+def kernel_call(body, outs, scratch, offsets, args, weights=()):
     vmem = pl.BlockSpec(memory_space=pltpu.VMEM)
     specs = [pl.BlockSpec(memory_space=pltpu.SMEM)] + [vmem] * len(args)
     specs += [pl.BlockSpec(memory_space=pltpu.HBM)] * len(weights)
-    scratch = scratch + [pltpu.VMEM(w.shape, w.dtype) for w in weights]
-    scratch.append(pltpu.SemaphoreType.DMA((len(weights), PIECES)))
     return pl.pallas_call(
         body,
         out_shape=outs,
         in_specs=specs,
-        out_specs=jax.tree.map(lambda _: vmem, outs),
+        out_specs=tuple(vmem for _ in outs),
         scratch_shapes=scratch,
         compiler_params=pltpu.CompilerParams(vmem_limit_bytes=VMEM_LIMIT),
     )(offsets, *args, *[pltpu.with_memory_space_constraint(w, pltpu.HBM) for w in weights])
 
 
-PIECES = 2
+PIECES = 4
 VMEM_LIMIT = 16 * 2**20
 
 
@@ -250,27 +241,30 @@
     outs = (
         jax.ShapeDtypeStruct((runs * lines, rows // 2, wide), BF16),
         jax.ShapeDtypeStruct((rows, wo.shape[0]), BF16),
+        pltpu.VMEM(wq.shape, wq.dtype),
     )
     scratch = [
         pltpu.VMEM((runs, lines, rows, wide), BF16),
         pltpu.VMEM((rows, width), BF16),
         pltpu.VMEM((rows, width), BF16),
+        *[pltpu.VMEM(w.shape, w.dtype) for w in (wk, wv, wo)],
+        pltpu.SemaphoreType.DMA((4, PIECES)),
     ]
     return kernel_call(forward_kernel, outs, scratch, offsets, (*blocks, gain), (wq, wk, wv, wo))
 
 
-def both_terms(offsets, blocks, term, dctx, gain, wq, wk, wv):
-    lines, half, wide = blocks[0].shape
+def both_terms(offsets, back, term, dctx, gain, wq, wk, wv):
+    parts, half, wide = back.shape
     width = gain.shape[1]
-    runs = len(blocks)
-    outs = jax.ShapeDtypeStruct((runs * lines, 2 * half, wide), BF16)
+    outs = (jax.ShapeDtypeStruct((parts, 2 * half, wide), BF16),)
     scratch = [
-        pltpu.VMEM((runs, lines, half, wide), BF16),
         pltpu.VMEM((2 * half, width), BF16),
         pltpu.VMEM((2 * half, width), BF16),
         pltpu.VMEM((2 * half, width), F32),
+        *[pltpu.VMEM(w.shape, w.dtype) for w in (wk, wv)],
+        pltpu.SemaphoreType.DMA((2, PIECES)),
     ]
-    return kernel_call(backward_kernel, outs, scratch, offsets, (*blocks, term, dctx, gain), (wq, wk, wv))
+    return kernel_call(backward_kernel, outs, scratch, offsets, (back, term, dctx, gain, wq), (wk, wv))[0]
 
 
 def folded(block):
@@ -315,20 +309,28 @@
 
 
 def spread(block):
-    own = exchanged(jnp.broadcast_to(block[None], (lax.axis_size("line"),) + block.shape), "line")
+    return exchanged(repeated(block, TENSOR), TENSOR)
+
+
+def spread_in_levels(*parts):
+    own = exchanged(repeated(jnp.concatenate(parts, axis=1), "line"), "line")
     return own, around(own, "run", 1), around(own, "run", -1)
+
+
+def repeated(block, axes):
+    return jnp.broadcast_to(block[None], (lax.axis_size(axes),) + block.shape)
 
 
 def local(fwd_input, bwd_grad, parked, norm_gain, w_query, w_key, w_value, w_out, offsets, mirror):
     fwd_rows = fwd_input[0]
     grad_rows = bwd_grad[0]
     half = fwd_rows.shape[0] // 2
-    pair = spread(jnp.concatenate([fwd_rows, grad_rows], axis=1))
+    pair = spread_in_levels(fwd_rows, grad_rows)
     swapped = mirrored(jnp.concatenate([folded(fwd_rows), folded(parked[0])], axis=0), mirror[0])
     back = spread(swapped[half:])
     parked_rows = unfolded(swapped[:half])
-    term, dctx = forward_term(offsets, pair, norm_gain, w_query[0], w_key[0], w_value[0], w_out[0])
-    terms = both_terms(offsets, back, term, dctx, norm_gain, w_query[0], w_key[0], w_value[0])
+    term, dctx, wq = forward_term(offsets, pair, norm_gain, w_query[0], w_key[0], w_value[0], w_out[0])
+    terms = both_terms(offsets, back, term, dctx, norm_gain, wq, w_key[0], w_value[0])
     summed = jnp.sum(exchanged(terms, TENSOR).astype(F32), axis=0)
     layer_out = unfolded((folded(fwd_rows).astype(F32) + summed[:half]).astype(BF16))
     grad_out = unfolded((folded(grad_rows).astype(F32) + summed[half:]).astype(BF16))

time: 132 us -> 133 us (level)
  the two profiles are of different devices: /device:TPU:66 before, /device:TPU:10 now
where the time goes in v7:
time: 133 us; the launch traced here: 132 us
  starting transfers between devices  59.2 us (45%)
  waiting for transfers between devices  54.7 us (41%)
  Pallas kernels  10.9 us (8%)
  local copies, waits for them, and re-layouts  4.61 us (3%)
  other arithmetic  1.86 us (1%)
    all_to_all x3, waiting for transfers between devices, exchanged(): return lax.all_to_all(blocks, axes, 0, 0, tiled=True)  27.3 us
    all_to_all x3, starting transfers between devices, exchanged(): return lax.all_to_all(blocks, axes, 0, 0, tiled=True)  24.5 us
    ppermute x2, waiting for transfers between devices, around(): lax.ppermute(block, axis, [(i, (i + distance) % count) for i in range(cou...  18.7 us
    ppermute x1, starting transfers between devices, swap_by(): return lambda held: lax.ppermute(held, SECTION, route)  16.1 us
    ppermute x2, starting transfers between devices, passed_along(): return lax.ppermute(block, SECTION, route)  11.9 us
    pallas_call x2, Pallas kernels, kernel_call(): pl.pallas_call(body, out_shape=outs, in_specs=specs, out_specs=tuple((vme...  10.9 us
    ppermute x2, starting transfers between devices, around(): lax.ppermute(block, axis, [(i, (i + distance) % count) for i in range(cou...  6.74 us
    ppermute x2, waiting for transfers between devices, passed_along(): return lax.ppermute(block, SECTION, route)  6.61 us
  transfers between devices with their start and end apart: 8, of which 5 were waited for; matrix products, arithmetic and copies ran while one was open for 2% of the time, Pallas kernels for 3%

profile of v7, /device:TPU:10, one launch (start us, length us, event | category | flops | bytes accessed | tf_op | source)
XLA Modules:
  0.0 132.1 jit_solution(7422742974446681578)
XLA Ops:
  0.7 0.9 pad_maximum_fusion
  1.5 0.8 broadcast_in_dim.22
  2.3 7.5 %all-to-all-start.1 = ((bf16[8,64,384]{2,1,0:T(8,128)(2,1)}), bf16[8,64,384]{2,1,0:T(8,128)(2,1)S(1)}, u32[]{:S(2)}, u32[]{:S(2)}) async-start(bf16[8,64,384]{2,1,0:T(8,128)(2,1)} %broadcast_in_dim.22), calls=%async_computation.1 | async-start | bytes 786432 | tf_op jit(solution)/shard_map/all_to_all | solution.py:308
  10.0 0.1 maximum_maximum_fusion
  10.1 18.2 %conditional.1 = (bf16[64,384]{1,0:T(8,128)(2,1)}) conditional(s32[]{:T(128)} %bitcast.2, bf16[64,384]{1,0:T(8,128)(2,1)S(1)} %maximum_maximum_fusion, bf16[64,384]{1,0:T(8,128)(2,1)S(1)} %maximum_maximum_fusion, bf16[64,384]{1,0:T(8,128)(2,1)S(1)} %maximum_maximum_fusion, ...), branch_computations={%region_0.0_spmd, %region_1.0_spmd, %region_2.0_spmd, %region_3.0_... | conditional | bytes 196656 | solution.py:304
  10.1 16.1 %collective-permute-start.12 = (bf16[64,384]{1,0:T(8,128)(2,1)S(1)}, bf16[64,384]{1,0:T(8,128)(2,1)}, u32[]{:S(2)}, u32[]{:S(2)}) collective-permute-start(bf16[64,384]{1,0:T(8,128)(2,1)S(1)} %param.12), channel_id=1, source_target_pairs={{0,672},{24,696},{48,720},{72,744},{96,576},{120,600},{144,624},{1... | collective-permute-start | bytes 147464 | tf_op jit(solution)/shard_map/cond/branch_12_fun/ppermute | solution.py:302
  26.1 2.2 %collective-permute-done.12 = bf16[64,384]{1,0:T(8,128)(2,1)} collective-permute-done((bf16[64,384]{1,0:T(8,128)(2,1)S(1)}, bf16[64,384]{1,0:T(8,128)(2,1)}, u32[]{:S(2)}, u32[]{:S(2)}) %collective-permute-start.12) | collective-permute-done | bytes 49184 | tf_op jit(solution)/shard_map/cond/branch_12_fun/ppermute | solution.py:302
  28.3 0.7 slice.93
  29.0 0.0 all-to-all-done.1.own_ref
  29.0 0.9 broadcast_in_dim.10
  29.9 8.8 %all-to-all-start = ((bf16[24,32,384]{2,1,0:T(8,128)(2,1)}), bf16[24,32,384]{2,1,0:T(8,128)(2,1)S(1)}, u32[]{:S(2)}, u32[]{:S(2)}) async-start(bf16[24,32,384]{2,1,0:T(8,128)(2,1)} %broadcast_in_dim.10), calls=%async_computation | async-start | bytes 1179648 | tf_op jit(solution)/shard_map/all_to_all | solution.py:308
  38.7 3.4 %collective-permute-start.16 = (bf16[8,64,384]{2,1,0:T(8,128)(2,1)S(1)}, bf16[8,64,384]{2,1,0:T(8,128)(2,1)S(1)}, u32[]{:S(2)}, u32[]{:S(2)}) collective-permute-start(bf16[8,64,384]{2,1,0:T(8,128)(2,1)S(1)} %all-to-all-done.1.own_ref), channel_id=1, source_target_pairs={{0,1},{1,2},{2,0},{3,4},{4,5},{5,3},{6,7},{7,8},{8,6},{9,10},{10,1... | collective-permute-start | bytes 1179656 | tf_op jit(solution)/shard_map/ppermute | solution.py:293
  42.1 3.4 %collective-permute-start.17 = (bf16[8,64,384]{2,1,0:T(8,128)(2,1)S(1)}, bf16[8,64,384]{2,1,0:T(8,128)(2,1)S(1)}, u32[]{:S(2)}, u32[]{:S(2)}) collective-permute-start(bf16[8,64,384]{2,1,0:T(8,128)(2,1)S(1)} %all-to-all-done.1.own_ref), channel_id=1, source_target_pairs={{0,2},{1,0},{2,1},{3,5},{4,3},{5,4},{6,8},{7,6},{8,7},{9,11},{10,9... | collective-permute-start | bytes 1179656 | tf_op jit(solution)/shard_map/ppermute | solution.py:293
  45.5 14.2 %collective-permute-done.16.low_ref = bf16[8,64,384]{2,1,0:T(8,128)(2,1)S(1)} collective-permute-done((bf16[8,64,384]{2,1,0:T(8,128)(2,1)S(1)}, bf16[8,64,384]{2,1,0:T(8,128)(2,1)S(1)}, u32[]{:S(2)}, u32[]{:S(2)}) %collective-permute-start.16) | collective-permute-done | bytes 393248 | tf_op jit(solution)/shard_map/ppermute | solution.py:293
  59.7 4.5 %collective-permute-done.17.high_ref = bf16[8,64,384]{2,1,0:T(8,128)(2,1)S(1)} collective-permute-done((bf16[8,64,384]{2,1,0:T(8,128)(2,1)S(1)}, bf16[8,64,384]{2,1,0:T(8,128)(2,1)S(1)}, u32[]{:S(2)}, u32[]{:S(2)}) %collective-permute-start.17) | collective-permute-done | bytes 393248 | tf_op jit(solution)/shard_map/ppermute | solution.py:293
  64.2 4.2 %shard_map.121 = (bf16[24,32,384]{2,1,0:T(8,128)(2,1)S(1)}, bf16[64,128]{1,0:T(8,128)(2,1)S(1)}, bf16[4608,128]{1,0:T(8,128)(2,1)S(1)}) custom-call(s32[1,2,8]{2,1,0:T(2,128)S(1)} %copy-done.1, bf16[8,64,384]{2,1,0:T(8,128)(2,1)S(1)} %all-to-all-done.1.own_ref, bf16[8,64,384]{2,1,0:T(8,128)(2,1)S(1)} %collective-permute-done.16.low_ref, ...), custom_call_target="tpu_custom_call" | custom-call | tf_op jit(solution)/shard_map/pallas_call | solution.py:223
  68.4 0.0 all-to-all-done.back_ref
  68.4 6.7 %shard_map.122 = bf16[24,64,384]{2,1,0:T(8,128)(2,1)} custom-call(s32[1,2,8]{2,1,0:T(2,128)S(1)} %copy-done.1, bf16[24,32,384]{2,1,0:T(8,128)(2,1)S(1)} %all-to-all-done.back_ref, bf16[24,32,384]{2,1,0:T(8,128)(2,1)S(1)} %get-tuple-element.39.forward_ref, bf16[64,128]{1,0:T(8,128)(2,1)S(1)} %get-tuple-element.40.dctx_ref, f32[1,4608]{1,0:T(1,128)S(1)} %copy-done, ...), custom_call_target="tpu_custom_call" | custom-call | tf_op jit(solution)/shard_map/pallas_call | solution.py:223
  75.1 0.0 copy-start.3
  75.1 8.1 %all-to-all-start.2 = ((bf16[24,64,384]{2,1,0:T(8,128)(2,1)}), bf16[24,64,384]{2,1,0:T(8,128)(2,1)S(1)}, u32[]{:S(2)}, u32[]{:S(2)}) async-start(bf16[24,64,384]{2,1,0:T(8,128)(2,1)} %shard_map.122), calls=%async_computation.2 | async-start | bytes 2359296 | tf_op jit(solution)/shard_map/all_to_all | solution.py:308
  83.3 0.9 fusion.2
  84.1 27.3 %all-to-all-done.2 = bf16[24,64,384]{2,1,0:T(8,128)(2,1)S(1)} async-done(((bf16[24,64,384]{2,1,0:T(8,128)(2,1)}), bf16[24,64,384]{2,1,0:T(8,128)(2,1)S(1)}, u32[]{:S(2)}, u32[]{:S(2)}) %all-to-all-start.2) | async-done | bytes 1179680 | tf_op jit(solution)/shard_map/all_to_all | solution.py:308
  111.4 0.2 convert_reduce_fusion
  111.6 0.1 fusion
  111.7 0.1 fusion.3
  111.8 9.9 %collective-permute-start.19 = (bf16[64,192]{1,0:T(8,128)(2,1)S(1)}, bf16[64,192]{1,0:T(8,128)(2,1)S(1)}, u32[]{:S(2)}, u32[]{:S(2)}) collective-permute-start(bf16[64,192]{1,0:T(8,128)(2,1)S(1)} %pad_maximum_fusion.2), channel_id=1, source_target_pairs={{24,0},{48,24},{72,48},{96,72},{120,96},{144,120},{168,144},{192,1... | collective-permute-start | bytes 73736 | tf_op jit(solution)/shard_map/ppermute | solution.py:288
  121.7 1.9 %collective-permute-start.18 = (bf16[64,192]{1,0:T(8,128)(2,1)S(1)}, bf16[64,192]{1,0:T(8,128)(2,1)S(1)}, u32[]{:S(2)}, u32[]{:S(2)}) collective-permute-start(bf16[64,192]{1,0:T(8,128)(2,1)S(1)} %pad_maximum_fusion.1), channel_id=1, source_target_pairs={{0,24},{24,48},{48,72},{72,96},{96,120},{120,144},{144,168},{168,1... | collective-permute-start | bytes 73736 | tf_op jit(solution)/shard_map/ppermute | solution.py:288
  123.7 0.6 maximum_bitcast_fusion
  124.3 0.0 collective-permute-done.19
  124.3 6.6 %collective-permute-done.18 = bf16[64,192]{1,0:T(8,128)(2,1)S(1)} collective-permute-done((bf16[64,192]{1,0:T(8,128)(2,1)S(1)}, bf16[64,192]{1,0:T(8,128)(2,1)S(1)}, u32[]{:S(2)}, u32[]{:S(2)}) %collective-permute-start.18) | collective-permute-done | bytes 24608 | tf_op jit(solution)/shard_map/ppermute | solution.py:288
  130.9 0.6 copy.31
  131.5 0.6 copy.32
  (16 shorter events, 0.1 us)
Async XLA Ops:
  0.6 9.3 %copy-start.2 = (bf16[1,64,192]{2,1,0:T(8,128)(2,1)S(1)}, bf16[1,64,192]{2,1,0:T(8,128)(2,1)}, u32[]{:S(2)}) copy-start(bf16[1,64,192]{2,1,0:T(8,128)(2,1)} %param.26) | copy-start | bytes 73732
  0.6 9.2 %copy-start.5 = (s32[32]{0:T(128)S(1)}, s32[32]{0:T(128)}, u32[]{:S(2)}) copy-start(s32[32]{0:T(128)} %param.35) | copy-start | bytes 388
  0.7 9.3 %copy-start.4 = (bf16[1,64,192]{2,1,0:T(8,128)(2,1)S(1)}, bf16[1,64,192]{2,1,0:T(8,128)(2,1)}, u32[]{:S(2)}) copy-start(bf16[1,64,192]{2,1,0:T(8,128)(2,1)} %param.28) | copy-start | bytes 73732
  2.3 26.7 %all-to-all-start.1 = ((bf16[8,64,384]{2,1,0:T(8,128)(2,1)}), bf16[8,64,384]{2,1,0:T(8,128)(2,1)S(1)}, u32[]{:S(2)}, u32[]{:S(2)}) async-start(bf16[8,64,384]{2,1,0:T(8,128)(2,1)} %broadcast_in_dim.22), calls=%async_computation.1 | async-start | bytes 786432 | tf_op jit(solution)/shard_map/all_to_all | solution.py:308
  9.9 54.3 %copy-start = (f32[1,4608]{1,0:T(1,128)S(1)}, f32[1,4608]{1,0:T(1,128)}, u32[]{:S(2)}) copy-start(f32[1,4608]{1,0:T(1,128)} %gain_ref.3) | copy-start | bytes 55300
  9.9 54.3 %copy-start.1 = (s32[1,2,8]{2,1,0:T(2,128)S(1)}, s32[1,2,8]{2,1,0:T(2,128)}, u32[]{:S(2)}) copy-start(s32[1,2,8]{2,1,0:T(2,128)} %off_ref.3) | copy-start | bytes 196
  10.1 18.2 %collective-permute-start.12 = (bf16[64,384]{1,0:T(8,128)(2,1)S(1)}, bf16[64,384]{1,0:T(8,128)(2,1)}, u32[]{:S(2)}, u32[]{:S(2)}) collective-permute-start(bf16[64,384]{1,0:T(8,128)(2,1)S(1)} %param.12), channel_id=1, source_target_pairs={{0,672},{24,696},{48,720},{72,744},{96,576},{120,600},{144,624},{1... | collective-permute-start | bytes 147464 | tf_op jit(solution)/shard_map/cond/branch_12_fun/ppermute | solution.py:302
  29.9 38.5 %all-to-all-start = ((bf16[24,32,384]{2,1,0:T(8,128)(2,1)}), bf16[24,32,384]{2,1,0:T(8,128)(2,1)S(1)}, u32[]{:S(2)}, u32[]{:S(2)}) async-start(bf16[24,32,384]{2,1,0:T(8,128)(2,1)} %broadcast_in_dim.10), calls=%async_computation | async-start | bytes 1179648 | tf_op jit(solution)/shard_map/all_to_all | solution.py:308
  38.7 21.0 %collective-permute-start.16 = (bf16[8,64,384]{2,1,0:T(8,128)(2,1)S(1)}, bf16[8,64,384]{2,1,0:T(8,128)(2,1)S(1)}, u32[]{:S(2)}, u32[]{:S(2)}) collective-permute-start(bf16[8,64,384]{2,1,0:T(8,128)(2,1)S(1)} %all-to-all-done.1.own_ref), channel_id=1, source_target_pairs={{0,1},{1,2},{2,0},{3,4},{4,5},{5,3},{6,7},{7,8},{8,6},{9,10},{10,1... | collective-permute-start | bytes 1179656 | tf_op jit(solution)/shard_map/ppermute | solution.py:293
  42.1 22.1 %collective-permute-start.17 = (bf16[8,64,384]{2,1,0:T(8,128)(2,1)S(1)}, bf16[8,64,384]{2,1,0:T(8,128)(2,1)S(1)}, u32[]{:S(2)}, u32[]{:S(2)}) collective-permute-start(bf16[8,64,384]{2,1,0:T(8,128)(2,1)S(1)} %all-to-all-done.1.own_ref), channel_id=1, source_target_pairs={{0,2},{1,0},{2,1},{3,5},{4,3},{5,4},{6,8},{7,6},{8,7},{9,11},{10,9... | collective-permute-start | bytes 1179656 | tf_op jit(solution)/shard_map/ppermute | solution.py:293
  75.1 8.2 %copy-start.3 = (bf16[1,64,192]{2,1,0:T(8,128)(2,1)S(1)}, bf16[1,64,192]{2,1,0:T(8,128)(2,1)}, u32[]{:S(2)}) copy-start(bf16[1,64,192]{2,1,0:T(8,128)(2,1)} %param.27) | copy-start | bytes 73732
  75.1 36.3 %all-to-all-start.2 = ((bf16[24,64,384]{2,1,0:T(8,128)(2,1)}), bf16[24,64,384]{2,1,0:T(8,128)(2,1)S(1)}, u32[]{:S(2)}, u32[]{:S(2)}) async-start(bf16[24,64,384]{2,1,0:T(8,128)(2,1)} %shard_map.122), calls=%async_computation.2 | async-start | bytes 2359296 | tf_op jit(solution)/shard_map/all_to_all | solution.py:308
  111.8 12.5 %collective-permute-start.19 = (bf16[64,192]{1,0:T(8,128)(2,1)S(1)}, bf16[64,192]{1,0:T(8,128)(2,1)S(1)}, u32[]{:S(2)}, u32[]{:S(2)}) collective-permute-start(bf16[64,192]{1,0:T(8,128)(2,1)S(1)} %pad_maximum_fusion.2), channel_id=1, source_target_pairs={{24,0},{48,24},{72,48},{96,72},{120,96},{144,120},{168,144},{192,1... | collective-permute-start | bytes 73736 | tf_op jit(solution)/shard_map/ppermute | solution.py:288
  121.7 9.2 %collective-permute-start.18 = (bf16[64,192]{1,0:T(8,128)(2,1)S(1)}, bf16[64,192]{1,0:T(8,128)(2,1)S(1)}, u32[]{:S(2)}, u32[]{:S(2)}) collective-permute-start(bf16[64,192]{1,0:T(8,128)(2,1)S(1)} %pad_maximum_fusion.1), channel_id=1, source_target_pairs={{0,24},{24,48},{48,72},{72,96},{96,120},{120,144},{144,168},{168,1... | collective-permute-start | bytes 73736 | tf_op jit(solution)/shard_map/ppermute | solution.py:288

commit v8 on v6

--- a/solution.py
+++ b/solution.py
@@ -144,9 +144,7 @@
 
 def backward_kernel(
     off_ref,
-    own_ref,
-    low_ref,
-    high_ref,
+    columns_ref,
     forward_ref,
     dctx_ref,
     gain_ref,
@@ -160,8 +158,8 @@
     ds,
 ):
     term_ref[:, : forward_ref.shape[1], :] = forward_ref[...]
-    gathered(own_ref, low_ref, high_ref, blocks)
     runs, lines, half, wide = blocks.shape
+    gathered(*[columns_ref.at[:, pl.ds(half * i, half), :] for i in range(runs)], blocks)
     parts = runs * lines
     share = wide // 2
     rows = half * 2
@@ -252,10 +250,11 @@
     return kernel_call(forward_kernel, outs, scratch, offsets, (*blocks, gain), (wq, wk, wv, wo))
 
 
-def both_terms(offsets, blocks, term, dctx, gain, wq, wk, wv):
-    lines, half, wide = blocks[0].shape
+def both_terms(offsets, columns, term, dctx, gain, wq, wk, wv):
+    lines, rows, wide = columns.shape
+    half = rows // RUN
+    runs = RUN
     width = gain.shape[1]
-    runs = len(blocks)
     outs = (jax.ShapeDtypeStruct((runs * lines, 2 * half, wide), BF16),)
     scratch = [
         pltpu.VMEM((runs, lines, half, wide), BF16),
@@ -263,7 +262,7 @@
         pltpu.VMEM((2 * half, width), BF16),
         pltpu.VMEM((2 * half, width), F32),
     ]
-    return kernel_call(backward_kernel, outs, scratch, offsets, (*blocks, term, dctx, gain, wq, wk, wv))[0]
+    return kernel_call(backward_kernel, outs, scratch, offsets, (columns, term, dctx, gain, wq, wk, wv))[0]
 
 
 def folded(block):
@@ -308,8 +307,17 @@
 
 
 def spread(block):
-    own = exchanged(jnp.broadcast_to(block[None], (lax.axis_size("line"),) + block.shape), "line")
+    own = exchanged(repeated(block), "line")
     return own, around(own, "run", 1), around(own, "run", -1)
+
+
+def spread_columns(block):
+    column = jnp.concatenate([block, around(block, "run", 1), around(block, "run", -1)], axis=0)
+    return exchanged(repeated(column), "line")
+
+
+def repeated(block):
+    return jnp.broadcast_to(block[None], (lax.axis_size("line"),) + block.shape)
 
 
 def local(fwd_input, bwd_grad, parked, norm_gain, w_query, w_key, w_value, w_out, offsets, mirror):
@@ -318,7 +326,7 @@
     half = fwd_rows.shape[0] // 2
     pair = spread(jnp.concatenate([fwd_rows, grad_rows], axis=1))
     swapped = mirrored(jnp.concatenate([folded(fwd_rows), folded(parked[0])], axis=0), mirror[0])
-    back = spread(swapped[half:])
+    back = spread_columns(swapped[half:])
     parked_rows = unfolded(swapped[:half])
     term, dctx, wq, wk, wv = forward_term(offsets, pair, norm_gain, w_query[0], w_key[0], w_value[0], w_out[0])
     terms = both_terms(offsets, back, term, dctx, norm_gain, wq, wk, wv)

time: 130 us -> 137 us (1.054)
  the two profiles are of different devices: /device:TPU:66 before, /device:TPU:1 now
where the time goes in v8:
time: 137 us; the launch traced here: 134 us
  starting transfers between devices  66.4 us (48%)
  waiting for transfers between devices  46.8 us (34%)
  Pallas kernels  9.59 us (7%)
  local copies, waits for them, and re-layouts  8.8 us (6%)
  other arithmetic  1.86 us (1%)
    all_to_all x3, waiting for transfers between devices, exchanged(): return lax.all_to_all(blocks, axes, 0, 0, tiled=True)  28.3 us
    all_to_all x3, starting transfers between devices, exchanged(): return lax.all_to_all(blocks, axes, 0, 0, tiled=True)  20.5 us
    ppermute x1, starting transfers between devices, swap_by(): return lambda held: lax.ppermute(held, SECTION, route)  17.1 us
    ppermute x4, waiting for transfers between devices, around(): lax.ppermute(block, axis, [(i, (i + distance) % count) for i in range(cou...  16.5 us
    ppermute x2, starting transfers between devices, passed_along(): return lax.ppermute(block, SECTION, route)  16.3 us
    ppermute x4, starting transfers between devices, around(): lax.ppermute(block, axis, [(i, (i + distance) % count) for i in range(cou...  12.6 us
    pallas_call x2, Pallas kernels, kernel_call(): pl.pallas_call(body, out_shape=outs, in_specs=specs, out_specs=tuple((vme...  9.59 us
    unnamed x22, local copies, waits for them, and re-layouts  5.43 us
  transfers between devices with their start and end apart: 10, of which 6 were waited for; matrix products, arithmetic and copies ran while one was open for 2% of the time, Pallas kernels for 3%

profile of v8, /device:TPU:1, one launch (start us, length us, event | category | flops | bytes accessed | tf_op | source)
XLA Modules:
  0.0 134.3 jit_solution(10357950515342638957)
XLA Ops:
  0.7 0.9 pad_maximum_fusion.1
  1.5 0.8 broadcast_in_dim.22
  2.3 7.6 %all-to-all-start.1 = ((bf16[8,64,384]{2,1,0:T(8,128)(2,1)}), bf16[8,64,384]{2,1,0:T(8,128)(2,1)S(1)}, u32[]{:S(2)}, u32[]{:S(2)}) async-start(bf16[8,64,384]{2,1,0:T(8,128)(2,1)} %broadcast_in_dim.22), calls=%async_computation.1 | async-start | bytes 786432 | tf_op jit(solution)/shard_map/all_to_all | solution.py:306
  10.2 18.7 %conditional.1 = (bf16[64,384]{1,0:T(8,128)(2,1)}) conditional(s32[]{:T(128)} %bitcast.2, bf16[64,384]{1,0:T(8,128)(2,1)S(1)} %maximum_maximum_fusion, bf16[64,384]{1,0:T(8,128)(2,1)S(1)} %maximum_maximum_fusion, bf16[64,384]{1,0:T(8,128)(2,1)S(1)} %maximum_maximum_fusion, ...), branch_computations={%region_0.0_spmd, %region_1.0_spmd, %region_2.0_spmd, %region_3.0_... | conditional | bytes 196656 | solution.py:302
  10.2 17.1 %collective-permute-start.12 = (bf16[64,384]{1,0:T(8,128)(2,1)S(1)}, bf16[64,384]{1,0:T(8,128)(2,1)}, u32[]{:S(2)}, u32[]{:S(2)}) collective-permute-start(bf16[64,384]{1,0:T(8,128)(2,1)S(1)} %param.12), channel_id=1, source_target_pairs={{0,672},{24,696},{48,720},{72,744},{96,576},{120,600},{144,624},{1... | collective-permute-start | bytes 147464 | tf_op jit(solution)/shard_map/cond/branch_12_fun/ppermute | solution.py:300
  27.2 1.6 %collective-permute-done.12 = bf16[64,384]{1,0:T(8,128)(2,1)} collective-permute-done((bf16[64,384]{1,0:T(8,128)(2,1)S(1)}, bf16[64,384]{1,0:T(8,128)(2,1)}, u32[]{:S(2)}, u32[]{:S(2)}) %collective-permute-start.12) | collective-permute-done | bytes 49184 | tf_op jit(solution)/shard_map/cond/branch_12_fun/ppermute | solution.py:300
  28.8 0.7 slice.93
  29.6 3.0 %collective-permute-start.16 = (bf16[32,384]{1,0:T(8,128)(2,1)S(1)}, bf16[32,384]{1,0:T(8,128)(2,1)S(1)}, u32[]{:S(2)}, u32[]{:S(2)}) collective-permute-start(bf16[32,384]{1,0:T(8,128)(2,1)S(1)} %slice.93), channel_id=1, source_target_pairs={{0,1},{1,2},{2,0},{3,4},{4,5},{5,3},{6,7},{7,8},{8,6},{9,10},{10,1... | collective-permute-start | bytes 73736 | tf_op jit(solution)/shard_map/ppermute | solution.py:291
  32.6 3.4 %collective-permute-start.17 = (bf16[32,384]{1,0:T(8,128)(2,1)S(1)}, bf16[32,384]{1,0:T(8,128)(2,1)S(1)}, u32[]{:S(2)}, u32[]{:S(2)}) collective-permute-start(bf16[32,384]{1,0:T(8,128)(2,1)S(1)} %slice.93), channel_id=1, source_target_pairs={{0,2},{1,0},{2,1},{3,5},{4,3},{5,4},{6,8},{7,6},{8,7},{9,11},{10,9... | collective-permute-start | bytes 73736 | tf_op jit(solution)/shard_map/ppermute | solution.py:291
  36.0 1.8 %collective-permute-done.17 = bf16[32,384]{1,0:T(8,128)(2,1)S(1)} collective-permute-done((bf16[32,384]{1,0:T(8,128)(2,1)S(1)}, bf16[32,384]{1,0:T(8,128)(2,1)S(1)}, u32[]{:S(2)}, u32[]{:S(2)}) %collective-permute-start.17) | collective-permute-done | bytes 24608 | tf_op jit(solution)/shard_map/ppermute | solution.py:291
  37.8 0.9 broadcast_in_dim.10
  38.7 6.1 %all-to-all-start = ((bf16[8,96,384]{2,1,0:T(8,128)(2,1)}), bf16[8,96,384]{2,1,0:T(8,128)(2,1)S(1)}, u32[]{:S(2)}, u32[]{:S(2)}) async-start(bf16[8,96,384]{2,1,0:T(8,128)(2,1)} %broadcast_in_dim.10), calls=%async_computation | async-start | bytes 1179648 | tf_op jit(solution)/shard_map/all_to_all | solution.py:306
  44.7 3.5 %collective-permute-start.18 = (bf16[8,64,384]{2,1,0:T(8,128)(2,1)S(1)}, bf16[8,64,384]{2,1,0:T(8,128)(2,1)S(1)}, u32[]{:S(2)}, u32[]{:S(2)}) collective-permute-start(bf16[8,64,384]{2,1,0:T(8,128)(2,1)S(1)} %all-to-all-done.1.own_ref), channel_id=1, source_target_pairs={{0,1},{1,2},{2,0},{3,4},{4,5},{5,3},{6,7},{7,8},{8,6},{9,10},{10,1... | collective-permute-start | bytes 1179656 | tf_op jit(solution)/shard_map/ppermute | solution.py:291
  48.3 2.7 %collective-permute-start.19 = (bf16[8,64,384]{2,1,0:T(8,128)(2,1)S(1)}, bf16[8,64,384]{2,1,0:T(8,128)(2,1)S(1)}, u32[]{:S(2)}, u32[]{:S(2)}) collective-permute-start(bf16[8,64,384]{2,1,0:T(8,128)(2,1)S(1)} %all-to-all-done.1.own_ref), channel_id=1, source_target_pairs={{0,2},{1,0},{2,1},{3,5},{4,3},{5,4},{6,8},{7,6},{8,7},{9,11},{10,9... | collective-permute-start | bytes 1179656 | tf_op jit(solution)/shard_map/ppermute | solution.py:291
  50.9 3.5 %collective-permute-done.18.low_ref = bf16[8,64,384]{2,1,0:T(8,128)(2,1)S(1)} collective-permute-done((bf16[8,64,384]{2,1,0:T(8,128)(2,1)S(1)}, bf16[8,64,384]{2,1,0:T(8,128)(2,1)S(1)}, u32[]{:S(2)}, u32[]{:S(2)}) %collective-permute-start.18) | collective-permute-done | bytes 393248 | tf_op jit(solution)/shard_map/ppermute | solution.py:291
  54.5 11.2 %collective-permute-done.19.high_ref = bf16[8,64,384]{2,1,0:T(8,128)(2,1)S(1)} collective-permute-done((bf16[8,64,384]{2,1,0:T(8,128)(2,1)S(1)}, bf16[8,64,384]{2,1,0:T(8,128)(2,1)S(1)}, u32[]{:S(2)}, u32[]{:S(2)}) %collective-permute-start.19) | collective-permute-done | bytes 393248 | tf_op jit(solution)/shard_map/ppermute | solution.py:291
  65.6 4.1 %shard_map.121 = (bf16[24,32,384]{2,1,0:T(8,128)(2,1)S(1)}, bf16[64,128]{1,0:T(8,128)(2,1)S(1)}, bf16[4608,128]{1,0:T(8,128)(2,1)S(1)}, bf16[4608,128]{1,0:T(8,128)(2,1)S(1)}, bf16[4608,128]{1,0:T(8,128)(2,1)S(1)}) custom-call(s32[1,2,8]{2,1,0:T(2,128)S(1)} %copy-done.5, bf16[8,64,384]{2,1,0:T(8,128)(2,1)S(1)} %all-to-all-done.1.own_ref, ...), custom_call_target="tpu_custom_call" | custom-call | tf_op jit(solution)/shard_map/pallas_call | solution.py:220
  69.8 1.0 copy-done
  70.8 0.8 copy-done.2
  71.6 1.3 copy-done.1
  72.9 1.1 copy-done.3
  74.0 5.5 %shard_map.122 = bf16[24,64,384]{2,1,0:T(8,128)(2,1)} custom-call(s32[1,2,8]{2,1,0:T(2,128)S(1)} %copy-done.5, bf16[8,96,384]{2,1,0:T(8,128)(2,1)S(1)} %all-to-all-done.columns_ref, bf16[24,32,384]{2,1,0:T(8,128)(2,1)S(1)} %copy-done.3, bf16[64,128]{1,0:T(8,128)(2,1)S(1)} %get-tuple-element.42.dctx_ref, f32[1,4608]{1,0:T(1,128)S(1)} %copy-done.4, ...), custom_call_target="tpu_custom_call" | custom-call | tf_op jit(solution)/shard_map/pallas_call | solution.py:220
  79.4 6.8 %all-to-all-start.2 = ((bf16[24,64,384]{2,1,0:T(8,128)(2,1)}), bf16[24,64,384]{2,1,0:T(8,128)(2,1)S(1)}, u32[]{:S(2)}, u32[]{:S(2)}) async-start(bf16[24,64,384]{2,1,0:T(8,128)(2,1)} %shard_map.122), calls=%async_computation.2 | async-start | bytes 2359296 | tf_op jit(solution)/shard_map/all_to_all | solution.py:306
  86.2 0.9 fusion.2
  87.1 28.3 %all-to-all-done.2 = bf16[24,64,384]{2,1,0:T(8,128)(2,1)S(1)} async-done(((bf16[24,64,384]{2,1,0:T(8,128)(2,1)}), bf16[24,64,384]{2,1,0:T(8,128)(2,1)S(1)}, u32[]{:S(2)}, u32[]{:S(2)}) %all-to-all-start.2) | async-done | bytes 1179680 | tf_op jit(solution)/shard_map/all_to_all | solution.py:306
  115.4 0.2 convert_reduce_fusion
  115.7 4.5 %collective-permute-start.21 = (bf16[64,192]{1,0:T(8,128)(2,1)S(1)}, bf16[64,192]{1,0:T(8,128)(2,1)S(1)}, u32[]{:S(2)}, u32[]{:S(2)}) collective-permute-start(bf16[64,192]{1,0:T(8,128)(2,1)S(1)} %pad_maximum_fusion.3), channel_id=1, source_target_pairs={{24,0},{48,24},{72,48},{96,72},{120,96},{144,120},{168,144},{192,1... | collective-permute-start | bytes 73736 | tf_op jit(solution)/shard_map/ppermute | solution.py:286
  120.2 11.8 %collective-permute-start.20 = (bf16[64,192]{1,0:T(8,128)(2,1)S(1)}, bf16[64,192]{1,0:T(8,128)(2,1)S(1)}, u32[]{:S(2)}, u32[]{:S(2)}) collective-permute-start(bf16[64,192]{1,0:T(8,128)(2,1)S(1)} %pad_maximum_fusion.2), channel_id=1, source_target_pairs={{0,24},{24,48},{48,72},{72,96},{96,120},{120,144},{144,168},{168,1... | collective-permute-start | bytes 73736 | tf_op jit(solution)/shard_map/ppermute | solution.py:286
  132.1 0.6 maximum_bitcast_fusion
  132.7 0.4 collective-permute-done.20
  133.1 0.6 copy.31
  133.7 0.6 copy.32
  (29 shorter events, 0.3 us)
Async XLA Ops:
  0.6 9.4 %copy-start.6 = (bf16[1,64,192]{2,1,0:T(8,128)(2,1)S(1)}, bf16[1,64,192]{2,1,0:T(8,128)(2,1)}, u32[]{:S(2)}) copy-start(bf16[1,64,192]{2,1,0:T(8,128)(2,1)} %param.26) | copy-start | bytes 73732
  0.6 9.3 %copy-start.9 = (s32[32]{0:T(128)S(1)}, s32[32]{0:T(128)}, u32[]{:S(2)}) copy-start(s32[32]{0:T(128)} %param.35) | copy-start | bytes 388
  0.7 9.4 %copy-start.8 = (bf16[1,64,192]{2,1,0:T(8,128)(2,1)S(1)}, bf16[1,64,192]{2,1,0:T(8,128)(2,1)}, u32[]{:S(2)}) copy-start(bf16[1,64,192]{2,1,0:T(8,128)(2,1)} %param.28) | copy-start | bytes 73732
  2.3 35.5 %all-to-all-start.1 = ((bf16[8,64,384]{2,1,0:T(8,128)(2,1)}), bf16[8,64,384]{2,1,0:T(8,128)(2,1)S(1)}, u32[]{:S(2)}, u32[]{:S(2)}) async-start(bf16[8,64,384]{2,1,0:T(8,128)(2,1)} %broadcast_in_dim.22), calls=%async_computation.1 | async-start | bytes 786432 | tf_op jit(solution)/shard_map/all_to_all | solution.py:306
  10.0 55.7 %copy-start.4 = (f32[1,4608]{1,0:T(1,128)S(1)}, f32[1,4608]{1,0:T(1,128)}, u32[]{:S(2)}) copy-start(f32[1,4608]{1,0:T(1,128)} %gain_ref.3) | copy-start | bytes 55300
  10.0 55.7 %copy-start.5 = (s32[1,2,8]{2,1,0:T(2,128)S(1)}, s32[1,2,8]{2,1,0:T(2,128)}, u32[]{:S(2)}) copy-start(s32[1,2,8]{2,1,0:T(2,128)} %off_ref.3) | copy-start | bytes 196
  10.2 18.7 %collective-permute-start.12 = (bf16[64,384]{1,0:T(8,128)(2,1)S(1)}, bf16[64,384]{1,0:T(8,128)(2,1)}, u32[]{:S(2)}, u32[]{:S(2)}) collective-permute-start(bf16[64,384]{1,0:T(8,128)(2,1)S(1)} %param.12), channel_id=1, source_target_pairs={{0,672},{24,696},{48,720},{72,744},{96,576},{120,600},{144,624},{1... | collective-permute-start | bytes 147464 | tf_op jit(solution)/shard_map/cond/branch_12_fun/ppermute | solution.py:300
  29.6 6.4 %collective-permute-start.16 = (bf16[32,384]{1,0:T(8,128)(2,1)S(1)}, bf16[32,384]{1,0:T(8,128)(2,1)S(1)}, u32[]{:S(2)}, u32[]{:S(2)}) collective-permute-start(bf16[32,384]{1,0:T(8,128)(2,1)S(1)} %slice.93), channel_id=1, source_target_pairs={{0,1},{1,2},{2,0},{3,4},{4,5},{5,3},{6,7},{7,8},{8,6},{9,10},{10,1... | collective-permute-start | bytes 73736 | tf_op jit(solution)/shard_map/ppermute | solution.py:291
  32.6 5.1 %collective-permute-start.17 = (bf16[32,384]{1,0:T(8,128)(2,1)S(1)}, bf16[32,384]{1,0:T(8,128)(2,1)S(1)}, u32[]{:S(2)}, u32[]{:S(2)}) collective-permute-start(bf16[32,384]{1,0:T(8,128)(2,1)S(1)} %slice.93), channel_id=1, source_target_pairs={{0,2},{1,0},{2,1},{3,5},{4,3},{5,4},{6,8},{7,6},{8,7},{9,11},{10,9... | collective-permute-start | bytes 73736 | tf_op jit(solution)/shard_map/ppermute | solution.py:291
  38.7 32.9 %all-to-all-start = ((bf16[8,96,384]{2,1,0:T(8,128)(2,1)}), bf16[8,96,384]{2,1,0:T(8,128)(2,1)S(1)}, u32[]{:S(2)}, u32[]{:S(2)}) async-start(bf16[8,96,384]{2,1,0:T(8,128)(2,1)} %broadcast_in_dim.10), calls=%async_computation | async-start | bytes 1179648 | tf_op jit(solution)/shard_map/all_to_all | solution.py:306
  44.7 9.7 %collective-permute-start.18 = (bf16[8,64,384]{2,1,0:T(8,128)(2,1)S(1)}, bf16[8,64,384]{2,1,0:T(8,128)(2,1)S(1)}, u32[]{:S(2)}, u32[]{:S(2)}) collective-permute-start(bf16[8,64,384]{2,1,0:T(8,128)(2,1)S(1)} %all-to-all-done.1.own_ref), channel_id=1, source_target_pairs={{0,1},{1,2},{2,0},{3,4},{4,5},{5,3},{6,7},{7,8},{8,6},{9,10},{10,1... | collective-permute-start | bytes 1179656 | tf_op jit(solution)/shard_map/ppermute | solution.py:291
  48.3 17.4 %collective-permute-start.19 = (bf16[8,64,384]{2,1,0:T(8,128)(2,1)S(1)}, bf16[8,64,384]{2,1,0:T(8,128)(2,1)S(1)}, u32[]{:S(2)}, u32[]{:S(2)}) collective-permute-start(bf16[8,64,384]{2,1,0:T(8,128)(2,1)S(1)} %all-to-all-done.1.own_ref), channel_id=1, source_target_pairs={{0,2},{1,0},{2,1},{3,5},{4,3},{5,4},{6,8},{7,6},{8,7},{9,11},{10,9... | collective-permute-start | bytes 1179656 | tf_op jit(solution)/shard_map/ppermute | solution.py:291
  69.8 1.0 copy-start
  70.8 0.8 copy-start.2
  71.6 1.3 copy-start.1
  72.9 1.1 copy-start.3
  79.4 6.8 %copy-start.7 = (bf16[1,64,192]{2,1,0:T(8,128)(2,1)S(1)}, bf16[1,64,192]{2,1,0:T(8,128)(2,1)}, u32[]{:S(2)}) copy-start(bf16[1,64,192]{2,1,0:T(8,128)(2,1)} %param.27) | copy-start | bytes 73732
  79.4 36.0 %all-to-all-start.2 = ((bf16[24,64,384]{2,1,0:T(8,128)(2,1)}), bf16[24,64,384]{2,1,0:T(8,128)(2,1)S(1)}, u32[]{:S(2)}, u32[]{:S(2)}) async-start(bf16[24,64,384]{2,1,0:T(8,128)(2,1)} %shard_map.122), calls=%async_computation.2 | async-start | bytes 2359296 | tf_op jit(solution)/shard_map/all_to_all | solution.py:306
  115.7 17.0 %collective-permute-start.21 = (bf16[64,192]{1,0:T(8,128)(2,1)S(1)}, bf16[64,192]{1,0:T(8,128)(2,1)S(1)}, u32[]{:S(2)}, u32[]{:S(2)}) collective-permute-start(bf16[64,192]{1,0:T(8,128)(2,1)S(1)} %pad_maximum_fusion.3), channel_id=1, source_target_pairs={{24,0},{48,24},{72,48},{96,72},{120,96},{144,120},{168,144},{192,1... | collective-permute-start | bytes 73736 | tf_op jit(solution)/shard_map/ppermute | solution.py:286
  120.2 12.9 %collective-permute-start.20 = (bf16[64,192]{1,0:T(8,128)(2,1)S(1)}, bf16[64,192]{1,0:T(8,128)(2,1)S(1)}, u32[]{:S(2)}, u32[]{:S(2)}) collective-permute-start(bf16[64,192]{1,0:T(8,128)(2,1)S(1)} %pad_maximum_fusion.2), channel_id=1, source_target_pairs={{0,24},{24,48},{48,72},{72,96},{96,120},{120,144},{144,168},{168,1... | collective-permute-start | bytes 73736 | tf_op jit(solution)/shard_map/ppermute | solution.py:286

commit v9 on v6

--- a/solution.py
+++ b/solution.py
@@ -147,7 +147,6 @@
     own_ref,
     low_ref,
     high_ref,
-    forward_ref,
     dctx_ref,
     gain_ref,
     wq_ref,
@@ -159,7 +158,6 @@
     ns,
     ds,
 ):
-    term_ref[:, : forward_ref.shape[1], :] = forward_ref[...]
     gathered(own_ref, low_ref, high_ref, blocks)
     runs, lines, half, wide = blocks.shape
     parts = runs * lines
@@ -211,8 +209,8 @@
     for u in range(parts // 2):
         span = slice(wide * u, wide * (u + 1))
         out = (ds[:, span] * inverse - xs[:, span].astype(F32) * factor).astype(BF16)
-        term_ref[2 * u, half:, :] = jnp.concatenate([out[:half, :share], out[half:, :share]], axis=1)
-        term_ref[2 * u + 1, half:, :] = jnp.concatenate([out[:half, share:], out[half:, share:]], axis=1)
+        term_ref[2 * u] = jnp.concatenate([out[:half, :share], out[half:, :share]], axis=1)
+        term_ref[2 * u + 1] = jnp.concatenate([out[:half, share:], out[half:, share:]], axis=1)
 
 
 def kernel_call(body, outs, scratch, offsets, args, weights=()):
@@ -252,18 +250,18 @@
     return kernel_call(forward_kernel, outs, scratch, offsets, (*blocks, gain), (wq, wk, wv, wo))
 
 
-def both_terms(offsets, blocks, term, dctx, gain, wq, wk, wv):
+def backward_term(offsets, blocks, dctx, gain, wq, wk, wv):
     lines, half, wide = blocks[0].shape
     width = gain.shape[1]
     runs = len(blocks)
-    outs = (jax.ShapeDtypeStruct((runs * lines, 2 * half, wide), BF16),)
+    outs = (jax.ShapeDtypeStruct((runs * lines, half, wide), BF16),)
     scratch = [
         pltpu.VMEM((runs, lines, half, wide), BF16),
         pltpu.VMEM((2 * half, width), BF16),
         pltpu.VMEM((2 * half, width), BF16),
         pltpu.VMEM((2 * half, width), F32),
     ]
-    return kernel_call(backward_kernel, outs, scratch, offsets, (*blocks, term, dctx, gain, wq, wk, wv))[0]
+    return kernel_call(backward_kernel, outs, scratch, offsets, (*blocks, dctx, gain, wq, wk, wv))[0]
 
 
 def folded(block):
@@ -310,6 +308,11 @@
 def spread(block):
     own = exchanged(jnp.broadcast_to(block[None], (lax.axis_size("line"),) + block.shape), "line")
     return own, around(own, "run", 1), around(own, "run", -1)
+
+
+def total(rows, terms):
+    summed = jnp.sum(exchanged(terms, TENSOR).astype(F32), axis=0)
+    return unfolded((folded(rows).astype(F32) + summed).astype(BF16))
 
 
 def local(fwd_input, bwd_grad, parked, norm_gain, w_query, w_key, w_value, w_out, offsets, mirror):
@@ -321,11 +324,10 @@
     back = spread(swapped[half:])
     parked_rows = unfolded(swapped[:half])
     term, dctx, wq, wk, wv = forward_term(offsets, pair, norm_gain, w_query[0], w_key[0], w_value[0], w_out[0])
-    terms = both_terms(offsets, back, term, dctx, norm_gain, wq, wk, wv)
-    summed = jnp.sum(exchanged(terms, TENSOR).astype(F32), axis=0)
-    layer_out = unfolded((folded(fwd_rows).astype(F32) + summed[:half]).astype(BF16))
-    grad_out = unfolded((folded(grad_rows).astype(F32) + summed[half:]).astype(BF16))
+    layer_out = total(fwd_rows, term)
     next_rows = passed_along(layer_out, 1)
+    back_term = backward_term(offsets, back, dctx, norm_gain, wq, wk, wv)
+    grad_out = total(grad_rows, back_term)
     prev_rows = passed_along(grad_out, -1)
     return (next_rows[None], prev_rows[None], parked_rows[None])
 

time: 130 us -> 143 us (1.10)
  the two profiles are of different devices: /device:TPU:66 before, /device:TPU:1 now
where the time goes in v9:
time: 143 us; the launch traced here: 142 us
  starting transfers between devices  73.2 us (51%)
  waiting for transfers between devices  46.4 us (32%)
  Pallas kernels  9.92 us (7%)
  local copies, waits for them, and re-layouts  8.55 us (6%)
  other arithmetic  3.02 us (2%)
    all_to_all x4, starting transfers between devices, exchanged(): return lax.all_to_all(blocks, axes, 0, 0, tiled=True)  26.1 us
    ppermute x4, starting transfers between devices, around(): lax.ppermute(block, axis, [(i, (i + distance) % count) for i in range(cou...  17.4 us
    all_to_all x4, waiting for transfers between devices, exchanged(): return lax.all_to_all(blocks, axes, 0, 0, tiled=True)  17.2 us
    ppermute x1, starting transfers between devices, swap_by(): return lambda held: lax.ppermute(held, SECTION, route)  16.7 us
    ppermute x2, starting transfers between devices, passed_along(): return lax.ppermute(block, SECTION, route)  13 us
    ppermute x1, waiting for transfers between devices, swap_by(): return lambda held: lax.ppermute(held, SECTION, route)  12.9 us
    ppermute x4, waiting for transfers between devices, around(): lax.ppermute(block, axis, [(i, (i + distance) % count) for i in range(cou...  12.4 us
    pallas_call x2, Pallas kernels, kernel_call(): pl.pallas_call(body, out_shape=outs, in_specs=specs, out_specs=tuple((vme...  9.92 us
  transfers between devices with their start and end apart: 11, of which 7 were waited for; matrix products, arithmetic and copies ran while one was open for 3% of the time, Pallas kernels for 7%

profile of v9, /device:TPU:1, one launch (start us, length us, event | category | flops | bytes accessed | tf_op | source)
XLA Modules:
  0.0 142.1 jit_solution(6330756244474087393)
XLA Ops:
  0.7 0.9 pad_maximum_fusion
  1.6 0.8 broadcast_in_dim.10
  2.4 7.6 %all-to-all-start = ((bf16[8,64,384]{2,1,0:T(8,128)(2,1)}), bf16[8,64,384]{2,1,0:T(8,128)(2,1)S(1)}, u32[]{:S(2)}, u32[]{:S(2)}) async-start(bf16[8,64,384]{2,1,0:T(8,128)(2,1)} %broadcast_in_dim.10), calls=%async_computation | async-start | bytes 786432 | tf_op jit(solution)/shard_map/all_to_all | solution.py:305
  10.0 10.7 %all-to-all-done.own_ref = bf16[8,64,384]{2,1,0:T(8,128)(2,1)S(1)} async-done(((bf16[8,64,384]{2,1,0:T(8,128)(2,1)}), bf16[8,64,384]{2,1,0:T(8,128)(2,1)S(1)}, u32[]{:S(2)}, u32[]{:S(2)}) %all-to-all-start) | async-done | bytes 393248 | tf_op jit(solution)/shard_map/all_to_all | solution.py:305
  20.8 7.5 %collective-permute-start.16 = (bf16[8,64,384]{2,1,0:T(8,128)(2,1)S(1)}, bf16[8,64,384]{2,1,0:T(8,128)(2,1)S(1)}, u32[]{:S(2)}, u32[]{:S(2)}) collective-permute-start(bf16[8,64,384]{2,1,0:T(8,128)(2,1)S(1)} %all-to-all-done.own_ref), channel_id=1, source_target_pairs={{0,1},{1,2},{2,0},{3,4},{4,5},{5,3},{6,7},{7,8},{8,6},{9,10},{10,1... | collective-permute-start | bytes 1179656 | tf_op jit(solution)/shard_map/ppermute | solution.py:290
  28.3 3.7 %collective-permute-start.17 = (bf16[8,64,384]{2,1,0:T(8,128)(2,1)S(1)}, bf16[8,64,384]{2,1,0:T(8,128)(2,1)S(1)}, u32[]{:S(2)}, u32[]{:S(2)}) collective-permute-start(bf16[8,64,384]{2,1,0:T(8,128)(2,1)S(1)} %all-to-all-done.own_ref), channel_id=1, source_target_pairs={{0,2},{1,0},{2,1},{3,5},{4,3},{5,4},{6,8},{7,6},{8,7},{9,11},{10,9... | collective-permute-start | bytes 1179656 | tf_op jit(solution)/shard_map/ppermute | solution.py:290
  32.1 29.7 %conditional.1 = (bf16[64,384]{1,0:T(8,128)(2,1)}) conditional(s32[]{:T(128)} %bitcast.11, bf16[64,384]{1,0:T(8,128)(2,1)S(1)} %maximum_maximum_fusion, bf16[64,384]{1,0:T(8,128)(2,1)S(1)} %maximum_maximum_fusion, bf16[64,384]{1,0:T(8,128)(2,1)S(1)} %maximum_maximum_fusion, ...), branch_computations={%region_1.0_spmd, %region_2.0_spmd, %region_3.0_spmd, %region_4.0_... | conditional | bytes 196656 | solution.py:301
  32.1 16.7 %collective-permute-start.12 = (bf16[64,384]{1,0:T(8,128)(2,1)S(1)}, bf16[64,384]{1,0:T(8,128)(2,1)}, u32[]{:S(2)}, u32[]{:S(2)}) collective-permute-start(bf16[64,384]{1,0:T(8,128)(2,1)S(1)} %param.12), channel_id=1, source_target_pairs={{0,672},{24,696},{48,720},{72,744},{96,576},{120,600},{144,624},{1... | collective-permute-start | bytes 147464 | tf_op jit(solution)/shard_map/cond/branch_12_fun/ppermute | solution.py:299
  48.9 12.9 %collective-permute-done.12 = bf16[64,384]{1,0:T(8,128)(2,1)} collective-permute-done((bf16[64,384]{1,0:T(8,128)(2,1)S(1)}, bf16[64,384]{1,0:T(8,128)(2,1)}, u32[]{:S(2)}, u32[]{:S(2)}) %collective-permute-start.12) | collective-permute-done | bytes 49184 | tf_op jit(solution)/shard_map/cond/branch_12_fun/ppermute | solution.py:299
  61.8 0.7 slice.87
  62.5 0.7 broadcast_in_dim.23
  63.2 3.4 %all-to-all-start.2 = ((bf16[8,32,384]{2,1,0:T(8,128)(2,1)}), bf16[8,32,384]{2,1,0:T(8,128)(2,1)S(1)}, u32[]{:S(2)}, u32[]{:S(2)}) async-start(bf16[8,32,384]{2,1,0:T(8,128)(2,1)} %broadcast_in_dim.23), calls=%async_computation.2 | async-start | bytes 393216 | tf_op jit(solution)/shard_map/all_to_all | solution.py:305
  66.7 0.7 copy-done.2
  67.4 1.0 copy-done.3
  68.4 4.7 %shard_map.121 = (bf16[24,32,384]{2,1,0:T(8,128)(2,1)}, bf16[64,128]{1,0:T(8,128)(2,1)S(1)}, bf16[4608,128]{1,0:T(8,128)(2,1)S(1)}, bf16[4608,128]{1,0:T(8,128)(2,1)S(1)}, bf16[4608,128]{1,0:T(8,128)(2,1)S(1)}) custom-call(s32[1,2,8]{2,1,0:T(2,128)S(1)} %copy-done.5, bf16[8,64,384]{2,1,0:T(8,128)(2,1)S(1)} %all-to-all-done.own_ref, ...), custom_call_target="tpu_custom_call" | custom-call | tf_op jit(solution)/shard_map/pallas_call | solution.py:220
  73.1 1.0 copy-done
  74.1 1.1 all-to-all-done.2.own_ref
  75.3 8.1 %all-to-all-start.1 = ((bf16[24,32,384]{2,1,0:T(8,128)(2,1)}), bf16[24,32,384]{2,1,0:T(8,128)(2,1)}, u32[]{:S(2)}, u32[]{:S(2)}) async-start(bf16[24,32,384]{2,1,0:T(8,128)(2,1)} %get-tuple-element.41), calls=%async_computation.1 | async-start | bytes 1179648 | tf_op jit(solution)/shard_map/all_to_all | solution.py:305
  83.4 3.1 %collective-permute-start.19 = (bf16[8,32,384]{2,1,0:T(8,128)(2,1)S(1)}, bf16[8,32,384]{2,1,0:T(8,128)(2,1)S(1)}, u32[]{:S(2)}, u32[]{:S(2)}) collective-permute-start(bf16[8,32,384]{2,1,0:T(8,128)(2,1)S(1)} %all-to-all-done.2.own_ref), channel_id=1, source_target_pairs={{0,1},{1,2},{2,0},{3,4},{4,5},{5,3},{6,7},{7,8},{8,6},{9,10},{10,1... | collective-permute-start | bytes 589832 | tf_op jit(solution)/shard_map/ppermute | solution.py:290
  86.6 3.1 %collective-permute-start.20 = (bf16[8,32,384]{2,1,0:T(8,128)(2,1)S(1)}, bf16[8,32,384]{2,1,0:T(8,128)(2,1)S(1)}, u32[]{:S(2)}, u32[]{:S(2)}) collective-permute-start(bf16[8,32,384]{2,1,0:T(8,128)(2,1)S(1)} %all-to-all-done.2.own_ref), channel_id=1, source_target_pairs={{0,2},{1,0},{2,1},{3,5},{4,3},{5,4},{6,8},{7,6},{8,7},{9,11},{10,9... | collective-permute-start | bytes 589832 | tf_op jit(solution)/shard_map/ppermute | solution.py:290
  89.6 8.4 %collective-permute-done.19.low_ref = bf16[8,32,384]{2,1,0:T(8,128)(2,1)S(1)} collective-permute-done((bf16[8,32,384]{2,1,0:T(8,128)(2,1)S(1)}, bf16[8,32,384]{2,1,0:T(8,128)(2,1)S(1)}, u32[]{:S(2)}, u32[]{:S(2)}) %collective-permute-start.19) | collective-permute-done | bytes 196640 | tf_op jit(solution)/shard_map/ppermute | solution.py:290
  98.0 4.0 %collective-permute-done.20.high_ref = bf16[8,32,384]{2,1,0:T(8,128)(2,1)S(1)} collective-permute-done((bf16[8,32,384]{2,1,0:T(8,128)(2,1)S(1)}, bf16[8,32,384]{2,1,0:T(8,128)(2,1)S(1)}, u32[]{:S(2)}, u32[]{:S(2)}) %collective-permute-start.20) | collective-permute-done | bytes 196640 | tf_op jit(solution)/shard_map/ppermute | solution.py:290
  102.0 1.3 copy-done.1
  103.3 5.2 %shard_map.122 = bf16[24,32,384]{2,1,0:T(8,128)(2,1)} custom-call(s32[1,2,8]{2,1,0:T(2,128)S(1)} %copy-done.5, bf16[8,32,384]{2,1,0:T(8,128)(2,1)S(1)} %all-to-all-done.2.own_ref, bf16[8,32,384]{2,1,0:T(8,128)(2,1)S(1)} %collective-permute-done.19.low_ref, bf16[8,32,384]{2,1,0:T(8,128)(2,1)S(1)} %collective-permute-done.20.high_ref, ...), custom_call_target="tpu_custom_call" | custom-call | tf_op jit(solution)/shard_map/pallas_call | solution.py:220
  108.5 6.9 %all-to-all-start.3 = ((bf16[24,32,384]{2,1,0:T(8,128)(2,1)}), bf16[24,32,384]{2,1,0:T(8,128)(2,1)S(1)}, u32[]{:S(2)}, u32[]{:S(2)}) async-start(bf16[24,32,384]{2,1,0:T(8,128)(2,1)} %shard_map.122), calls=%async_computation.3 | async-start | bytes 1179648 | tf_op jit(solution)/shard_map/all_to_all | solution.py:305
  115.4 0.9 fusion
  116.3 1.2 convert_reduce_fusion.1
  117.6 6.8 %collective-permute-start.18 = (bf16[64,192]{1,0:T(8,128)(2,1)S(1)}, bf16[64,192]{1,0:T(8,128)(2,1)S(1)}, u32[]{:S(2)}, u32[]{:S(2)}) collective-permute-start(bf16[64,192]{1,0:T(8,128)(2,1)S(1)} %pad_maximum_fusion.1), channel_id=1, source_target_pairs={{0,24},{24,48},{48,72},{72,96},{96,120},{120,144},{144,168},{168,1... | collective-permute-start | bytes 73736 | tf_op jit(solution)/shard_map/ppermute | solution.py:285
  124.5 5.4 %all-to-all-done.3 = bf16[24,32,384]{2,1,0:T(8,128)(2,1)S(1)} async-done(((bf16[24,32,384]{2,1,0:T(8,128)(2,1)}), bf16[24,32,384]{2,1,0:T(8,128)(2,1)S(1)}, u32[]{:S(2)}, u32[]{:S(2)}) %all-to-all-start.3) | async-done | bytes 589856 | tf_op jit(solution)/shard_map/all_to_all | solution.py:305
  130.1 6.2 %collective-permute-start.21 = (bf16[64,192]{1,0:T(8,128)(2,1)S(1)}, bf16[64,192]{1,0:T(8,128)(2,1)S(1)}, u32[]{:S(2)}, u32[]{:S(2)}) collective-permute-start(bf16[64,192]{1,0:T(8,128)(2,1)S(1)} %pad_maximum_fusion.2), channel_id=1, source_target_pairs={{24,0},{48,24},{72,48},{96,72},{120,96},{144,120},{168,144},{192,1... | collective-permute-start | bytes 73736 | tf_op jit(solution)/shard_map/ppermute | solution.py:285
  136.3 0.6 maximum_bitcast_fusion
  136.9 3.9 %collective-permute-done.21 = bf16[64,192]{1,0:T(8,128)(2,1)S(1)} collective-permute-done((bf16[64,192]{1,0:T(8,128)(2,1)S(1)}, bf16[64,192]{1,0:T(8,128)(2,1)S(1)}, u32[]{:S(2)}, u32[]{:S(2)}) %collective-permute-start.21) | collective-permute-done | bytes 24608 | tf_op jit(solution)/shard_map/ppermute | solution.py:285
  (33 shorter events, 1.8 us)
Async XLA Ops:
  0.6 9.4 %copy-start.6 = (bf16[1,64,192]{2,1,0:T(8,128)(2,1)S(1)}, bf16[1,64,192]{2,1,0:T(8,128)(2,1)}, u32[]{:S(2)}) copy-start(bf16[1,64,192]{2,1,0:T(8,128)(2,1)} %param.26) | copy-start | bytes 73732
  0.6 9.4 %copy-start.8 = (bf16[1,64,192]{2,1,0:T(8,128)(2,1)S(1)}, bf16[1,64,192]{2,1,0:T(8,128)(2,1)}, u32[]{:S(2)}) copy-start(bf16[1,64,192]{2,1,0:T(8,128)(2,1)} %param.28) | copy-start | bytes 73732
  0.7 31.4 %copy-start.9 = (s32[32]{0:T(128)S(1)}, s32[32]{0:T(128)}, u32[]{:S(2)}) copy-start(s32[32]{0:T(128)} %param.35) | copy-start | bytes 388
  0.7 66.7 %copy-start.5 = (s32[1,2,8]{2,1,0:T(2,128)S(1)}, s32[1,2,8]{2,1,0:T(2,128)}, u32[]{:S(2)}) copy-start(s32[1,2,8]{2,1,0:T(2,128)} %off_ref.3) | copy-start | bytes 196
  0.7 66.7 %copy-start.4 = (f32[1,4608]{1,0:T(1,128)S(1)}, f32[1,4608]{1,0:T(1,128)}, u32[]{:S(2)}) copy-start(f32[1,4608]{1,0:T(1,128)} %gain_ref.3) | copy-start | bytes 55300
  2.4 18.4 %all-to-all-start = ((bf16[8,64,384]{2,1,0:T(8,128)(2,1)}), bf16[8,64,384]{2,1,0:T(8,128)(2,1)S(1)}, u32[]{:S(2)}, u32[]{:S(2)}) async-start(bf16[8,64,384]{2,1,0:T(8,128)(2,1)} %broadcast_in_dim.10), calls=%async_computation | async-start | bytes 786432 | tf_op jit(solution)/shard_map/all_to_all | solution.py:305
  20.8 45.9 %collective-permute-start.16 = (bf16[8,64,384]{2,1,0:T(8,128)(2,1)S(1)}, bf16[8,64,384]{2,1,0:T(8,128)(2,1)S(1)}, u32[]{:S(2)}, u32[]{:S(2)}) collective-permute-start(bf16[8,64,384]{2,1,0:T(8,128)(2,1)S(1)} %all-to-all-done.own_ref), channel_id=1, source_target_pairs={{0,1},{1,2},{2,0},{3,4},{4,5},{5,3},{6,7},{7,8},{8,6},{9,10},{10,1... | collective-permute-start | bytes 1179656 | tf_op jit(solution)/shard_map/ppermute | solution.py:290
  28.3 38.4 %collective-permute-start.17 = (bf16[8,64,384]{2,1,0:T(8,128)(2,1)S(1)}, bf16[8,64,384]{2,1,0:T(8,128)(2,1)S(1)}, u32[]{:S(2)}, u32[]{:S(2)}) collective-permute-start(bf16[8,64,384]{2,1,0:T(8,128)(2,1)S(1)} %all-to-all-done.own_ref), channel_id=1, source_target_pairs={{0,2},{1,0},{2,1},{3,5},{4,3},{5,4},{6,8},{7,6},{8,7},{9,11},{10,9... | collective-permute-start | bytes 1179656 | tf_op jit(solution)/shard_map/ppermute | solution.py:290
  32.1 29.7 %collective-permute-start.12 = (bf16[64,384]{1,0:T(8,128)(2,1)S(1)}, bf16[64,384]{1,0:T(8,128)(2,1)}, u32[]{:S(2)}, u32[]{:S(2)}) collective-permute-start(bf16[64,384]{1,0:T(8,128)(2,1)S(1)} %param.12), channel_id=1, source_target_pairs={{0,672},{24,696},{48,720},{72,744},{96,576},{120,600},{144,624},{1... | collective-permute-start | bytes 147464 | tf_op jit(solution)/shard_map/cond/branch_12_fun/ppermute | solution.py:299
  63.2 12.0 %all-to-all-start.2 = ((bf16[8,32,384]{2,1,0:T(8,128)(2,1)}), bf16[8,32,384]{2,1,0:T(8,128)(2,1)S(1)}, u32[]{:S(2)}, u32[]{:S(2)}) async-start(bf16[8,32,384]{2,1,0:T(8,128)(2,1)} %broadcast_in_dim.23), calls=%async_computation.2 | async-start | bytes 393216 | tf_op jit(solution)/shard_map/all_to_all | solution.py:305
  66.7 0.7 copy-start.2
  67.4 1.0 copy-start.3
  73.1 1.0 copy-start
  75.3 33.2 %all-to-all-start.1 = ((bf16[24,32,384]{2,1,0:T(8,128)(2,1)}), bf16[24,32,384]{2,1,0:T(8,128)(2,1)}, u32[]{:S(2)}, u32[]{:S(2)}) async-start(bf16[24,32,384]{2,1,0:T(8,128)(2,1)} %get-tuple-element.41), calls=%async_computation.1 | async-start | bytes 1179648 | tf_op jit(solution)/shard_map/all_to_all | solution.py:305
  83.4 14.6 %collective-permute-start.19 = (bf16[8,32,384]{2,1,0:T(8,128)(2,1)S(1)}, bf16[8,32,384]{2,1,0:T(8,128)(2,1)S(1)}, u32[]{:S(2)}, u32[]{:S(2)}) collective-permute-start(bf16[8,32,384]{2,1,0:T(8,128)(2,1)S(1)} %all-to-all-done.2.own_ref), channel_id=1, source_target_pairs={{0,1},{1,2},{2,0},{3,4},{4,5},{5,3},{6,7},{7,8},{8,6},{9,10},{10,1... | collective-permute-start | bytes 589832 | tf_op jit(solution)/shard_map/ppermute | solution.py:290
  86.6 15.4 %collective-permute-start.20 = (bf16[8,32,384]{2,1,0:T(8,128)(2,1)S(1)}, bf16[8,32,384]{2,1,0:T(8,128)(2,1)S(1)}, u32[]{:S(2)}, u32[]{:S(2)}) collective-permute-start(bf16[8,32,384]{2,1,0:T(8,128)(2,1)S(1)} %all-to-all-done.2.own_ref), channel_id=1, source_target_pairs={{0,2},{1,0},{2,1},{3,5},{4,3},{5,4},{6,8},{7,6},{8,7},{9,11},{10,9... | collective-permute-start | bytes 589832 | tf_op jit(solution)/shard_map/ppermute | solution.py:290
  102.0 1.3 copy-start.1
  108.5 6.9 %copy-start.7 = (bf16[1,64,192]{2,1,0:T(8,128)(2,1)S(1)}, bf16[1,64,192]{2,1,0:T(8,128)(2,1)}, u32[]{:S(2)}) copy-start(bf16[1,64,192]{2,1,0:T(8,128)(2,1)} %param.27) | copy-start | bytes 73732
  108.5 21.3 %all-to-all-start.3 = ((bf16[24,32,384]{2,1,0:T(8,128)(2,1)}), bf16[24,32,384]{2,1,0:T(8,128)(2,1)S(1)}, u32[]{:S(2)}, u32[]{:S(2)}) async-start(bf16[24,32,384]{2,1,0:T(8,128)(2,1)} %shard_map.122), calls=%async_computation.3 | async-start | bytes 1179648 | tf_op jit(solution)/shard_map/all_to_all | solution.py:305
  117.6 19.3 %collective-permute-start.18 = (bf16[64,192]{1,0:T(8,128)(2,1)S(1)}, bf16[64,192]{1,0:T(8,128)(2,1)S(1)}, u32[]{:S(2)}, u32[]{:S(2)}) collective-permute-start(bf16[64,192]{1,0:T(8,128)(2,1)S(1)} %pad_maximum_fusion.1), channel_id=1, source_target_pairs={{0,24},{24,48},{48,72},{72,96},{96,120},{120,144},{144,168},{168,1... | collective-permute-start | bytes 73736 | tf_op jit(solution)/shard_map/ppermute | solution.py:285
  130.1 10.7 %collective-permute-start.21 = (bf16[64,192]{1,0:T(8,128)(2,1)S(1)}, bf16[64,192]{1,0:T(8,128)(2,1)S(1)}, u32[]{:S(2)}, u32[]{:S(2)}) collective-permute-start(bf16[64,192]{1,0:T(8,128)(2,1)S(1)} %pad_maximum_fusion.2), channel_id=1, source_target_pairs={{24,0},{48,24},{72,48},{96,72},{120,96},{144,120},{168,144},{192,1... | collective-permute-start | bytes 73736 | tf_op jit(solution)/shard_map/ppermute | solution.py:285
